TPU v7x, 128 devices: a whole 4x4x4 slice. The times are simulated.
128 devices in a mesh: gx: 16 (over z, x), gy: 8 (over y, core).
Axes of the slice: x: 4, y: 4, z: 4, core: 2. Of those that a mesh axis runs over, the one named last changes fastest.
Arguments:
- anchors: float32 [3, 4096], P(None, ('gx', 'gy')), may hold values from 0 to 1
- directions: float32 [3, 4096], P(None, ('gx', 'gy')), may hold values from -1 to 1
- ray_start: float32 [4096], P(('gx', 'gy')), may hold values from 0 to 1
- camera_ids: int32 [4096], P(('gx', 'gy')), may hold values from 0 to 255
- brick_ids: int32 [4096, 4], P(('gx', 'gy')), may hold values from 0 to 127, all different within a row; in each aligned block of 32 rows (0 to 31, 32 to 63, ...) at most 2 rows name the same one
- brick_rank: int32 [4096, 4], P(('gx', 'gy')), may hold values from 0 to 3, each once within a row
- targets: float32 [4096, 128], P(('gx', 'gy')), may hold values from -6 to 6
- planes: float32 [128, 12288, 128], P(('gx', 'gy')), may hold values from -6 to 6
- first_weight: float32 [128, 128, 256], P(('gx', 'gy')), may hold values from -0.5 to 0.5
- hidden_weight: float32 [128, 1, 256, 256], P(('gx', 'gy')), may hold values from -0.375 to 0.375
- feature_weight: float32 [128, 256, 128], P(('gx', 'gy')), may hold values from -0.375 to 0.375
- density_weight: float32 [128, 256], P(('gx', 'gy')), may hold values from -0.375 to 0.375
- poses: float32 [6, 256], replicated, may hold values from -0.1 to 0.1
Outputs:
- ray_feature: float32 [4096, 128], P(('gx', 'gy'))
- plane_grad: float32 [128, 12288, 128], P(('gx', 'gy'))
- first_grad: float32 [128, 128, 256], P(('gx', 'gy'))
- hidden_grad: float32 [128, 1, 256, 256], P(('gx', 'gy'))
- feature_grad: float32 [128, 256, 128], P(('gx', 'gy'))
- density_grad: float32 [128, 256], P(('gx', 'gy'))
- pose_grad: float32 [6, 256], replicated
Inputs may be any that keep to these rules, and one draw needn't show every extreme that they name: `brick_ids`: each ray names 4 different bricks; among the rays of one device no brick is named more than 2 times, and in every draw some device's rays name some brick exactly 2 times. `brick_rank`: each row holds every number of 0 to 3 once.
All inputs are finite; a program needn't handle non-finite values.
Results may differ from a plain program's by a relative error of at most 0.014.
Values sent between devices are 32-bit elements; how exact they have to be, the bound alone decides.
No kernel may reach another device: no remote copies, remote signals or barrier semaphores. Data moves between devices by JAX's collectives and lax.ppermute only.
A program may use at most 256 MiB of HBM per device.

v0:
```python
import jax
import jax.numpy as jnp
from jax import lax
from jax.sharding import PartitionSpec as P

K = 4
S = 4
P_SIZE = 64


sample_step = 0.125
plane_pairs = ((0, 1), (0, 2), (1, 2))


def smooth_weight(fraction):
    return fraction * fraction * (3.0 - 2.0 * fraction)


def axis_weights(coord, cells):
    scaled = coord * P_SIZE
    floor_c = jnp.floor(scaled)
    weight = smooth_weight(scaled - floor_c)[:, None]
    low_c = jnp.mod(floor_c.astype(jnp.int32), P_SIZE)
    high_c = jnp.mod(low_c + 1, P_SIZE)
    low_hit = (cells[None, :] == low_c[:, None]).astype(jnp.float32)
    high_hit = (cells[None, :] == high_c[:, None]).astype(jnp.float32)
    return (1.0 - weight) * low_hit + weight * high_hit


def lookup_block(planes_flat, points):
    count = points.shape[1]
    cells = jnp.arange(P_SIZE)
    summed = jnp.zeros((count, planes_flat.shape[1]), jnp.float32)
    for plane_index, coord_pair in enumerate(plane_pairs):
        row_factor = axis_weights(points[coord_pair[0]], cells)
        col_factor = axis_weights(points[coord_pair[1]], cells)
        table = (row_factor[:, :, None] * col_factor[:, None, :]).reshape(count, P_SIZE * P_SIZE)
        plane_rows = planes_flat[
            plane_index * P_SIZE * P_SIZE : (plane_index + 1) * P_SIZE * P_SIZE
        ]
        summed = summed + jnp.dot(
            table, plane_rows, precision=lax.Precision.HIGHEST, preferred_element_type=jnp.float32
        )
    return summed


def lookup(planes_flat, points):
    count = points.shape[1]
    block = min(512, count)
    blocks = count // block
    grouped = points.reshape(3, blocks, block).transpose(1, 0, 2)

    def one_block(piece):
        return lookup_block(planes_flat, piece)

    return lax.map(one_block, grouped).reshape(count, planes_flat.shape[1])


def brick_samples(
    planes_flat, first_weight, hidden_weight, feature_weight, density_weight, received
):
    sources, slot_total, flat_width = received.shape
    points = received.reshape(sources * slot_total, 3, S).transpose(1, 0, 2).reshape(3, -1)
    features = lookup(planes_flat, points).astype(jnp.bfloat16)
    hidden = jax.nn.silu(
        jnp.dot(features, first_weight.astype(jnp.bfloat16), preferred_element_type=jnp.float32)
    ).astype(jnp.bfloat16)
    hidden = jax.nn.silu(
        jnp.dot(hidden, hidden_weight[0].astype(jnp.bfloat16), preferred_element_type=jnp.float32)
    ).astype(jnp.bfloat16)
    colors = jnp.tanh(
        jnp.dot(hidden, feature_weight.astype(jnp.bfloat16), preferred_element_type=jnp.float32)
    )
    density = jax.nn.softplus(
        jnp.dot(hidden, density_weight.astype(jnp.bfloat16), preferred_element_type=jnp.float32)
    )
    return (colors.reshape(sources, slot_total, -1), density.reshape(sources, slot_total, S))


def composite(density, colors):
    optical_depth = density * sample_step
    before = jnp.cumsum(optical_depth, axis=-1) - optical_depth
    weight = jnp.exp(-before) * (1.0 - jnp.exp(-optical_depth))
    feature = jnp.sum(weight[..., None] * colors, axis=-2)
    passing = jnp.exp(-jnp.sum(optical_depth, axis=-1))
    return (feature, passing)


def pick_brick():
    return brick_samples


def ray_composite(segment_feature, segment_pass, brick_rank):
    transmit = jnp.ones(segment_pass.shape, segment_pass.dtype)
    for other_seg in range(K):
        in_front = brick_rank[:, other_seg][:, None] < brick_rank
        transmit = transmit * jnp.where(in_front, segment_pass[:, other_seg][:, None], 1.0)
    return jnp.sum(transmit[:, :, None] * segment_feature, axis=1)


def cross_rows(left, right):
    return jnp.stack(
        [
            left[1] * right[2] - left[2] * right[1],
            left[2] * right[0] - left[0] * right[2],
            left[0] * right[1] - left[1] * right[0],
        ]
    )


def sample_points(anchors, directions, ray_start, ray_pose, brick_rank):
    rotation = ray_pose[0:3]
    offset = ray_pose[3:6]
    moved_anchor = anchors + cross_rows(rotation, anchors) + offset
    moved_direction = directions + cross_rows(rotation, directions)
    place_along = (
        brick_rank.astype(jnp.float32)[:, :, None] * S + jnp.arange(S)[None, None, :] + 0.5
    )
    distance = ray_start[:, None, None] + place_along * sample_step
    return moved_anchor[:, :, None, None] + distance[None] * moved_direction[:, :, None, None]


def slot_numbers(target_brick, brick_count):
    onehot = (target_brick[:, None] == jnp.arange(brick_count)[None, :]).astype(jnp.float32)
    rows = target_brick.shape[0]
    lower = (jnp.arange(rows)[:, None] > jnp.arange(rows)[None, :]).astype(jnp.float32)
    before = jnp.dot(
        lower, onehot, precision=lax.Precision.HIGHEST, preferred_element_type=jnp.float32
    )
    return jnp.sum(before * onehot, axis=1).astype(jnp.int32)


def to_slots(route, rows):
    return lax.dot_general(
        route,
        rows,
        (((0,), (0,)), ((), ())),
        precision=lax.Precision.HIGHEST,
        preferred_element_type=jnp.float32,
    )


def from_slots(route, rows):
    return jnp.dot(route, rows, precision=lax.Precision.HIGHEST, preferred_element_type=jnp.float32)


def per_device(
    anchors,
    directions,
    ray_start,
    camera_ids,
    brick_ids,
    brick_rank,
    targets,
    planes,
    first_weight,
    hidden_weight,
    feature_weight,
    density_weight,
    poses,
):
    brick_count = lax.axis_size(("gx", "gy"))
    ray_count = anchors.shape[1]
    capacity = 2 * ray_count * K // brick_count
    selector = (jnp.arange(poses.shape[1])[:, None] == camera_ids[None, :]).astype(jnp.float32)

    def place(pose_table):
        ray_pose = jnp.dot(pose_table, selector, precision=lax.Precision.HIGHEST)
        return sample_points(anchors, directions, ray_start, ray_pose, brick_rank)

    points, pose_pullback = jax.vjp(place, poses)
    payload = points.transpose(1, 2, 0, 3).reshape(ray_count * K, 3 * S)
    target_brick = brick_ids.reshape(-1)
    flat_slot = target_brick * capacity + slot_numbers(target_brick, brick_count)
    route = (flat_slot[:, None] == jnp.arange(brick_count * capacity)[None, :]).astype(jnp.float32)
    outgoing = to_slots(route, payload).reshape(brick_count, capacity, 3 * S)
    params = (planes[0], first_weight[0], hidden_weight[0], feature_weight[0], density_weight[0])
    brick_fn = pick_brick()
    received = lax.all_to_all(outgoing, ("gx", "gy"), split_axis=0, concat_axis=0, tiled=True)
    values_out, optical_out = brick_fn(
        params[0], params[1], params[2], params[3], params[4], received
    )
    values_sent, optical_sent, received = (values_out, optical_out, received)
    values_home, optical_home = (
        lax.all_to_all(values_sent, ("gx", "gy"), split_axis=0, concat_axis=0, tiled=True),
        lax.all_to_all(optical_sent, ("gx", "gy"), split_axis=0, concat_axis=0, tiled=True),
    )
    segment_values = from_slots(route, values_home.reshape(brick_count * capacity, -1))
    segment_optical = from_slots(route, optical_home.reshape(brick_count * capacity, -1))

    def ray_from(values_part, optical_part):
        segment_feature, segment_pass = composite(
            optical_part.reshape(ray_count, K, S), values_part.reshape(ray_count, K, S, -1)
        )
        return ray_composite(segment_feature, segment_pass, brick_rank)

    ray_feature, ray_pullback = jax.vjp(ray_from, segment_values, segment_optical)
    values_grad, optical_grad = ray_pullback(ray_feature - targets)
    values_back = to_slots(route, values_grad).reshape(values_sent.shape)
    optical_back = to_slots(route, optical_grad).reshape(optical_sent.shape)
    values_cot, optical_cot = (
        lax.all_to_all(values_back, ("gx", "gy"), split_axis=0, concat_axis=0, tiled=True),
        lax.all_to_all(optical_back, ("gx", "gy"), split_axis=0, concat_axis=0, tiled=True),
    )
    outputs_unused, brick_pullback = jax.vjp(
        brick_fn, params[0], params[1], params[2], params[3], params[4], received
    )
    gradients = brick_pullback((values_cot, optical_cot))
    point_home = lax.all_to_all(gradients[5], ("gx", "gy"), split_axis=0, concat_axis=0, tiled=True)
    point_rows = from_slots(route, point_home.reshape(brick_count * capacity, 3 * S))
    point_grad = point_rows.reshape(ray_count, K, 3, S).transpose(2, 0, 1, 3)
    pose_local = pose_pullback(point_grad)[0]
    pose_grad = lax.psum(pose_local, ("gx", "gy"))
    return (
        ray_feature,
        gradients[0][None],
        gradients[1][None],
        gradients[2][None],
        gradients[3][None],
        gradients[4][None],
        pose_grad,
    )


def solution(mesh):
    in_specs = (
        P(None, ("gx", "gy")),
        P(None, ("gx", "gy")),
        P(("gx", "gy")),
        P(("gx", "gy")),
        P(("gx", "gy"), None),
        P(("gx", "gy"), None),
        P(("gx", "gy"), None),
        P(("gx", "gy"), None, None),
        P(("gx", "gy"), None, None),
        P(("gx", "gy"), None, None, None),
        P(("gx", "gy"), None, None),
        P(("gx", "gy"), None),
        P(),
    )
    out_specs = (
        P(("gx", "gy"), None),
        P(("gx", "gy"), None, None),
        P(("gx", "gy"), None, None),
        P(("gx", "gy"), None, None, None),
        P(("gx", "gy"), None, None),
        P(("gx", "gy"), None),
        P(),
    )
    return jax.shard_map(
        per_device, mesh=mesh, in_specs=in_specs, out_specs=out_specs, check_vma=False
    )
```

profile of v0, /device:TPU:1, one launch (start us, length us, event | category | flops | bytes accessed | tf_op | source)
XLA Modules:
  0.0 686.8 jit_solution(6408502191183947123)
XLA Ops:
  8.3 11.5 %all-to-all-start = ((f32[128,2,12]{2,1,0:T(2,128)}), f32[128,2,12]{2,1,0:T(2,128)S(1)}, u32[]{:S(2)}, u32[]{:S(2)}) async-start(f32[128,2,12]{2,1,0:T(2,128)} %copy.89), calls=%async_computation | async-start | bytes 262144 | tf_op jit(solution)/shard_map/all_to_all | solution.py:179
  30.5 135.7 %while.108 = (s32[]{:T(128)}, bf16[2,512,128]{2,1,0:T(8,128)(2,1)S(1)}, f32[2,3,512]{2,1,0:T(4,128)S(1)}, f32[12288,128]{1,0:T(8,128)}, s32[]{:T(128)}, /*index=5*/s32[]{:T(128)}, s32[]{}, s32[]{}) while((s32[]{:T(128)}, bf16[2,512,128]{2,1,0:T(8,128)(2,1)S(1)}, f32[2,3,512]{2,1,0:T(4,128)S(1)}, f32[12288,128]{1,0:T(8,128)}, s32[]{:T(128)}, ...), condition=%wide.region_2.3_spmd, body=%wide.region_1.2_spmd.sunk | while | flops 9670641664 | bytes 117514952 | solution.py:56
  64.2 16.0 %fusion.281 = f32[512,128]{1,0:T(8,128)S(1)} fusion(f32[512,4096]{0,1:T(8,128)} %bitcast.418, f32[12288,128]{1,0:T(8,128)} %get-tuple-element.2989), kind=kOutput, calls=%fused_computation.4.clone.1 | convolution fusion | flops 3221225472 | bytes 10747904 | tf_op jit(solution)/shard_map/while/body/eval_jaxpr/dot_general | solution.py:41
  80.2 15.1 %fusion.282 = f32[512,128]{1,0:T(8,128)S(1)} fusion(f32[512,4096]{0,1:T(8,128)S(1)} %bitcast.417, f32[12288,128]{1,0:T(8,128)} %get-tuple-element.2989), kind=kOutput, calls=%fused_computation.6.clone.1 | convolution fusion | flops 3221225472 | bytes 10747904 | tf_op jit(solution)/shard_map/while/body/eval_jaxpr/dot_general | solution.py:41
  95.3 15.0 %fusion.283 = bf16[2,512,128]{2,1,0:T(8,128)(2,1)S(1)} fusion(bf16[2,512,128]{2,1,0:T(8,128)(2,1)S(1)} %get-tuple-element.2979, s32[]{:T(128)} %get-tuple-element.2978, f32[512,128]{1,0:T(8,128)S(1)} %fusion.281, f32[512,128]{1,0:T(8,128)S(1)} %fusion.282, f32[512,4096]{0,1:T(8,128)S(1)} %bitcast.416, f32[12288,128]{1,0:T(8,128)} %get-tuple-element.2989), kind=kOutput, calls=%fused_computation.13.clone.1 | convolution fusion | flops 3221356544 | bytes 11272704 | tf_op jit(solution)/shard_map/while/body/eval_jaxpr/dot_general | solution.py:41
  120.0 16.0 %fusion.281 = f32[512,128]{1,0:T(8,128)S(1)} fusion(f32[512,4096]{0,1:T(8,128)} %bitcast.418, f32[12288,128]{1,0:T(8,128)} %get-tuple-element.2989), kind=kOutput, calls=%fused_computation.4.clone.1 | convolution fusion | flops 3221225472 | bytes 10747904 | tf_op jit(solution)/shard_map/while/body/eval_jaxpr/dot_general | solution.py:41
  136.0 15.1 %fusion.282 = f32[512,128]{1,0:T(8,128)S(1)} fusion(f32[512,4096]{0,1:T(8,128)S(1)} %bitcast.417, f32[12288,128]{1,0:T(8,128)} %get-tuple-element.2989), kind=kOutput, calls=%fused_computation.6.clone.1 | convolution fusion | flops 3221225472 | bytes 10747904 | tf_op jit(solution)/shard_map/while/body/eval_jaxpr/dot_general | solution.py:41
  151.1 15.0 %fusion.283 = bf16[2,512,128]{2,1,0:T(8,128)(2,1)S(1)} fusion(bf16[2,512,128]{2,1,0:T(8,128)(2,1)S(1)} %get-tuple-element.2979, s32[]{:T(128)} %get-tuple-element.2978, f32[512,128]{1,0:T(8,128)S(1)} %fusion.281, f32[512,128]{1,0:T(8,128)S(1)} %fusion.282, f32[512,4096]{0,1:T(8,128)S(1)} %bitcast.416, f32[12288,128]{1,0:T(8,128)} %get-tuple-element.2989), kind=kOutput, calls=%fused_computation.13.clone.1 | convolution fusion | flops 3221356544 | bytes 11272704 | tf_op jit(solution)/shard_map/while/body/eval_jaxpr/dot_general | solution.py:41
  178.7 182.8 %while.109 = (s32[]{:T(128)}, bf16[2,512,128]{2,1,0:T(8,128)(2,1)S(1)}, f32[2,512]{1,0:T(2,128)S(1)}, f32[2,512]{1,0:T(2,128)S(1)}, f32[2,512]{1,0:T(2,128)S(1)}...) while((s32[]{:T(128)}, ...), condition=%wide.region_15.16_spmd.clone.clone, body=%wide.region_14.15_spmd.clone.clone.sunk | while | flops 9671700480 | bytes 198627264 | solution.py:56
  191.6 13.0 %constant_dynamic-update-slice_fusion.22 = (f32[2,512,4096]{1,2,0:T(8,128)}, f32[2,512,4096]{1,2,0:T(8,128)}) fusion(f32[2,512,4096]{1,2,0:T(8,128)} %get-tuple-element.3049, f32[1,512,4096]{1,2,0:T(8,128)} %bitcast.404, s32[]{:T(128)} %get-tuple-element.3026, f32[2,512,4096]{1,2,0:T(8,128)} %get-tuple-element.3047, f32[1,512,4096]{1,2,0:T(8,128)} %bitcast.408), kind=kLoop, calls=%fused_computation.106.clone.1 | loop fusion | bytes 33554944 | tf_op jit(solution)/shard_map/jvp()/while/body/jit(dynamic_update_index_in_dim)/dynamic_update_slice | solution.py:56
  209.9 15.5 %fusion.291 = f32[512,128]{1,0:T(8,128)S(1)} fusion(f32[512,4096]{0,1:T(8,128)S(1)} %bitcast.413, f32[4096,128]{1,0:T(8,128)} %get-tuple-element.3083), kind=kOutput, calls=%fused_computation.444.clone.1 | convolution fusion | flops 3221225472 | bytes 10747904 | tf_op jit(solution)/shard_map/jvp()/while/body/eval_jaxpr/dot_general | solution.py:41
  225.5 15.4 %convolution_add_fusion.3 = f32[512,128]{1,0:T(8,128)S(1)} fusion(f32[512,128]{1,0:T(8,128)S(1)} %fusion.291, f32[512,4096]{0,1:T(8,128)S(1)} %bitcast.411, f32[4096,128]{1,0:T(8,128)} %get-tuple-element.3084), kind=kOutput, calls=%fused_computation.68.clone.1 | convolution fusion | flops 3221291008 | bytes 11010048 | tf_op jit(solution)/shard_map/jvp()/while/body/eval_jaxpr/dot_general | solution.py:41
  240.9 15.2 %fusion.292 = bf16[2,512,128]{2,1,0:T(8,128)(2,1)S(1)} fusion(bf16[2,512,128]{2,1,0:T(8,128)(2,1)S(1)} %get-tuple-element.3027, s32[]{:T(128)} %get-tuple-element.3026, f32[512,128]{1,0:T(8,128)S(1)} %convolution_add_fusion.3, f32[512,4096]{0,1:T(8,128)S(1)} %bitcast.407, f32[4096,128]{1,0:T(8,128)} %get-tuple-element.3085), kind=kOutput, calls=%fused_computation.67.clone.1 | convolution fusion | flops 3221291008 | bytes 11010052 | tf_op jit(solution)/shard_map/jvp()/while/body/eval_jaxpr/dot_general | solution.py:41
  278.0 13.2 %constant_dynamic-update-slice_fusion.22 = (f32[2,512,4096]{1,2,0:T(8,128)}, f32[2,512,4096]{1,2,0:T(8,128)}) fusion(f32[2,512,4096]{1,2,0:T(8,128)} %get-tuple-element.3049, f32[1,512,4096]{1,2,0:T(8,128)} %bitcast.404, s32[]{:T(128)} %get-tuple-element.3026, f32[2,512,4096]{1,2,0:T(8,128)} %get-tuple-element.3047, f32[1,512,4096]{1,2,0:T(8,128)} %bitcast.408), kind=kLoop, calls=%fused_computation.106.clone.1 | loop fusion | bytes 33554944 | tf_op jit(solution)/shard_map/jvp()/while/body/jit(dynamic_update_index_in_dim)/dynamic_update_slice | solution.py:56
  296.6 15.3 %fusion.291 = f32[512,128]{1,0:T(8,128)S(1)} fusion(f32[512,4096]{0,1:T(8,128)S(1)} %bitcast.413, f32[4096,128]{1,0:T(8,128)} %get-tuple-element.3083), kind=kOutput, calls=%fused_computation.444.clone.1 | convolution fusion | flops 3221225472 | bytes 10747904 | tf_op jit(solution)/shard_map/jvp()/while/body/eval_jaxpr/dot_general | solution.py:41
  312.0 15.4 %convolution_add_fusion.3 = f32[512,128]{1,0:T(8,128)S(1)} fusion(f32[512,128]{1,0:T(8,128)S(1)} %fusion.291, f32[512,4096]{0,1:T(8,128)S(1)} %bitcast.411, f32[4096,128]{1,0:T(8,128)} %get-tuple-element.3084), kind=kOutput, calls=%fused_computation.68.clone.1 | convolution fusion | flops 3221291008 | bytes 11010048 | tf_op jit(solution)/shard_map/jvp()/while/body/eval_jaxpr/dot_general | solution.py:41
  327.4 15.3 %fusion.292 = bf16[2,512,128]{2,1,0:T(8,128)(2,1)S(1)} fusion(bf16[2,512,128]{2,1,0:T(8,128)(2,1)S(1)} %get-tuple-element.3027, s32[]{:T(128)} %get-tuple-element.3026, f32[512,128]{1,0:T(8,128)S(1)} %convolution_add_fusion.3, f32[512,4096]{0,1:T(8,128)S(1)} %bitcast.407, f32[4096,128]{1,0:T(8,128)} %get-tuple-element.3085), kind=kOutput, calls=%fused_computation.67.clone.1 | convolution fusion | flops 3221291008 | bytes 11010052 | tf_op jit(solution)/shard_map/jvp()/while/body/eval_jaxpr/dot_general | solution.py:41
  375.9 12.2 %all-to-all-done.2 = f32[128,2,512]{2,1,0:T(2,128)S(1)} async-done(((f32[128,2,512]{2,1,0:T(2,128)}), f32[128,2,512]{2,1,0:T(2,128)S(1)}, u32[]{:S(2)}, u32[]{:S(2)}) %all-to-all-start.2) | async-done | bytes 524320 | tf_op jit(solution)/shard_map/all_to_all | solution.py:185
  411.3 12.6 %all-to-all-done.4 = f32[128,2,512]{2,1,0:T(2,128)S(1)} async-done(((f32[128,2,512]{2,1,0:T(2,128)}), f32[128,2,512]{2,1,0:T(2,128)S(1)}, u32[]{:S(2)}, u32[]{:S(2)}) %all-to-all-start.4) | async-done | bytes 524320 | tf_op jit(solution)/shard_map/all_to_all | solution.py:202
  430.5 176.5 %while.110 = (s32[]{:T(128)}, f32[12288,128]{1,0:T(8,128)}, f32[2,3,512]{2,1,0:T(4,128)S(1)}, f32[2,512,4096]{1,2,0:T(8,128)}, f32[2,512,128]{2,1,0:T(8,128)S(1)...) while((s32[]{:T(128)}, f32[12288,128]{1,0:T(8,128)}, ...), condition=%wide.region_35.36_spmd.clone, body=%wide.region_16.35_spmd.clone.sunk | while | flops 19359428608 | bytes 96335152 | solution.py:56
  473.7 13.7 %multiply_reduce_fusion.12 = (f32[512,64]{0,1:T(8,128)S(1)}, f32[512,64]{0,1:T(8,128)S(1)}, f32[512,64]{0,1:T(8,128)S(1)}, f32[512,64]{0,1:T(8,128)S(1)}, f32[512,64]{0,1:T(8,128)S(1)}, /*index=5*/f32[512,64]{0,1:T(8,128)S(1)}) fusion(f32[512,64]{0,1:T(8,128)S(1)} %bitcast.421, f32[512,64]{0,1:T(8,128)S(1)} %dynamic-slice_bitcast_fusion.4, ...), kind=kOutput, calls=%fused_computation.177.clone.1 | convolution fusion | flops 3246194688 | bytes 20447236 | tf_op jit(solution)/shard_map/transpose(jvp())/while/body/eval_jaxpr/dot_general | solution.py:41
  499.2 10.1 %fusion.314 = f32[4096,128]{1,0:T(8,128)} fusion(f32[2,512,4096]{1,2,0:T(8,128)} %get-tuple-element.3157, s32[]{:T(128)S(6)} %sub.691, f32[2,512,128]{2,1,0:T(8,128)S(1)} %get-tuple-element.3156), kind=kOutput, calls=%fused_computation.168.clone.1 | convolution fusion | flops 3221225472 | bytes 10748928 | tf_op jit(solution)/shard_map/transpose(jvp())/while/body/eval_jaxpr/dot_general | solution.py:41
  549.0 13.7 %multiply_reduce_fusion.12 = (f32[512,64]{0,1:T(8,128)S(1)}, f32[512,64]{0,1:T(8,128)S(1)}, f32[512,64]{0,1:T(8,128)S(1)}, f32[512,64]{0,1:T(8,128)S(1)}, f32[512,64]{0,1:T(8,128)S(1)}, /*index=5*/f32[512,64]{0,1:T(8,128)S(1)}) fusion(f32[512,64]{0,1:T(8,128)S(1)} %bitcast.421, f32[512,64]{0,1:T(8,128)S(1)} %dynamic-slice_bitcast_fusion.4, ...), kind=kOutput, calls=%fused_computation.177.clone.1 | convolution fusion | flops 3246194688 | bytes 20447236 | tf_op jit(solution)/shard_map/transpose(jvp())/while/body/eval_jaxpr/dot_general | solution.py:41
  623.9 62.7 %psum.7 = f32[6,256]{1,0:T(8,128)} all-reduce(f32[6,256]{1,0:T(8,128)S(1)} %fusion.126), channel_id=1, replica_groups=mesh['gx'=16,'gy'=8] {'gx','gy'}, use_global_device_ids=true, to_apply=%region_38.39 | all-reduce | flops 1536 | bytes 12288 | tf_op jit(solution)/shard_map/psum | solution.py:213
  (382 shorter events, 277.6 us)
Async XLA Ops:
  8.3 21.5 %all-to-all-start = ((f32[128,2,12]{2,1,0:T(2,128)}), f32[128,2,12]{2,1,0:T(2,128)S(1)}, u32[]{:S(2)}, u32[]{:S(2)}) async-start(f32[128,2,12]{2,1,0:T(2,128)} %copy.89), calls=%async_computation | async-start | bytes 262144 | tf_op jit(solution)/shard_map/all_to_all | solution.py:179
  30.5 135.7 %copy-start.11 = (f32[1,128,256]{2,1,0:T(8,128)S(1)}, f32[1,128,256]{2,1,0:T(8,128)}, u32[]{:S(2)}) copy-start(f32[1,128,256]{2,1,0:T(8,128)} %param.27) | copy-start | bytes 393220
  30.5 135.7 %copy-start.32 = (f32[1,1,256,256]{3,2,1,0:T(8,128)S(1)}, f32[1,1,256,256]{3,2,1,0:T(8,128)}, u32[]{:S(2)}) copy-start(f32[1,1,256,256]{3,2,1,0:T(8,128)} %param.28) | copy-start | bytes 786436
  64.2 31.1 %slice-start.4 = ((s8[8388608]{0:T(1024)(128)(4,1)}), s8[4194304]{0:T(1024)(128)(4,1)S(1)}, s32[]{:S(2)}) async-start(s8[8388608]{0:T(1024)(128)(4,1)} %bitcast.414), calls=%async_computation.10 | async-start | bytes 8388608 | tf_op jit(solution)/shard_map/while
  120.0 31.1 %slice-start.4 = ((s8[8388608]{0:T(1024)(128)(4,1)}), s8[4194304]{0:T(1024)(128)(4,1)S(1)}, s32[]{:S(2)}) async-start(s8[8388608]{0:T(1024)(128)(4,1)} %bitcast.414), calls=%async_computation.10 | async-start | bytes 8388608 | tf_op jit(solution)/shard_map/while
  168.1 196.7 %all-to-all-start.1 = ((f32[128,2,4]{2,1,0:T(2,128)}), f32[128,2,4]{2,1,0:T(2,128)}, u32[]{:S(2)}, u32[]{:S(2)}) async-start(f32[128,2,4]{2,1,0:T(2,128)} %reshape.2828), calls=%async_computation.1 | async-start | bytes 262144 | tf_op jit(solution)/shard_map/all_to_all | solution.py:186
  178.7 182.9 %copy-start.12 = (f32[1,128,256]{2,1,0:T(8,128)S(1)}, f32[1,128,256]{2,1,0:T(8,128)}, u32[]{:S(2)}) copy-start(f32[1,128,256]{2,1,0:T(8,128)} %param.27) | copy-start | bytes 393220
  178.7 183.2 %copy-start.33 = (f32[1,1,256,256]{3,2,1,0:T(8,128)S(1)}, f32[1,1,256,256]{3,2,1,0:T(8,128)}, u32[]{:S(2)}) copy-start(f32[1,1,256,256]{3,2,1,0:T(8,128)} %param.28) | copy-start | bytes 786436
  209.9 30.9 %slice-start = ((s8[8388608]{0:T(1024)(128)(4,1)}), s8[4194304]{0:T(1024)(128)(4,1)S(1)}, s32[]{:S(2)}) async-start(s8[8388608]{0:T(1024)(128)(4,1)} %bitcast.405), calls=%async_computation.6 | async-start | bytes 8388608 | tf_op jit(solution)/shard_map/jvp()/while
  296.6 30.7 %slice-start = ((s8[8388608]{0:T(1024)(128)(4,1)}), s8[4194304]{0:T(1024)(128)(4,1)S(1)}, s32[]{:S(2)}) async-start(s8[8388608]{0:T(1024)(128)(4,1)} %bitcast.405), calls=%async_computation.6 | async-start | bytes 8388608 | tf_op jit(solution)/shard_map/jvp()/while
  363.4 60.8 %copy-start.10 = (f32[1,256,128]{2,1,0:T(8,128)S(1)}, f32[1,256,128]{2,1,0:T(8,128)}, u32[]{:S(2)}) copy-start(f32[1,256,128]{2,1,0:T(8,128)} %param.29) | copy-start | bytes 393220
  363.4 62.2 %copy-start.35 = (f32[256]{0:T(256)S(1)}, f32[256]{0:T(256)}, u32[]{:S(2)}) copy-start(f32[256]{0:T(256)} %convert.8) | copy-start | bytes 3076
  364.8 23.3 %all-to-all-start.2 = ((f32[128,2,512]{2,1,0:T(2,128)}), f32[128,2,512]{2,1,0:T(2,128)S(1)}, u32[]{:S(2)}, u32[]{:S(2)}) async-start(f32[128,2,512]{2,1,0:T(2,128)} %reshape.2830), calls=%async_computation.2 | async-start | bytes 1048576 | tf_op jit(solution)/shard_map/all_to_all | solution.py:185
  391.6 14.6 %all-to-all-start.3 = ((f32[128,2,4]{2,1,0:T(2,128)}), f32[128,2,4]{2,1,0:T(2,128)S(1)}, u32[]{:S(2)}, u32[]{:S(2)}) async-start(f32[128,2,4]{2,1,0:T(2,128)} %copy.96), calls=%async_computation.3 | async-start | bytes 262144 | tf_op jit(solution)/shard_map/all_to_all | solution.py:203
  406.2 17.7 %all-to-all-start.4 = ((f32[128,2,512]{2,1,0:T(2,128)}), f32[128,2,512]{2,1,0:T(2,128)S(1)}, u32[]{:S(2)}, u32[]{:S(2)}) async-start(f32[128,2,512]{2,1,0:T(2,128)} %copy.98), calls=%async_computation.4 | async-start | bytes 1048576 | tf_op jit(solution)/shard_map/all_to_all | solution.py:202
  430.4 182.7 %copy-start.5 = (bf16[2,512,128]{2,1,0:T(8,128)(2,1)S(1)}, bf16[2,512,128]{2,1,0:T(8,128)(2,1)}, u32[]{:S(2)}) copy-start(bf16[2,512,128]{2,1,0:T(8,128)(2,1)} %copy-done.4) | copy-start | bytes 786436
  430.5 182.7 %copy-start.7 = (bf16[1024,256]{1,0:T(8,128)(2,1)S(1)}, bf16[1024,256]{1,0:T(8,128)(2,1)}, u32[]{:S(2)}) copy-start(bf16[1024,256]{1,0:T(8,128)(2,1)} %copy-done.6) | copy-start | bytes 1572868
  430.5 192.8 %copy-start.15 = (f32[32,4,4]{0,2,1:T(4,128)S(1)}, f32[32,4,4]{0,2,1:T(4,128)}, u32[]{:S(2)}) copy-start(f32[32,4,4]{0,2,1:T(4,128)} %copy-done.14) | copy-start | bytes 6148
  430.5 192.8 %copy-start.17 = (s32[32,4]{0,1:T(4,128)S(1)}, s32[32,4]{0,1:T(4,128)}, u32[]{:S(2)}) copy-start(s32[32,4]{0,1:T(4,128)} %multiply_add_fusion.2) | copy-start | bytes 1540
  430.5 193.2 %copy-start.20 = (f32[3,32]{1,0:T(4,128)S(1)}, f32[3,32]{1,0:T(4,128)}, u32[]{:S(2)}) copy-start(f32[3,32]{1,0:T(4,128)} %param.20) | copy-start | bytes 1156
  430.5 193.2 %copy-start.21 = (f32[3,32]{1,0:T(4,128)S(1)}, f32[3,32]{1,0:T(4,128)}, u32[]{:S(2)}) copy-start(f32[3,32]{1,0:T(4,128)} %param.19) | copy-start | bytes 1156
  430.5 193.2 %copy-start.34 = (s32[32]{0:T(128)S(1)}, s32[32]{0:T(128)}, u32[]{:S(2)}) copy-start(s32[32]{0:T(128)} %param.22) | copy-start | bytes 388
  607.0 79.6 %copy-start.1 = (f32[6,256]{1,0:T(8,128)S(1)}, f32[6,256]{1,0:T(8,128)}, u32[]{:S(2)}) copy-start(f32[6,256]{1,0:T(8,128)} %param.31) | copy-start | bytes 18436
  608.7 14.5 %all-to-all-start.5 = ((f32[128,2,12]{2,1,0:T(2,128)}), f32[128,2,12]{2,1,0:T(2,128)S(1)}, u32[]{:S(2)}, u32[]{:S(2)}) async-start(f32[128,2,12]{2,1,0:T(2,128)} %reshape.2838), calls=%async_computation.5 | async-start | bytes 262144 | tf_op jit(solution)/shard_map/all_to_all | solution.py:209
  (32 other events, 520.7 us)
where the time goes:
time: 691 us; the launch traced here: 687 us
  matrix products  320 us (46%)
  other arithmetic  83.6 us (12%)
  local copies, waits for them, and re-layouts  71.2 us (10%)
  blocking collectives  62.7 us (9%)
  loops' own time  60.5 us (9%)
  starting transfers between devices  43.9 us (6%)
  waiting for transfers between devices  42.7 us (6%)
    dot_general x24, matrix products, lookup_block(): jnp.dot(table, plane_rows, precision=lax.Precision.HIGHEST, preferred_ele...  305 us
    psum x1, blocking collectives, per_device(): pose_grad = lax.psum(pose_local, ('gx', 'gy'))  62.7 us
    another operation x3, loops' own time, lookup(): return lax.map(one_block, grouped).reshape(count, planes_flat.shape[1])  60.5 us
    dynamic_update_slice x46, local copies, waits for them, and re-layouts, lookup(): return lax.map(one_block, grouped).reshape(count, planes_flat.shape[1])  43.5 us
    mul x4, other arithmetic, lookup_block(): row_factor[:, :, None] * col_factor[:, None, :]  37.7 us
    add_any x2, other arithmetic, lookup_block(): planes_flat[plane_index * P_SIZE * P_SIZE:(plane_index + 1) * P_SIZE * P_...  17.8 us
  transfers between devices with their start and end apart: 6, of which 5 were waited for; matrix products, arithmetic and copies ran while one was open for 27% of the time, Pallas kernels for 0%

commit v1 on v0

v1 whole, which is shorter than its diff:
```python
import jax
import jax.numpy as jnp
from jax import lax
from jax.experimental import pallas as pl
from jax.experimental.pallas import tpu as pltpu
from jax.sharding import PartitionSpec as P

K = 4
S = 4
CELLS = 64
LANES = 128
STEP = 0.125
AXES = ("gx", "gy")
F32 = jnp.float32
BF16 = jnp.bfloat16
EXACT = lax.Precision.HIGHEST


def contract(left, right, left_dim, right_dim, precision=None):
    return lax.dot_general(
        left,
        right,
        (((left_dim,), (right_dim,)), ((), ())),
        precision=precision,
        preferred_element_type=F32,
    )


def iota(shape, dim):
    return lax.broadcasted_iota(jnp.int32, shape, dim)


def eye(size):
    return (iota((size, size), 0) == iota((size, size), 1)).astype(F32)


def dispatch_kernel(anchors, directions, start, cameras, ids, ranks, out, route, packed):
    rays = anchors.shape[1]
    segs = rays * K
    bricks = route.shape[0] // 2
    spread = (iota((rays, segs), 0) == iota((rays, segs), 1) % rays).astype(F32)
    own = iota((K, segs), 0) == iota((K, segs), 1) // rays
    id4 = contract(ids[...].astype(F32), spread, 0, 0, EXACT)
    id_row = jnp.sum(jnp.where(own, id4, 0.0), axis=0, keepdims=True)
    rank4 = contract(ranks[...].astype(F32), spread, 0, 0, EXACT)
    rank_row = jnp.sum(jnp.where(own, rank4, 0.0), axis=0, keepdims=True)
    packed[0:3, :] = contract(anchors[...], spread, 1, 0, EXACT)
    packed[3:6, :] = contract(directions[...], spread, 1, 0, EXACT)
    packed[6:7, :] = contract(start[...], spread, 1, 0, EXACT) + rank_row * (S * STEP)
    packed[7:8, :] = contract(cameras[...].astype(F32), spread, 1, 0, EXACT)
    onehot = (iota((bricks, segs), 0) == id_row.astype(jnp.int32)).astype(F32)
    earlier = (iota((segs, segs), 0) < iota((segs, segs), 1)).astype(F32)
    before = contract(onehot, earlier, 1, 0)
    for slot in range(2):
        taken = jnp.where((before > 0.5) == (slot == 1), onehot, 0.0)
        route[slot * bricks : (slot + 1) * bricks, :] = taken
        rows = contract(taken, packed[...], 1, 1, EXACT)
        out[:, slot * LANES : slot * LANES + 8] = rows


def dispatch(anchors, directions, start, cameras, ids, ranks, bricks):
    rays = anchors.shape[1]
    return pl.pallas_call(
        dispatch_kernel,
        out_shape=(
            jax.ShapeDtypeStruct((bricks, 2 * LANES), F32),
            jax.ShapeDtypeStruct((2 * bricks, rays * K), F32),
        ),
        scratch_shapes=[pltpu.VMEM((8, rays * K), F32)],
        name="dispatch",
    )(anchors, directions, start, cameras, ids, ranks)


def ray_rows(received, poses, sources):
    cols = contract(received[...], eye(sources), 0, 0, EXACT)
    rows = jnp.concatenate([cols[0:8], cols[LANES : LANES + 8]], axis=1)
    slots = 2 * sources
    cams = poses.shape[1]
    picked = (iota((cams, slots), 0) == rows[7:8].astype(jnp.int32)).astype(F32)
    pose = contract(poses[...], picked, 1, 0, EXACT)
    return rows, picked, pose


def cross(a, b):
    return (
        a[1] * b[2] - a[2] * b[1],
        a[2] * b[0] - a[0] * b[2],
        a[0] * b[1] - a[1] * b[0],
    )


def sample_rows(rows, pose):
    anchor = [rows[i : i + 1] for i in range(3)]
    direction = [rows[3 + i : 4 + i] for i in range(3)]
    turn = [pose[i : i + 1] for i in range(3)]
    shift = [pose[3 + i : 4 + i] for i in range(3)]
    turned = cross(turn, anchor)
    moved = [anchor[i] + turned[i] + shift[i] for i in range(3)]
    bent = cross(turn, direction)
    heading = [direction[i] + bent[i] for i in range(3)]
    distance = [rows[6:7] + (s + 0.5) * STEP for s in range(S)]
    return [
        jnp.concatenate([moved[i] + distance[s] * heading[i] for s in range(S)], axis=1)
        for i in range(3)
    ]


def factors(coordinate):
    count = coordinate.shape[1]
    scaled = coordinate * CELLS
    floor_c = jnp.floor(scaled)
    fraction = scaled - floor_c
    weight = fraction * fraction * (3.0 - 2.0 * fraction)
    slope = (6.0 * CELLS) * fraction * (1.0 - fraction)
    low = lax.bitwise_and(floor_c.astype(jnp.int32), CELLS - 1)
    high = lax.bitwise_and(low + 1, CELLS - 1)
    cell = iota((CELLS, count), 0)
    at_low = cell == low
    at_high = cell == high
    value = jnp.where(at_low, 1.0 - weight, 0.0) + jnp.where(at_high, weight, 0.0)
    change = jnp.where(at_high, slope, 0.0) - jnp.where(at_low, slope, 0.0)
    return value, change


BLOCK = 1024
TILE = 256


def plane_axes(step):
    plane = step // (CELLS * CELLS // BLOCK)
    first = plane // 2
    second = jnp.minimum(plane + 1, 2)
    start = (step % (CELLS * CELLS // BLOCK)) * (BLOCK // CELLS)
    return first * CELLS + start, second * CELLS, first, second


def table_tile(rows_ref, row_base, part, columns, lane):
    pieces = []
    for i in range(TILE // CELLS):
        row = rows_ref[pl.ds(row_base + part * (TILE // CELLS) + i, 1), lane : lane + TILE]
        pieces.append((row * columns).astype(BF16))
    return jnp.concatenate(pieces, axis=0)


def forward_kernel(
    received, poses, planes, first_w, hidden_w, feature_w, density_w,
    out, rows_out, pose_out, factor_out, slope_out, feats_out, v1_out, v2_out, colors_out, dens_out,
    total, turned,
):
    step = pl.program_id(0)
    sources = received.shape[0]
    count = 2 * sources * S

    @pl.when(step == 0)
    def _():
        rows, _, pose = ray_rows(received, poses, sources)
        rows_out[...] = rows
        pose_out[...] = jnp.concatenate([pose, pose[0:2]], axis=0)
        for axis, coordinate in enumerate(sample_rows(rows, pose)):
            value, change = factors(coordinate)
            factor_out[axis * CELLS : (axis + 1) * CELLS, :] = value
            slope_out[axis * CELLS : (axis + 1) * CELLS, :] = change
        total[...] = jnp.zeros_like(total)

    row_base, col_base, _, _ = plane_axes(step)
    turned[...] = planes[...].T.astype(BF16)
    for lane in range(0, count, TILE):
        columns = factor_out[pl.ds(pl.multiple_of(col_base, CELLS), CELLS), lane : lane + TILE]
        acc = total[:, lane : lane + TILE]
        for part in range(BLOCK // TILE):
            tile = table_tile(factor_out, row_base, part, columns, lane)
            acc = acc + contract(turned[:, part * TILE : (part + 1) * TILE], tile, 1, 0)
        total[:, lane : lane + TILE] = acc

    @pl.when(step == pl.num_programs(0) - 1)
    def _():
        slots = 2 * sources
        feats = total[...].astype(BF16)
        feats_out[...] = feats
        v1 = contract(first_w[...].T.astype(BF16), feats, 1, 0)
        v1_out[...] = v1
        h1 = (v1 * jax.nn.sigmoid(v1)).astype(BF16)
        v2 = contract(hidden_w[...].T.astype(BF16), h1, 1, 0)
        v2_out[...] = v2
        h2 = (v2 * jax.nn.sigmoid(v2)).astype(BF16)
        colors = jnp.tanh(contract(feature_w[...].T.astype(BF16), h2, 1, 0))
        colors_out[...] = colors
        raw = contract(density_w[...].astype(BF16), h2, 1, 0)
        dens_out[...] = raw
        depth = (jnp.maximum(raw, 0.0) + jnp.log1p(jnp.exp(-jnp.abs(raw)))) * STEP
        seg = jnp.zeros((LANES, slots), F32)
        front = jnp.zeros((1, slots), F32)
        for s in range(S):
            e = depth[:, s * slots : (s + 1) * slots]
            weight = jnp.exp(-front) * (1.0 - jnp.exp(-e))
            seg = seg + weight * colors[:, s * slots : (s + 1) * slots]
            front = front + e
        through = jnp.exp(-front)
        out[:, 0:LANES] = seg[:, 0:sources].T
        out[:, LANES : 2 * LANES] = seg[:, sources:slots].T
        sub = iota((8, sources), 0)
        both = jnp.where(
            sub == 0, through[:, 0:sources], jnp.where(sub == 1, through[:, sources:slots], 0.0)
        )
        place = (iota((8, LANES), 0) == iota((8, LANES), 1)).astype(F32)
        out[:, 2 * LANES : 3 * LANES] = contract(both, place, 0, 0, EXACT)


def whole(shape):
    return pl.BlockSpec(shape, lambda step: (0,) * len(shape))


def forward(received, poses, planes, first_w, hidden_w, feature_w, density_w):
    sources = received.shape[0]
    slots = 2 * sources
    count = slots * S
    channels = planes.shape[1]
    hidden = first_w.shape[1]
    outs = [
        ((sources, 3 * LANES), F32),
        ((8, slots), F32),
        ((8, slots), F32),
        ((3 * CELLS, count), F32),
        ((3 * CELLS, count), F32),
        ((channels, count), BF16),
        ((hidden, count), F32),
        ((hidden, count), F32),
        ((channels, count), F32),
        ((1, count), F32),
    ]
    ins = [received, poses, planes, first_w, hidden_w, feature_w, density_w]
    specs = [whole(x.shape) for x in ins]
    specs[2] = pl.BlockSpec((BLOCK, channels), lambda step: (step, 0))
    return pl.pallas_call(
        forward_kernel,
        grid=(planes.shape[0] // BLOCK,),
        in_specs=specs,
        out_specs=[whole(shape) for shape, _ in outs],
        out_shape=[jax.ShapeDtypeStruct(shape, kind) for shape, kind in outs],
        scratch_shapes=[pltpu.VMEM((channels, count), F32), pltpu.VMEM((channels, BLOCK), BF16)],
        compiler_params=pltpu.CompilerParams(vmem_limit_bytes=40 * 2**20),
        name="forward",
    )(*ins)


def slope_kernel(factor, slope, planes, out, turned):
    step = pl.program_id(0)
    count = factor.shape[1]

    @pl.when(step == 0)
    def _():
        out[...] = jnp.zeros_like(out)

    row_base, col_base, first, second = plane_axes(step)
    turned[...] = planes[...].T.astype(BF16)
    for rows_ref, cols_ref, axis in ((slope, factor, first), (factor, slope, second)):
        base = pl.multiple_of(axis * LANES, LANES)
        for lane in range(0, count, TILE):
            columns = cols_ref[pl.ds(pl.multiple_of(col_base, CELLS), CELLS), lane : lane + TILE]
            acc = out[pl.ds(base, LANES), lane : lane + TILE]
            for part in range(BLOCK // TILE):
                tile = table_tile(rows_ref, row_base, part, columns, lane)
                acc = acc + contract(turned[:, part * TILE : (part + 1) * TILE], tile, 1, 0)
            out[pl.ds(base, LANES), lane : lane + TILE] = acc


def slopes(factor, slope, planes):
    count = factor.shape[1]
    channels = planes.shape[1]
    return pl.pallas_call(
        slope_kernel,
        grid=(planes.shape[0] // BLOCK,),
        in_specs=[
            whole(factor.shape),
            whole(slope.shape),
            pl.BlockSpec((BLOCK, channels), lambda step: (step, 0)),
        ],
        out_specs=whole((3 * channels, count)),
        out_shape=jax.ShapeDtypeStruct((3 * channels, count), F32),
        scratch_shapes=[pltpu.VMEM((channels, BLOCK), BF16)],
        compiler_params=pltpu.CompilerParams(vmem_limit_bytes=40 * 2**20),
        name="slopes",
    )(factor, slope, planes)


def rays_kernel(home, route, ranks, targets, ray_out, back, grads):
    bricks = home.shape[0]
    rays = targets.shape[0]
    slot = [route[0:bricks, :].T, route[bricks : 2 * bricks, :].T]
    seg = contract(slot[0], home[:, 0:LANES], 1, 0, EXACT) + contract(
        slot[1], home[:, LANES : 2 * LANES], 1, 0, EXACT
    )
    lane = iota((1, LANES), 1)
    through = home[:, 2 * LANES : 3 * LANES]
    passing = jnp.sum(
        contract(slot[0], jnp.where(lane == 0, through, 0.0), 1, 0, EXACT)
        + contract(slot[1], jnp.where(lane == 1, through, 0.0), 1, 0, EXACT),
        axis=1,
        keepdims=True,
    )
    feature = [seg[k * rays : (k + 1) * rays] for k in range(K)]
    pass_k = [passing[k * rays : (k + 1) * rays] for k in range(K)]
    rank = [ranks[:, k : k + 1] for k in range(K)]
    ones = jnp.ones((rays, 1), F32)

    def seen(k, skip=None):
        product = ones
        for other in range(K):
            if other != k and other != skip:
                product = product * jnp.where(rank[other] < rank[k], pass_k[other], 1.0)
        return product

    transmit = [seen(k) for k in range(K)]
    ray = jnp.zeros_like(feature[0])
    for k in range(K):
        ray = ray + transmit[k] * feature[k]
    ray_out[...] = ray
    grad = ray - targets[...]
    pull = [jnp.sum(grad * feature[k], axis=1, keepdims=True) for k in range(K)]
    for k in range(K):
        grads[k * rays : (k + 1) * rays, 0:LANES] = transmit[k] * grad
        pass_grad = jnp.zeros((rays, 1), F32)
        for behind in range(K):
            if behind != k:
                pass_grad = pass_grad + jnp.where(
                    rank[k] < rank[behind], pull[behind] * seen(behind, k), 0.0
                )
        grads[k * rays : (k + 1) * rays, LANES : 2 * LANES] = jnp.broadcast_to(
            pass_grad, (rays, LANES)
        )
    spread = None
    for c in range(2):
        both = contract(route[c * bricks : (c + 1) * bricks, :], grads[...], 1, 0, EXACT)
        back[:, c * LANES : (c + 1) * LANES] = both[:, 0:LANES]
        own = jnp.where(lane == c, both[:, LANES : 2 * LANES], 0.0)
        spread = own if spread is None else spread + own
    back[:, 2 * LANES : 3 * LANES] = spread


def rays_step(home, route, ranks, targets):
    return pl.pallas_call(
        rays_kernel,
        out_shape=(
            jax.ShapeDtypeStruct(targets.shape, F32),
            jax.ShapeDtypeStruct(home.shape, F32),
        ),
        scratch_shapes=[pltpu.VMEM((route.shape[1], 2 * LANES), F32)],
        name="rays",
    )(home, route, ranks, targets)


def backward_kernel(
    cot, feats, v1_ref, v2_ref, colors_ref, dens_ref, slope_ref, rows_ref, pose_ref,
    first_w, hidden_w, feature_w, density_w,
    first_g, hidden_g, feature_g, density_g, feat_cot, pose_g,
    color_cot,
):
    sources = cot.shape[0]
    slots = 2 * sources
    seg_cot = jnp.concatenate([cot[:, 0:LANES].T, cot[:, LANES : 2 * LANES].T], axis=1)
    turned = cot[:, 2 * LANES : 3 * LANES].T
    pass_cot = jnp.concatenate([turned[0:1], turned[1:2]], axis=1)
    raw = dens_ref[...]
    depth = (jnp.maximum(raw, 0.0) + jnp.log1p(jnp.exp(-jnp.abs(raw)))) * STEP
    front = jnp.zeros((1, slots), F32)
    weights, kept, pulls = [], [], []
    for s in range(S):
        span = slice(s * slots, (s + 1) * slots)
        e = depth[:, span]
        reach = jnp.exp(-front)
        weight = reach * (1.0 - jnp.exp(-e))
        colors = colors_ref[:, span]
        pulls.append(jnp.sum(colors * seg_cot, axis=0, keepdims=True))
        color_cot[:, span] = (weight * seg_cot * (1.0 - colors * colors)).astype(BF16)
        weights.append(weight)
        kept.append(reach * jnp.exp(-e))
        front = front + e
    behind = pass_cot * jnp.exp(-front)
    depth_cot = [None] * S
    for s in reversed(range(S)):
        depth_cot[s] = pulls[s] * kept[s] - behind
        behind = behind + pulls[s] * weights[s]
    raw_cot = (jnp.concatenate(depth_cot, axis=1) * STEP * jax.nn.sigmoid(raw)).astype(BF16)

    v2 = v2_ref[...]
    gate2 = jax.nn.sigmoid(v2)
    h2 = (v2 * gate2).astype(BF16)
    color_c = color_cot[...]
    feature_g[...] = contract(h2, color_c, 1, 1).astype(BF16).astype(F32)
    density_g[...] = contract(raw_cot, h2, 1, 1).astype(BF16).astype(F32)
    wide = jnp.where(iota((8, 1), 0) == 0, density_w[...].astype(F32), 0.0).astype(BF16)
    wide_cot = jnp.where(iota((8, 1), 0) == 0, raw_cot.astype(F32), 0.0).astype(BF16)
    h2_cot = (
        contract(feature_w[...].astype(BF16), color_c, 1, 0) + contract(wide.T, wide_cot, 1, 0)
    ).astype(BF16).astype(F32)
    v2_cot = (h2_cot * gate2 * (1.0 + v2 * (1.0 - gate2))).astype(BF16)
    v1 = v1_ref[...]
    gate1 = jax.nn.sigmoid(v1)
    h1 = (v1 * gate1).astype(BF16)
    hidden_g[...] = contract(h1, v2_cot, 1, 1).astype(BF16).astype(F32)
    h1_cot = contract(hidden_w[...].astype(BF16), v2_cot, 1, 0).astype(BF16).astype(F32)
    v1_cot = (h1_cot * gate1 * (1.0 + v1 * (1.0 - gate1))).astype(BF16)
    first_g[...] = contract(feats[...], v1_cot, 1, 1).astype(BF16).astype(F32)
    f_cot = contract(first_w[...].astype(BF16), v1_cot, 1, 0).astype(BF16).astype(F32)
    feat_cot[...] = f_cot.T.astype(BF16)

    pull = [
        jnp.sum(slope_ref[a * LANES : (a + 1) * LANES, :] * f_cot, axis=0, keepdims=True)
        for a in range(3)
    ]
    rows = rows_ref[...]
    shift = [jnp.zeros((1, slots), F32)] * 3
    turn = [jnp.zeros((1, slots), F32)] * 3
    for s in range(S):
        distance = rows[6:7] + (s + 0.5) * STEP
        place = [rows[i : i + 1] + distance * rows[3 + i : 4 + i] for i in range(3)]
        part = [pull[a][:, s * slots : (s + 1) * slots] for a in range(3)]
        twist = cross(place, part)
        for a in range(3):
            shift[a] = shift[a] + part[a]
            turn[a] = turn[a] + twist[a]
    sub = iota((8, slots), 0)
    grads = jnp.zeros((8, slots), F32)
    for a in range(3):
        grads = jnp.where(sub == a, turn[a], grads)
        grads = jnp.where(sub == 3 + a, shift[a], grads)
    cams = pose_g.shape[1]
    picked = (iota((cams, slots), 0) == rows[7:8].astype(jnp.int32)).astype(F32)
    pose_g[...] = contract(grads, picked, 1, 1, EXACT)


def backward(cot, saved, slope, rows, pose, weights, cams):
    feats, v1, v2, colors, dens = saved
    count = feats.shape[1]
    outs = [(w.shape, F32) for w in weights]
    outs += [((count, feats.shape[0]), BF16), ((8, cams), F32)]
    return pl.pallas_call(
        backward_kernel,
        out_shape=[jax.ShapeDtypeStruct(shape, kind) for shape, kind in outs],
        scratch_shapes=[pltpu.VMEM((feats.shape[0], count), BF16)],
        compiler_params=pltpu.CompilerParams(vmem_limit_bytes=40 * 2**20),
        name="backward",
    )(cot, feats, v1, v2, colors, dens, slope, rows, pose, *weights)


def plane_kernel(factor, cot, out):
    step = pl.program_id(0)
    count = factor.shape[1]
    row_base, col_base, _, _ = plane_axes(step)
    for part in range(BLOCK // TILE):
        acc = jnp.zeros((TILE, cot.shape[1]), F32)
        for lane in range(0, count, TILE):
            columns = factor[pl.ds(pl.multiple_of(col_base, CELLS), CELLS), lane : lane + TILE]
            tile = table_tile(factor, row_base, part, columns, lane)
            acc = acc + contract(tile, cot[lane : lane + TILE, :], 1, 0)
        out[part * TILE : (part + 1) * TILE, :] = acc


def plane_grads(factor, cot, cells):
    channels = cot.shape[1]
    return pl.pallas_call(
        plane_kernel,
        grid=(cells // BLOCK,),
        in_specs=[whole(factor.shape), whole(cot.shape)],
        out_specs=pl.BlockSpec((BLOCK, channels), lambda step: (step, 0)),
        out_shape=jax.ShapeDtypeStruct((cells, channels), F32),
        compiler_params=pltpu.CompilerParams(vmem_limit_bytes=40 * 2**20),
        name="plane_grads",
    )(factor, cot)


def exchange(rows):
    wide = rows.reshape(rows.shape[0], 1, rows.shape[1])
    moved = lax.all_to_all(wide, AXES, split_axis=0, concat_axis=0, tiled=True)
    return moved.reshape(rows.shape)


def share_sum(part, axis):
    size = lax.axis_size(axis)
    copies = jnp.broadcast_to(part[None], (size,) + part.shape)
    gathered = lax.all_to_all(copies, (axis,), split_axis=0, concat_axis=0, tiled=True)
    return jnp.sum(gathered, axis=0)


def per_device(
    anchors, directions, ray_start, camera_ids, brick_ids, brick_rank, targets,
    planes, first_weight, hidden_weight, feature_weight, density_weight, poses,
):
    bricks = lax.axis_size(AXES)
    table = planes[0]
    weights = (first_weight[0], hidden_weight[0, 0], feature_weight[0], density_weight)
    outgoing, route = dispatch(
        anchors, directions, ray_start[None], camera_ids[None], brick_ids, brick_rank, bricks
    )
    received = exchange(outgoing)
    sent, rows, pose, factor, slope, *saved = forward(received, poses, table, *weights)
    home = exchange(sent)
    feature_slopes = slopes(factor, slope, table)
    ray_feature, back = rays_step(home, route, brick_rank, targets)
    cot = exchange(back)
    first_g, hidden_g, feature_g, density_g, feat_cot, pose_part = backward(
        cot, saved, feature_slopes, rows, pose, weights, poses.shape[1]
    )
    pose_grad = share_sum(share_sum(pose_part, "gy"), "gx")[0:6]
    plane_grad = plane_grads(factor, feat_cot, table.shape[0])
    return (
        ray_feature,
        plane_grad[None],
        first_g[None],
        hidden_g[None, None],
        feature_g[None],
        density_g,
        pose_grad,
    )


def solution(mesh):
    rays = P(AXES)
    in_specs = (
        P(None, AXES), P(None, AXES), rays, rays, P(AXES, None), P(AXES, None), P(AXES, None),
        P(AXES, None, None), P(AXES, None, None), P(AXES, None, None, None), P(AXES, None, None),
        P(AXES, None), P(),
    )
    out_specs = (
        P(AXES, None), P(AXES, None, None), P(AXES, None, None), P(AXES, None, None, None),
        P(AXES, None, None), P(AXES, None), P(),
    )
    return jax.shard_map(
        per_device, mesh=mesh, in_specs=in_specs, out_specs=out_specs, check_vma=False
    )
```

time: 691 us -> 127 us (0.18)
  matrix products: 320 us -> 0 us
  other arithmetic: 83.6 us -> 0.63 us
  loops' own time: 60.5 us -> 0 us
  waiting for transfers between devices: 42.7 us -> 0.01 us
  local copies, waits for them, and re-layouts: 71.2 us -> 30.9 us
  Pallas kernels: 0 us -> 36.2 us
  starting transfers between devices: 43.9 us -> 12 us
  blocking collectives: 62.7 us -> 45.6 us
    dot_general x47 -> x0, matrix products: 320 us -> none  [the longest x24 305 us: lookup_block(): jnp.dot(table, plane_rows, precision=lax.Precision.HIGHEST, preferred_ele...]
    psum x1 -> x0, blocking collectives: 62.7 us -> none  [per_device(): pose_grad = lax.psum(pose_local, ('gx', 'gy'))]
    another operation x3 -> x0, loops' own time: 60.5 us -> none  [lookup(): return lax.map(one_block, grouped).reshape(count, planes_flat.shape[1])]
    all_to_all x0 -> x3, blocking collectives: none -> 45.6 us  [the longest x2 36 us: exchange(): moved = lax.all_to_all(wide, AXES, split_axis=0, concat_axis=0, tiled=True)]
    dynamic_update_slice x46 -> x0, local copies, waits for them, and re-layouts: 43.5 us -> none  [lookup(): return lax.map(one_block, grouped).reshape(count, planes_flat.shape[1])]
    all_to_all x6 -> x2, waiting for transfers between devices: 42.7 us -> 0.01 us  [the longest x1 0.01 us: exchange(): moved = lax.all_to_all(wide, AXES, split_axis=0, concat_axis=0, tiled=True)]
    mul x20 -> x0, other arithmetic: 38.7 us -> none  [the longest x4 37.7 us: lookup_block(): row_factor[:, :, None] * col_factor[:, None, :]]
    pallas_call x0 -> x6, Pallas kernels: none -> 36.2 us  [the longest x1 9.96 us: slopes(): pl.pallas_call(slope_kernel, grid=(planes.shape[0] // BLOCK,), in_specs=[...]
  transfers between devices with their start and end apart: 6 -> 2, of which waited for: 5 -> 0; matrix products, arithmetic and copies ran while one was open for 27% -> 0% of each run, Pallas kernels for 0% -> 16%
where the time goes in v1:
time: 127 us; the launch traced here: 126 us
  blocking collectives  45.6 us (36%)
  Pallas kernels  36.2 us (29%)
  local copies, waits for them, and re-layouts  30.9 us (24%)
  starting transfers between devices  12 us (9%)
    all_to_all x2, blocking collectives, exchange(): moved = lax.all_to_all(wide, AXES, split_axis=0, concat_axis=0, tiled=True)  36 us
    unnamed x51, local copies, waits for them, and re-layouts  27.2 us
    pallas_call x1, Pallas kernels, slopes(): pl.pallas_call(slope_kernel, grid=(planes.shape[0] // BLOCK,), in_specs=[...  9.96 us
    pallas_call x1, Pallas kernels, plane_grads(): pl.pallas_call(plane_kernel, grid=(cells // BLOCK,), in_specs=[whole(fact...  9.71 us
    all_to_all x1, blocking collectives, share_sum(): lax.all_to_all(copies, (axis,), split_axis=0, concat_axis=0, tiled=True)  9.57 us
    pallas_call x1, Pallas kernels, forward(): pl.pallas_call(forward_kernel, grid=(planes.shape[0] // BLOCK,), in_specs...  8.64 us
    all_to_all x1, starting transfers between devices, share_sum(): lax.all_to_all(copies, (axis,), split_axis=0, concat_axis=0, tiled=True)  7.04 us
    all_to_all x1, starting transfers between devices, exchange(): moved = lax.all_to_all(wide, AXES, split_axis=0, concat_axis=0, tiled=True)  4.94 us
  transfers between devices with their start and end apart: 2, of which 0 were waited for; matrix products, arithmetic and copies ran while one was open for 0% of the time, Pallas kernels for 16%

profile of v1, /device:TPU:1, one launch (start us, length us, event | category | flops | bytes accessed | tf_op | source)
XLA Modules:
  0.0 126.0 jit_solution(763885900977419295)
XLA Ops:
  0.6 1.4 %copy.30.ranks = s32[32,4]{1,0:T(8,128)} copy(s32[32,4]{0,1:T(4,128)} %param.18) | data formatting | bytes 1024 | tf_op args[5]
  2.0 1.4 %copy.29.ids = s32[32,4]{1,0:T(8,128)} copy(s32[32,4]{0,1:T(4,128)} %param.17) | data formatting | bytes 1024 | tf_op args[4]
  3.4 2.1 %dispatch.1 = (f32[128,256]{1,0:T(8,128)}, f32[256,128]{1,0:T(8,128)}) custom-call(f32[3,32]{1,0:T(4,128)} %anchors.1, f32[3,32]{1,0:T(4,128)} %directions.1, f32[1,32]{1,0:T(1,128)} %bitcast.39, s32[1,32]{1,0:T(1,128)} %bitcast.40, s32[32,4]{1,0:T(8,128)} %copy.29.ids, s32[32,4]{1,0:T(8,128)} %copy.30.ranks), custom_call_target="tpu_custom_call" | custom-call | tf_op jit(solution)/shard_map/dispatch/pallas_call | solution.py:63
  5.4 1.0 copy.31
  6.5 21.4 %all_to_all.25 = f32[128,1,256]{2,1,0:T(1,128)S(1)} all-to-all(f32[128,1,256]{2,1,0:T(1,128)S(1)} %copy.31), channel_id=1, replica_groups=mesh['gx'=16,'gy'=8] {'gx','gy'}, dimensions={0} | all-to-all | bytes 262144 | tf_op jit(solution)/shard_map/all_to_all | solution.py:474
  27.9 2.8 %copy-done = f32[1,12288,128]{2,1,0:T(8,128)S(1)} copy-done((f32[1,12288,128]{2,1,0:T(8,128)S(1)}, f32[1,12288,128]{2,1,0:T(8,128)}, u32[]{:S(2)}) %copy-start) | copy-done | bytes 6291480
  30.7 0.9 copy-done.4
  34.8 8.6 %forward.1 = (f32[128,384]{1,0:T(8,128)S(1)}, f32[8,256]{1,0:T(8,128)S(1)}, f32[8,256]{1,0:T(8,128)S(1)}, f32[192,1024]{1,0:T(8,128)S(1)}, f32[192,1024]{1,0:T(8...) custom-call(f32[128,256]{1,0:T(8,128)S(1)} %bitcast.32, ...), custom_call_target="tpu_custom_call" | custom-call | tf_op jit(solution)/shard_map/forward/pallas_call | solution.py:234
  43.5 1.0 copy-done.2
  47.7 14.6 %all_to_all.26 = f32[128,1,384]{2,1,0:T(1,128)S(1)} all-to-all(f32[128,1,384]{2,1,0:T(1,128)S(1)} %copy.32), channel_id=1, replica_groups=mesh['gx'=16,'gy'=8] {'gx','gy'}, dimensions={0} | all-to-all | bytes 393216 | tf_op jit(solution)/shard_map/all_to_all | solution.py:474
  62.9 2.9 %rays.1 = (f32[32,128]{1,0:T(8,128)}, f32[128,384]{1,0:T(8,128)}) custom-call(f32[128,384]{1,0:T(8,128)} %bitcast.35, f32[256,128]{1,0:T(8,128)} %get-tuple-element.29.route, s32[32,4]{1,0:T(8,128)} %copy.30.ranks, f32[32,128]{1,0:T(8,128)} %targets.1), custom_call_target="tpu_custom_call" | custom-call | tf_op jit(solution)/shard_map/rays/pallas_call | solution.py:341
  65.9 1.8 %copy.34 = f32[128,1,384]{2,1,0:T(1,128)} copy(f32[128,1,384]{2,0,1:T(8,128)} %bitcast.36) | data formatting | bytes 393216 | tf_op jit(solution)/shard_map/reshape | solution.py:473
  67.7 4.9 %all-to-all-start.2 = ((f32[128,1,384]{2,1,0:T(1,128)}), f32[128,1,384]{2,1,0:T(1,128)}, u32[]{:S(2)}, u32[]{:S(2)}) async-start(f32[128,1,384]{2,1,0:T(1,128)} %copy.34), calls=%async_computation.2 | async-start | bytes 393216 | tf_op jit(solution)/shard_map/all_to_all | solution.py:474
  72.6 2.8 %copy-done.1 = f32[1,12288,128]{2,1,0:T(8,128)S(1)} copy-done((f32[1,12288,128]{2,1,0:T(8,128)S(1)}, f32[1,12288,128]{2,1,0:T(8,128)}, u32[]{:S(2)}) %copy-start.1) | copy-done | bytes 6291480
  75.4 1.1 copy-done.7
  76.5 10.0 %slopes.1.slope_ref = f32[384,1024]{1,0:T(8,128)S(1)} custom-call(f32[192,1024]{1,0:T(8,128)S(1)} %get-tuple-element.31.factor, f32[192,1024]{1,0:T(8,128)S(1)} %copy-done.7, f32[12288,128]{1,0:T(8,128)S(1)} %bitcast.24), custom_call_target="tpu_custom_call" | custom-call | tf_op jit(solution)/shard_map/slopes/pallas_call | solution.py:270
  87.5 1.2 copy-done.3
  88.7 0.9 copy-done.5
  89.6 1.0 copy-done.9
  91.6 0.9 copy-done.15
  93.9 2.9 %backward.1 = (f32[128,256]{1,0:T(8,128)}, f32[256,256]{1,0:T(8,128)}, f32[256,128]{1,0:T(8,128)}, f32[1,256]{1,0:T(1,128)}, bf16[1024,128]{1,0:T(8,128)(2,1)S(1)}, /*index=5*/f32[8,256]{1,0:T(8,128)S(1)}) custom-call(f32[128,384]{1,0:T(8,128)S(1)} %bitcast.27, bf16[128,1024]{1,0:T(8,128)(2,1)S(1)} %copy-done.15, f32[256,1024]{1,0:T(8,128)S(1)} %get-tuple-element.34.v1_ref, ...), custom_call_target="tpu_custom_call" | custom-call | tf_op jit(solution)/shard_map/backward/pallas_call | solution.py:437
  97.5 9.6 %all_to_all.27 = f32[8,8,256]{2,1,0:T(8,128)S(1)} all-to-all(f32[8,8,256]{2,1,0:T(8,128)S(1)} %broadcast_in_dim.36), channel_id=1, replica_groups=mesh['gx'=16,'gy'=8] {'gy'}, dimensions={0} | all-to-all | bytes 131072 | tf_op jit(solution)/shard_map/all_to_all | solution.py:481
  107.7 7.0 %all-to-all-start.4 = ((f32[16,8,256]{2,1,0:T(8,128)}), f32[16,8,256]{2,1,0:T(8,128)S(1)}, u32[]{:S(2)}, u32[]{:S(2)}) async-start(f32[16,8,256]{2,1,0:T(8,128)} %broadcast_in_dim.37), calls=%async_computation.4 | async-start | bytes 262144 | tf_op jit(solution)/shard_map/all_to_all | solution.py:481
  115.7 9.7 %plane_grads.1 = f32[12288,128]{1,0:T(8,128)} custom-call(f32[192,1024]{1,0:T(8,128)S(1)} %get-tuple-element.31.factor, bf16[1024,128]{1,0:T(8,128)(2,1)S(1)} %copy-done.17), custom_call_target="tpu_custom_call" | custom-call | tf_op jit(solution)/shard_map/plane_grads/pallas_call | solution.py:461
  (47 shorter events, 13.2 us)
Async XLA Ops:
  27.9 2.8 %copy-start = (f32[1,12288,128]{2,1,0:T(8,128)S(1)}, f32[1,12288,128]{2,1,0:T(8,128)}, u32[]{:S(2)}) copy-start(f32[1,12288,128]{2,1,0:T(8,128)} %param.20) | copy-start | bytes 18874372
  30.7 0.9 copy-start.4
  31.6 0.9 copy-start.10
  32.6 0.9 copy-start.12
  33.5 0.7 copy-start.18
  34.2 0.7 copy-start.21
  43.5 1.0 copy-start.2
  44.5 0.9 copy-start.6
  45.3 0.8 copy-start.8
  46.2 0.7 copy-start.14
  47.5 40.0 %copy-start.11 = (f32[1,128,256]{2,1,0:T(8,128)S(1)}, f32[1,128,256]{2,1,0:T(8,128)}, u32[]{:S(2)}) copy-start(f32[1,128,256]{2,1,0:T(8,128)} %param.21) | copy-start | bytes 393220
  67.7 18.8 %all-to-all-start.2 = ((f32[128,1,384]{2,1,0:T(1,128)}), f32[128,1,384]{2,1,0:T(1,128)}, u32[]{:S(2)}, u32[]{:S(2)}) async-start(f32[128,1,384]{2,1,0:T(1,128)} %copy.34), calls=%async_computation.2 | async-start | bytes 393216 | tf_op jit(solution)/shard_map/all_to_all | solution.py:474
  72.6 2.8 %copy-start.1 = (f32[1,12288,128]{2,1,0:T(8,128)S(1)}, f32[1,12288,128]{2,1,0:T(8,128)}, u32[]{:S(2)}) copy-start(f32[1,12288,128]{2,1,0:T(8,128)} %param.20) | copy-start | bytes 18874372
  75.4 1.1 copy-start.7
  87.5 1.2 copy-start.3
  88.7 0.9 copy-start.5
  89.6 1.0 copy-start.9
  90.7 0.9 copy-start.13
  91.6 0.9 copy-start.15
  92.5 0.7 copy-start.20
  93.2 0.7 copy-start.22
  96.7 0.7 copy-start.16
  107.7 17.7 %all-to-all-start.4 = ((f32[16,8,256]{2,1,0:T(8,128)}), f32[16,8,256]{2,1,0:T(8,128)S(1)}, u32[]{:S(2)}, u32[]{:S(2)}) async-start(f32[16,8,256]{2,1,0:T(8,128)} %broadcast_in_dim.37), calls=%async_computation.4 | async-start | bytes 262144 | tf_op jit(solution)/shard_map/all_to_all | solution.py:481
  114.7 1.0 copy-start.17
  (1 other events, 0.6 us)

commit v2 on v1

v2 whole, which is shorter than its diff:
```python
import jax
import jax.numpy as jnp
from jax import lax
from jax.experimental import pallas as pl
from jax.experimental.pallas import tpu as pltpu
from jax.sharding import PartitionSpec as P

K = 4
S = 4
CELLS = 64
LANES = 128
STEP = 0.125
AXES = ("gx", "gy")
F32 = jnp.float32
BF16 = jnp.bfloat16
EXACT = lax.Precision.HIGHEST


def contract(left, right, left_dim, right_dim, precision=None):
    return lax.dot_general(
        left,
        right,
        (((left_dim,), (right_dim,)), ((), ())),
        precision=precision,
        preferred_element_type=F32,
    )


def iota(shape, dim):
    return lax.broadcasted_iota(jnp.int32, shape, dim)


def grant(mebibytes):
    return pltpu.CompilerParams(vmem_limit_bytes=mebibytes * 2**20)


def far(x):
    return pltpu.with_memory_space_constraint(x, pltpu.HBM)


def price(flops, moved):
    return pl.CostEstimate(flops=flops, bytes_accessed=moved, transcendentals=0)


def eye(size):
    return (iota((size, size), 0) == iota((size, size), 1)).astype(F32)


def spread_of(rays):
    segs = rays * K
    spread = (iota((rays, segs), 0) == iota((rays, segs), 1) % rays).astype(F32)
    own = iota((K, segs), 0) == iota((K, segs), 1) // rays
    return spread, own


def segment_row(table, spread, own):
    return jnp.sum(
        jnp.where(own, contract(table[...].astype(F32), spread, 1, 0, EXACT), 0.0), axis=0, keepdims=True
    )


def route_of(id_row, bricks):
    segs = id_row.shape[1]
    onehot = (iota((bricks, segs), 0) == id_row.astype(jnp.int32)).astype(F32)
    earlier = (iota((segs, segs), 0) < iota((segs, segs), 1)).astype(F32)
    before = contract(onehot, earlier, 1, 0)
    return [jnp.where((before > 0.5) == (slot == 1), onehot, 0.0) for slot in range(2)]


def dispatch_kernel(anchors, directions, start, cameras, ids, ranks, out, packed):
    bricks = out.shape[0] // 2
    spread, own = spread_of(anchors.shape[1])
    id_row = segment_row(ids, spread, own)
    packed[0:3, :] = contract(anchors[...], spread, 1, 0, EXACT)
    packed[3:6, :] = contract(directions[...], spread, 1, 0, EXACT)
    packed[6:7, :] = contract(start[...], spread, 1, 0, EXACT) + segment_row(ranks, spread, own) * (S * STEP)
    packed[7:8, :] = contract(cameras[...].astype(F32), spread, 1, 0, EXACT)
    for slot, taken in enumerate(route_of(id_row, bricks)):
        rows = contract(taken, packed[...], 1, 1, EXACT)
        both = jnp.concatenate([rows, jnp.zeros((bricks, LANES - 8), F32)], axis=1)
        out[pl.ds(slot, bricks, stride=2), :] = both


def dispatch(anchors, directions, start, cameras, ids, ranks, bricks):
    return pl.pallas_call(
        dispatch_kernel,
        out_shape=jax.ShapeDtypeStruct((2 * bricks, LANES), F32),
        scratch_shapes=[pltpu.VMEM((8, anchors.shape[1] * K), F32)],
        compiler_params=grant(2),
        name="dispatch",
    )(*map(far, (anchors, directions, start, cameras, ids, ranks)))


def ray_rows(received, poses, sources):
    same = eye(sources)
    rows = jnp.concatenate(
        [
            contract(received[pl.ds(slot, sources, stride=2), :], same, 0, 0, EXACT)[0:8]
            for slot in range(2)
        ],
        axis=1,
    )
    slots = 2 * sources
    cams = poses.shape[1]
    picked = (iota((cams, slots), 0) == rows[7:8].astype(jnp.int32)).astype(F32)
    pose = contract(poses[...], picked, 1, 0, EXACT)
    return rows, picked, pose


def cross(a, b):
    return (
        a[1] * b[2] - a[2] * b[1],
        a[2] * b[0] - a[0] * b[2],
        a[0] * b[1] - a[1] * b[0],
    )


def sample_rows(rows, pose):
    anchor = [rows[i : i + 1] for i in range(3)]
    direction = [rows[3 + i : 4 + i] for i in range(3)]
    turn = [pose[i : i + 1] for i in range(3)]
    shift = [pose[3 + i : 4 + i] for i in range(3)]
    turned = cross(turn, anchor)
    moved = [anchor[i] + turned[i] + shift[i] for i in range(3)]
    bent = cross(turn, direction)
    heading = [direction[i] + bent[i] for i in range(3)]
    distance = [rows[6:7] + (s + 0.5) * STEP for s in range(S)]
    return [
        jnp.concatenate([moved[i] + distance[s] * heading[i] for s in range(S)], axis=1)
        for i in range(3)
    ]


def factors(coordinate):
    count = coordinate.shape[1]
    scaled = coordinate * CELLS
    floor_c = jnp.floor(scaled)
    fraction = scaled - floor_c
    weight = fraction * fraction * (3.0 - 2.0 * fraction)
    slope = (6.0 * CELLS) * fraction * (1.0 - fraction)
    low = lax.bitwise_and(floor_c.astype(jnp.int32), CELLS - 1)
    high = lax.bitwise_and(low + 1, CELLS - 1)
    cell = iota((CELLS, count), 0)
    at_low = cell == low
    at_high = cell == high
    value = jnp.where(at_low, 1.0 - weight, 0.0) + jnp.where(at_high, weight, 0.0)
    change = jnp.where(at_high, slope, 0.0) - jnp.where(at_low, slope, 0.0)
    return value, change


BLOCK = 1024
TILE = 256


def plane_axes(step):
    plane = step // (CELLS * CELLS // BLOCK)
    first = plane // 2
    second = jnp.minimum(plane + 1, 2)
    start = (step % (CELLS * CELLS // BLOCK)) * (BLOCK // CELLS)
    return first * CELLS + start, second * CELLS, first, second


def table_tile(rows_ref, row_base, part, columns, lane):
    pieces = []
    for i in range(TILE // CELLS):
        row = rows_ref[pl.ds(row_base + part * (TILE // CELLS) + i, 1), lane : lane + TILE]
        pieces.append((row * columns).astype(BF16))
    return jnp.concatenate(pieces, axis=0)


def prepare_kernel(
    planes, first_w, hidden_w, feature_w, ids,
    turned, first_o, first_t, hidden_o, hidden_t, feature_o, feature_t, route,
):
    turned[...] = planes[...].T.astype(BF16)

    @pl.when(pl.program_id(0) == 0)
    def _():
        for source, plain, flipped in (
            (first_w, first_o, first_t),
            (hidden_w, hidden_o, hidden_t),
            (feature_w, feature_o, feature_t),
        ):
            plain[...] = source[...].astype(BF16)
            flipped[...] = source[...].T.astype(BF16)
        bricks = route.shape[0] // 2
        spread, own = spread_of(ids.shape[1])
        for slot, taken in enumerate(route_of(segment_row(ids, spread, own), bricks)):
            route[slot * bricks : (slot + 1) * bricks, :] = taken


def whole(shape):
    return pl.BlockSpec(shape, lambda step: (0,) * len(shape))


def prepare(planes, first_w, hidden_w, feature_w, ids, bricks):
    cells, channels = planes.shape
    ins = [planes, first_w, hidden_w, feature_w, ids]
    outs = [((channels, cells), BF16)]
    for w in (first_w, hidden_w, feature_w):
        outs += [(w.shape, BF16), (w.shape[::-1], BF16)]
    outs += [((2 * bricks, ids.shape[1] * K), F32)]
    in_specs = [whole(x.shape) for x in ins]
    in_specs[0] = pl.BlockSpec((2 * BLOCK, channels), lambda step: (step, 0))
    out_specs = [whole(shape) for shape, _ in outs]
    out_specs[0] = pl.BlockSpec((channels, 2 * BLOCK), lambda step: (0, step))
    return pl.pallas_call(
        prepare_kernel,
        grid=(cells // (2 * BLOCK),),
        in_specs=in_specs,
        out_specs=out_specs,
        out_shape=[pltpu.HBM(shape, kind) for shape, kind in outs],
        compiler_params=grant(8),
        cost_estimate=price(0, 10 * 2**20),
        name="prepare",
    )(*map(far, ins))


def fetch(sources, places, sems, first=0):
    copies = [
        pltpu.make_async_copy(source, place, sems.at[first + i])
        for i, (source, place) in enumerate(zip(sources, places))
    ]
    for copy in copies:
        copy.start()
    return copies


def turned_copies(turned, held, sems, first_step, last_step):
    def copy(step):
        start = pl.multiple_of(step * BLOCK, BLOCK)
        local = pl.multiple_of((step - first_step) * BLOCK, BLOCK)
        return pltpu.make_async_copy(
            turned.at[:, pl.ds(start, BLOCK)], held.at[:, pl.ds(local, BLOCK)], sems.at[step - first_step]
        )

    for step in range(first_step, last_step):
        copy(step).start()
    return copy


def plane_tile(held, step, part):
    return held[:, pl.ds(pl.multiple_of(step * BLOCK + part * TILE, TILE), TILE)]


def forward_kernel(
    received, poses_h, turned_h, first_h, hidden_h, feature_h, density_h,
    out, rows_h, points_h, feats_h, v1_h, v2_h, colors_h, dens_h,
    poses, turned, first_t, hidden_t, feature_t, density_w,
    rows_v, points_v, feats_v, v1_v, v2_v, colors_v, dens_v,
    factor, total, plane_sems, in_sems, out_sems,
):
    sources = received.shape[0] // 2
    slots = 2 * sources
    count = slots * S
    steps = turned.shape[1] // BLOCK
    arriving = fetch(
        (poses_h, first_h, hidden_h, feature_h, density_h),
        (poses, first_t, hidden_t, feature_t, density_w),
        in_sems,
    )
    plane_copy = turned_copies(turned_h, turned, plane_sems, 0, steps)
    arriving[0].wait()
    rows, _, pose = ray_rows(received, poses, sources)
    rows_v[...] = rows
    points = sample_rows(rows, pose)
    for axis, coordinate in enumerate(points):
        factor[axis * CELLS : (axis + 1) * CELLS, :] = factors(coordinate)[0]
        points_v[axis : axis + 1, :] = coordinate
    points_v[3:8, :] = jnp.zeros((5, count), F32)
    leaving = fetch((rows_v, points_v), (rows_h, points_h), out_sems)
    total[...] = jnp.zeros_like(total)

    @pl.loop(0, steps)
    def _(step):
        plane_copy(step).wait()
        row_base, col_base, _, _ = plane_axes(step)
        for lane in range(0, count, TILE):
            columns = factor[pl.ds(pl.multiple_of(col_base, CELLS), CELLS), lane : lane + TILE]
            acc = total[:, lane : lane + TILE]
            for part in range(BLOCK // TILE):
                tile = table_tile(factor, row_base, part, columns, lane)
                acc = acc + contract(plane_tile(turned, step, part), tile, 1, 0)
            total[:, lane : lane + TILE] = acc

    for copy in arriving[1:]:
        copy.wait()
    feats = total[...].astype(BF16)
    feats_v[...] = feats
    v1 = contract(first_t[...], feats, 1, 0)
    v1_v[...] = v1
    leaving += fetch((feats_v, v1_v), (feats_h, v1_h), out_sems, 2)
    h1 = (v1 * jax.nn.sigmoid(v1)).astype(BF16)
    v2 = contract(hidden_t[...], h1, 1, 0)
    v2_v[...] = v2
    leaving += fetch((v2_v,), (v2_h,), out_sems, 4)
    h2 = (v2 * jax.nn.sigmoid(v2)).astype(BF16)
    colors = jnp.tanh(contract(feature_t[...], h2, 1, 0))
    colors_v[...] = colors
    raw = contract(density_w[...].astype(BF16), h2, 1, 0)
    dens_v[...] = raw
    leaving += fetch((colors_v, dens_v), (colors_h, dens_h), out_sems, 5)
    depth = (jnp.maximum(raw, 0.0) + jnp.log1p(jnp.exp(-jnp.abs(raw)))) * STEP
    seg = jnp.zeros((LANES, slots), F32)
    front = jnp.zeros((1, slots), F32)
    for s in range(S):
        e = depth[:, s * slots : (s + 1) * slots]
        weight = jnp.exp(-front) * (1.0 - jnp.exp(-e))
        seg = seg + weight * colors[:, s * slots : (s + 1) * slots]
        front = front + e
    through = jnp.exp(-front)
    out[pl.ds(0, sources, stride=3), :] = seg[:, 0:sources].T
    out[pl.ds(1, sources, stride=3), :] = seg[:, sources:slots].T
    sub = iota((8, sources), 0)
    both = jnp.where(
        sub == 0, through[:, 0:sources], jnp.where(sub == 1, through[:, sources:slots], 0.0)
    )
    place = (iota((8, LANES), 0) == iota((8, LANES), 1)).astype(F32)
    out[pl.ds(2, sources, stride=3), :] = contract(both, place, 0, 0, EXACT)
    for copy in leaving:
        copy.wait()


IN_HBM = pl.BlockSpec(memory_space=pltpu.HBM)
IN_VMEM = pl.BlockSpec(memory_space=pltpu.VMEM)


def forward(received, poses, turned, first_t, hidden_t, feature_t, density_w):
    sources = received.shape[0] // 2
    slots = 2 * sources
    count = slots * S
    channels, cells = turned.shape
    hidden = first_t.shape[0]
    saved = [
        ((8, slots), F32),
        ((8, count), F32),
        ((channels, count), BF16),
        ((hidden, count), F32),
        ((hidden, count), F32),
        ((channels, count), F32),
        ((1, count), F32),
    ]
    params = [poses, turned, first_t, hidden_t, feature_t, density_w]
    return pl.pallas_call(
        forward_kernel,
        in_specs=[IN_VMEM] + [IN_HBM] * len(params),
        out_specs=[IN_VMEM] + [IN_HBM] * len(saved),
        out_shape=[jax.ShapeDtypeStruct((3 * sources, LANES), F32)]
        + [pltpu.HBM(shape, kind) for shape, kind in saved],
        scratch_shapes=[pltpu.VMEM(x.shape, x.dtype) for x in params]
        + [pltpu.VMEM(shape, kind) for shape, kind in saved]
        + [
            pltpu.VMEM((3 * CELLS, count), F32),
            pltpu.VMEM((channels, count), F32),
            pltpu.SemaphoreType.DMA((cells // BLOCK,)),
            pltpu.SemaphoreType.DMA((5,)),
            pltpu.SemaphoreType.DMA((7,)),
        ],
        compiler_params=grant(24),
        cost_estimate=price(2 * cells * count * channels, 8 * 2**20),
        name="forward",
    )(received, *map(far, params))


def slopes(points, turned, first_step, last_step):
    count = points.shape[1]
    channels = turned.shape[0]
    steps = last_step - first_step

    def slope_kernel(points, turned_h, out, held, factor, slope, total, sems):
        plane_copy = turned_copies(turned_h, held, sems, first_step, last_step)
        for axis in range(3):
            span = slice(axis * CELLS, (axis + 1) * CELLS)
            factor[span, :], slope[span, :] = factors(points[axis : axis + 1, :])
        total[...] = jnp.zeros_like(total)

        @pl.loop(first_step, last_step)
        def _(step):
            plane_copy(step).wait()
            row_base, col_base, first, second = plane_axes(step)
            for rows_ref, cols_ref, axis in ((slope, factor, first), (factor, slope, second)):
                base = pl.multiple_of(axis * LANES, LANES)
                for lane in range(0, count, TILE):
                    columns = cols_ref[
                        pl.ds(pl.multiple_of(col_base, CELLS), CELLS), lane : lane + TILE
                    ]
                    acc = total[pl.ds(base, LANES), lane : lane + TILE]
                    for part in range(BLOCK // TILE):
                        tile = table_tile(rows_ref, row_base, part, columns, lane)
                        acc = acc + contract(plane_tile(held, step - first_step, part), tile, 1, 0)
                    total[pl.ds(base, LANES), lane : lane + TILE] = acc

        out[...] = total[...].astype(BF16)

    return pl.pallas_call(
        slope_kernel,
        in_specs=[IN_VMEM, IN_HBM],
        out_shape=pltpu.HBM((3 * channels, count), BF16),
        scratch_shapes=[
            pltpu.VMEM((channels, steps * BLOCK), BF16),
            pltpu.VMEM((3 * CELLS, count), F32),
            pltpu.VMEM((3 * CELLS, count), F32),
            pltpu.VMEM((3 * channels, count), F32),
            pltpu.SemaphoreType.DMA((steps,)),
        ],
        compiler_params=grant(16),
        cost_estimate=price(4 * steps * BLOCK * count * channels, 6 * 2**20),
        name="slopes",
    )(far(points), far(turned))


def rays_kernel(home, route, ranks, targets, ray_out, back, grads):
    bricks = home.shape[0] // 3
    rays = targets.shape[0]
    slot = [route[0:bricks, :].T, route[bricks : 2 * bricks, :].T]
    seg = contract(slot[0], home[pl.ds(0, bricks, stride=3), :], 1, 0, EXACT) + contract(
        slot[1], home[pl.ds(1, bricks, stride=3), :], 1, 0, EXACT
    )
    lane = iota((1, LANES), 1)
    through = home[pl.ds(2, bricks, stride=3), :]
    passing = jnp.sum(
        contract(slot[0], jnp.where(lane == 0, through, 0.0), 1, 0, EXACT)
        + contract(slot[1], jnp.where(lane == 1, through, 0.0), 1, 0, EXACT),
        axis=1,
        keepdims=True,
    )
    feature = [seg[k * rays : (k + 1) * rays] for k in range(K)]
    pass_k = [passing[k * rays : (k + 1) * rays] for k in range(K)]
    rank_cols = contract(eye(rays), ranks[...].astype(F32), 1, 1, EXACT)
    rank = [rank_cols[:, k : k + 1] for k in range(K)]
    ones = jnp.ones((rays, 1), F32)

    def seen(k, skip=None):
        product = ones
        for other in range(K):
            if other != k and other != skip:
                product = product * jnp.where(rank[other] < rank[k], pass_k[other], 1.0)
        return product

    transmit = [seen(k) for k in range(K)]
    ray = jnp.zeros_like(feature[0])
    for k in range(K):
        ray = ray + transmit[k] * feature[k]
    ray_out[...] = ray
    grad = ray - targets[...]
    pull = [jnp.sum(grad * feature[k], axis=1, keepdims=True) for k in range(K)]
    for k in range(K):
        grads[k * rays : (k + 1) * rays, 0:LANES] = transmit[k] * grad
        pass_grad = jnp.zeros((rays, 1), F32)
        for behind in range(K):
            if behind != k:
                pass_grad = pass_grad + jnp.where(
                    rank[k] < rank[behind], pull[behind] * seen(behind, k), 0.0
                )
        grads[k * rays : (k + 1) * rays, LANES : 2 * LANES] = jnp.broadcast_to(
            pass_grad, (rays, LANES)
        )
    spread = None
    for c in range(2):
        both = contract(route[c * bricks : (c + 1) * bricks, :], grads[...], 1, 0, EXACT)
        back[pl.ds(c, bricks, stride=3), :] = both[:, 0:LANES]
        own = jnp.where(lane == c, both[:, LANES : 2 * LANES], 0.0)
        spread = own if spread is None else spread + own
    back[pl.ds(2, bricks, stride=3), :] = spread


def rays_step(home, route, ranks, targets):
    return pl.pallas_call(
        rays_kernel,
        out_shape=(
            pltpu.HBM(targets.shape, F32),
            jax.ShapeDtypeStruct(home.shape, F32),
        ),
        scratch_shapes=[pltpu.VMEM((route.shape[1], 2 * LANES), F32)],
        compiler_params=grant(4),
        name="rays",
    )(home, *map(far, (route, ranks, targets)))


def backward_kernel(
    cot, dens_h, colors_h, v2_h, feature_h, density_h, v1_h, hidden_h, feats_h, first_h, rows_h, slope_ah, slope_bh,
    pose_g, feature_gh, density_gh, hidden_gh, first_gh, feat_cot_h,
    dens_ref, colors_ref, v2_ref, feature_w, density_w, v1_ref, hidden_w, feats, first_w, rows_ref, slope_a, slope_b,
    feature_g, density_g, hidden_g, first_g, feat_cot,
    color_cot, in_sems, out_sems,
):
    arriving = fetch(
        (dens_h, colors_h, v2_h, feature_h, density_h, v1_h, hidden_h, feats_h, first_h, rows_h, slope_ah, slope_bh),
        (dens_ref, colors_ref, v2_ref, feature_w, density_w, v1_ref, hidden_w, feats, first_w, rows_ref, slope_a, slope_b),
        in_sems,
    )
    sources = cot.shape[0] // 3
    slots = 2 * sources
    seg_cot = jnp.concatenate(
        [cot[pl.ds(slot, sources, stride=3), :].T for slot in range(2)], axis=1
    )
    turned = cot[pl.ds(2, sources, stride=3), :].T
    pass_cot = jnp.concatenate([turned[0:1], turned[1:2]], axis=1)
    arriving[0].wait()
    arriving[1].wait()
    raw = dens_ref[...]
    depth = (jnp.maximum(raw, 0.0) + jnp.log1p(jnp.exp(-jnp.abs(raw)))) * STEP
    front = jnp.zeros((1, slots), F32)
    weights, kept, pulls = [], [], []
    for s in range(S):
        span = slice(s * slots, (s + 1) * slots)
        e = depth[:, span]
        reach = jnp.exp(-front)
        weight = reach * (1.0 - jnp.exp(-e))
        colors = colors_ref[:, span]
        pulls.append(jnp.sum(colors * seg_cot, axis=0, keepdims=True))
        color_cot[:, span] = (weight * seg_cot * (1.0 - colors * colors)).astype(BF16)
        weights.append(weight)
        kept.append(reach * jnp.exp(-e))
        front = front + e
    behind = pass_cot * jnp.exp(-front)
    depth_cot = [None] * S
    for s in reversed(range(S)):
        depth_cot[s] = pulls[s] * kept[s] - behind
        behind = behind + pulls[s] * weights[s]
    raw_cot = (jnp.concatenate(depth_cot, axis=1) * STEP * jax.nn.sigmoid(raw)).astype(BF16)

    for copy in arriving[2:5]:
        copy.wait()
    v2 = v2_ref[...]
    gate2 = jax.nn.sigmoid(v2)
    h2 = (v2 * gate2).astype(BF16)
    color_c = color_cot[...]
    feature_g[...] = contract(h2, color_c, 1, 1).astype(BF16).astype(F32)
    density_g[...] = contract(raw_cot, h2, 1, 1).astype(BF16).astype(F32)
    leaving = fetch((feature_g, density_g), (feature_gh, density_gh), out_sems)
    wide = jnp.where(iota((8, 1), 0) == 0, density_w[...].astype(F32), 0.0).astype(BF16)
    wide_cot = jnp.where(iota((8, 1), 0) == 0, raw_cot.astype(F32), 0.0).astype(BF16)
    h2_cot = (
        contract(feature_w[...], color_c, 1, 0) + contract(wide.T, wide_cot, 1, 0)
    ).astype(BF16).astype(F32)
    v2_cot = (h2_cot * gate2 * (1.0 + v2 * (1.0 - gate2))).astype(BF16)
    for copy in arriving[5:9]:
        copy.wait()
    v1 = v1_ref[...]
    gate1 = jax.nn.sigmoid(v1)
    h1 = (v1 * gate1).astype(BF16)
    hidden_g[...] = contract(h1, v2_cot, 1, 1).astype(BF16).astype(F32)
    leaving += fetch((hidden_g,), (hidden_gh,), out_sems, 2)
    h1_cot = contract(hidden_w[...], v2_cot, 1, 0).astype(BF16).astype(F32)
    v1_cot = (h1_cot * gate1 * (1.0 + v1 * (1.0 - gate1))).astype(BF16)
    first_g[...] = contract(feats[...], v1_cot, 1, 1).astype(BF16).astype(F32)
    f_cot = contract(first_w[...], v1_cot, 1, 0).astype(BF16).astype(F32)
    feat_cot[...] = f_cot.T.astype(BF16)
    leaving += fetch((first_g, feat_cot), (first_gh, feat_cot_h), out_sems, 3)
    for copy in arriving[9:]:
        copy.wait()

    pull = [
        jnp.sum(
            (
                slope_a[a * LANES : (a + 1) * LANES, :].astype(F32)
                + slope_b[a * LANES : (a + 1) * LANES, :].astype(F32)
            )
            * f_cot,
            axis=0,
            keepdims=True,
        )
        for a in range(3)
    ]
    rows = rows_ref[...]
    shift = [jnp.zeros((1, slots), F32)] * 3
    turn = [jnp.zeros((1, slots), F32)] * 3
    for s in range(S):
        distance = rows[6:7] + (s + 0.5) * STEP
        place = [rows[i : i + 1] + distance * rows[3 + i : 4 + i] for i in range(3)]
        part = [pull[a][:, s * slots : (s + 1) * slots] for a in range(3)]
        twist = cross(place, part)
        for a in range(3):
            shift[a] = shift[a] + part[a]
            turn[a] = turn[a] + twist[a]
    sub = iota((8, slots), 0)
    grads = jnp.zeros((8, slots), F32)
    for a in range(3):
        grads = jnp.where(sub == a, turn[a], grads)
        grads = jnp.where(sub == 3 + a, shift[a], grads)
    cams = pose_g.shape[1]
    picked = (iota((cams, slots), 0) == rows[7:8].astype(jnp.int32)).astype(F32)
    pose = contract(grads, picked, 1, 1, EXACT)
    for copy in range(pose_g.shape[0] // 8):
        pose_g[copy * 8 : (copy + 1) * 8, :] = pose
    for copy in leaving:
        copy.wait()


def backward(cot, saved, slope_a, slope_b, rows, weights, cams, copies):
    feats, v1, v2, colors, dens = saved
    first_w, hidden_w, feature_w, density_w = weights
    channels, count = feats.shape
    ins = [dens, colors, v2, feature_w, density_w, v1, hidden_w, feats, first_w, rows, slope_a, slope_b]
    outs = [(w.shape, F32) for w in (feature_w, density_w, hidden_w, first_w)] + [((count, channels), BF16)]
    return pl.pallas_call(
        backward_kernel,
        in_specs=[IN_VMEM] + [IN_HBM] * len(ins),
        out_specs=[IN_VMEM] + [IN_HBM] * len(outs),
        out_shape=[jax.ShapeDtypeStruct((8 * copies, cams), F32)]
        + [pltpu.HBM(shape, kind) for shape, kind in outs],
        scratch_shapes=[pltpu.VMEM(x.shape, x.dtype) for x in ins]
        + [pltpu.VMEM(shape, kind) for shape, kind in outs]
        + [
            pltpu.VMEM((channels, count), BF16),
            pltpu.SemaphoreType.DMA((len(ins),)),
            pltpu.SemaphoreType.DMA((len(outs),)),
        ],
        compiler_params=grant(24),
        name="backward",
    )(cot, *map(far, ins))


def plane_grads(points, cot, cells, first_step, last_step, begun=None):
    count = points.shape[1]
    channels = cot.shape[1]

    def plane_kernel(points, cot, *rest):
        out, factor = rest[-2:]

        @pl.when(pl.program_id(0) == 0)
        def _():
            for axis in range(3):
                factor[axis * CELLS : (axis + 1) * CELLS, :] = factors(points[axis : axis + 1, :])[0]

        row_base, col_base, _, _ = plane_axes(pl.program_id(0) + first_step)
        for part in range(BLOCK // TILE):
            acc = jnp.zeros((TILE, channels), F32)
            for lane in range(0, count, TILE):
                columns = factor[pl.ds(pl.multiple_of(col_base, CELLS), CELLS), lane : lane + TILE]
                tile = table_tile(factor, row_base, part, columns, lane)
                acc = acc + contract(tile, cot[lane : lane + TILE, :], 1, 0)
            out[part * TILE : (part + 1) * TILE, :] = acc

    steps = last_step - first_step
    earlier = [] if begun is None else [begun]
    return pl.pallas_call(
        plane_kernel,
        grid=(steps,),
        in_specs=[whole(points.shape), whole(cot.shape)] + [IN_HBM] * len(earlier),
        out_specs=pl.BlockSpec((BLOCK, channels), lambda step: (step + first_step, 0)),
        out_shape=pltpu.HBM((cells, channels), F32),
        scratch_shapes=[pltpu.VMEM((3 * CELLS, count), F32)],
        input_output_aliases={2: 0} if earlier else {},
        compiler_params=grant(8),
        cost_estimate=price(2 * steps * BLOCK * count * channels, steps * BLOCK * channels * 4),
        name="plane_grads",
    )(far(points), far(cot), *map(far, earlier))


def exchange(rows, peers):
    wide = rows.reshape(peers, 1, rows.size // peers)
    moved = lax.all_to_all(wide, AXES, split_axis=0, concat_axis=0, tiled=True)
    return moved.reshape(rows.shape)


def swap(copies, axis):
    stacked = copies.reshape(lax.axis_size(axis), 8, copies.shape[1])
    moved = lax.all_to_all(stacked, (axis,), split_axis=0, concat_axis=0, tiled=True)
    return moved.reshape(copies.shape)


def add_kernel(parts, out):
    total = parts[0:8, :]
    for source in range(1, parts.shape[0] // 8):
        total = total + parts[source * 8 : (source + 1) * 8, :]
    rows = min(8, out.shape[0])
    for copy in range(out.shape[0] // rows):
        out[copy * rows : (copy + 1) * rows, :] = total[0:rows]


def add(parts, out_shape):
    return pl.pallas_call(
        add_kernel, out_shape=out_shape, compiler_params=grant(2), name="add"
    )(parts)


def per_device(
    anchors, directions, ray_start, camera_ids, brick_ids, brick_rank, targets,
    planes, first_weight, hidden_weight, feature_weight, density_weight, poses,
):
    bricks = lax.axis_size(AXES)
    cells = planes.shape[1]
    steps = cells // BLOCK
    cams = poses.shape[1]
    ids, ranks = brick_ids.T, brick_rank.T
    outgoing = dispatch(anchors, directions, ray_start[None], camera_ids[None], ids, ranks, bricks)
    received = exchange(outgoing, bricks)
    turned, first_o, first_t, hidden_o, hidden_t, feature_o, feature_t, route = prepare(
        planes[0], first_weight[0], hidden_weight[0, 0], feature_weight[0], ids, bricks
    )
    sent, rows, points, *saved = forward(
        received, poses, turned, first_t, hidden_t, feature_t, density_weight
    )
    home = exchange(sent, bricks)
    slope_a = slopes(points, turned, 0, steps // 2)
    ray_feature, back = rays_step(home, route, ranks, targets)
    cot = exchange(back, bricks)
    later_points, back = lax.optimization_barrier((points, back))
    slope_b = slopes(later_points, turned, steps // 2, steps)
    pose_part, feature_g, density_g, hidden_g, first_g, feat_cot = backward(
        cot, saved, slope_a, slope_b, rows, (first_o, hidden_o, feature_o, density_weight), cams, lax.axis_size("gy")
    )
    column_parts = swap(pose_part, "gy")
    plane_grad = plane_grads(points, feat_cot, cells, 0, steps // 2)
    column_sum = add(column_parts, jax.ShapeDtypeStruct((8 * lax.axis_size("gx"), cams), F32))
    later_cot, column_sum = lax.optimization_barrier((feat_cot, column_sum))
    pose_grad = add(swap(column_sum, "gx"), pltpu.HBM(poses.shape, F32))
    plane_grad = plane_grads(points, later_cot, cells, steps // 2, steps, plane_grad)
    return (
        ray_feature,
        plane_grad[None],
        first_g[None],
        hidden_g[None, None],
        feature_g[None],
        density_g,
        pose_grad,
    )


def solution(mesh):
    rays = P(AXES)
    in_specs = (
        P(None, AXES), P(None, AXES), rays, rays, P(AXES, None), P(AXES, None), P(AXES, None),
        P(AXES, None, None), P(AXES, None, None), P(AXES, None, None, None), P(AXES, None, None),
        P(AXES, None), P(),
    )
    out_specs = (
        P(AXES, None), P(AXES, None, None), P(AXES, None, None), P(AXES, None, None, None),
        P(AXES, None, None), P(AXES, None), P(),
    )
    return jax.shard_map(
        per_device, mesh=mesh, in_specs=in_specs, out_specs=out_specs, check_vma=False
    )
```

time: 127 us -> 102 us (0.80)
  blocking collectives: 45.6 us -> 0 us
  local copies, waits for them, and re-layouts: 30.9 us -> 0 us
  starting transfers between devices: 12 us -> 34 us
  Pallas kernels: 36.2 us -> 56.8 us
  waiting for transfers between devices: 0.01 us -> 9.65 us
    all_to_all x3 -> x0, blocking collectives: 45.6 us -> none  [the longest x2 36 us: exchange(): moved = lax.all_to_all(wide, AXES, split_axis=0, concat_axis=0, tiled=True)]
    unnamed x51 -> x0, local copies, waits for them, and re-layouts: 27.2 us -> none
    pallas_call x6 -> x11, Pallas kernels: 36.2 us -> 56.8 us  [the longest x2 15.1 us: slopes(): pl.pallas_call(slope_kernel, in_specs=[IN_VMEM, IN_HBM], out_shape=pltpu....]
    all_to_all x1 -> x3, starting transfers between devices: 4.94 us -> 25.1 us  [exchange(): moved = lax.all_to_all(wide, AXES, split_axis=0, concat_axis=0, tiled=True)]
    all_to_all x1 -> x3, waiting for transfers between devices: 0.01 us -> 8.87 us  [exchange(): moved = lax.all_to_all(wide, AXES, split_axis=0, concat_axis=0, tiled=True)]
    reshape x3 -> x0, local copies, waits for them, and re-layouts: 3.04 us -> none  [exchange(): wide = rows.reshape(rows.shape[0], 1, rows.shape[1])]
    all_to_all x1 -> x2, starting transfers between devices: 7.04 us -> 8.92 us  [swap(): lax.all_to_all(stacked, (axis,), split_axis=0, concat_axis=0, tiled=True)]
  transfers between devices with their start and end apart: 2 -> 5, of which waited for: 0 -> 4; matrix products, arithmetic and copies ran while one was open for 0% -> 0% of each run, Pallas kernels for 16% -> 34%
where the time goes in v2:
time: 102 us; the launch traced here: 101 us
  Pallas kernels  56.8 us (56%)
  starting transfers between devices  34 us (33%)
  waiting for transfers between devices  9.65 us (9%)
    all_to_all x3, starting transfers between devices, exchange(): moved = lax.all_to_all(wide, AXES, split_axis=0, concat_axis=0, tiled=True)  25.1 us
    pallas_call x2, Pallas kernels, slopes(): pl.pallas_call(slope_kernel, in_specs=[IN_VMEM, IN_HBM], out_shape=pltpu....  15.1 us
    pallas_call x2, Pallas kernels, plane_grads(): pl.pallas_call(plane_kernel, grid=(steps,), in_specs=[whole(points.shape)...  12.7 us
    pallas_call x1, Pallas kernels, forward(): pl.pallas_call(forward_kernel, in_specs=[IN_VMEM] + [IN_HBM] * len(params...  10.8 us
    all_to_all x2, starting transfers between devices, swap(): lax.all_to_all(stacked, (axis,), split_axis=0, concat_axis=0, tiled=True)  8.92 us
    all_to_all x3, waiting for transfers between devices, exchange(): moved = lax.all_to_all(wide, AXES, split_axis=0, concat_axis=0, tiled=True)  8.87 us
    pallas_call x1, Pallas kernels, prepare(): pl.pallas_call(prepare_kernel, grid=(cells // (2 * BLOCK),), in_specs=in_...  7.03 us
    pallas_call x1, Pallas kernels, backward(): pl.pallas_call(backward_kernel, in_specs=[IN_VMEM] + [IN_HBM] * len(ins),...  4.92 us
  transfers between devices with their start and end apart: 5, of which 4 were waited for; matrix products, arithmetic and copies ran while one was open for 0% of the time, Pallas kernels for 34%

profile of v2, /device:TPU:1, one launch (start us, length us, event | category | flops | bytes accessed | tf_op | source)
XLA Modules:
  0.0 101.2 jit_solution(2494136256178407650)
XLA Ops:
  0.6 2.0 %dispatch.1 = f32[256,128]{1,0:T(8,128)} custom-call(f32[3,32]{1,0:T(4,128)} %anchors.1, f32[3,32]{1,0:T(4,128)} %directions.1, f32[1,32]{1,0:T(1,128)} %bitcast.36, s32[1,32]{1,0:T(1,128)} %bitcast.37, s32[4,32]{1,0:T(4,128)} %bitcast.32, s32[4,32]{1,0:T(4,128)} %bitcast.34), custom_call_target="tpu_custom_call" | custom-call | tf_op jit(solution)/shard_map/dispatch/pallas_call | solution.py:85
  2.6 11.5 %all-to-all-start = ((f32[128,1,256]{2,1,0:T(1,128)}), f32[128,1,256]{2,1,0:T(1,128)S(1)}, u32[]{:S(2)}, u32[]{:S(2)}) async-start(f32[128,1,256]{2,1,0:T(1,128)} %bitcast.4), calls=%async_computation | async-start | bytes 262144 | tf_op jit(solution)/shard_map/all_to_all | solution.py:654
  14.1 7.0 %prepare.1 = (bf16[128,12288]{1,0:T(8,128)(2,1)}, bf16[128,256]{1,0:T(8,128)(2,1)}, bf16[256,128]{1,0:T(8,128)(2,1)}, bf16[256,256]{1,0:T(8,128)(2,1)}, bf16[256...) custom-call(f32[12288,128]{1,0:T(8,128)} %bitcast.28, ...), custom_call_target="tpu_custom_call" | custom-call | bytes 10485760 | tf_op jit(solution)/shard_map/prepare/pallas_call | solution.py:207
  21.1 3.0 %all-to-all-done = f32[128,1,256]{2,1,0:T(1,128)S(1)} async-done(((f32[128,1,256]{2,1,0:T(1,128)}), f32[128,1,256]{2,1,0:T(1,128)S(1)}, u32[]{:S(2)}, u32[]{:S(2)}) %all-to-all-start) | async-done | bytes 131104 | tf_op jit(solution)/shard_map/all_to_all | solution.py:654
  24.1 10.8 %forward.1 = (f32[384,128]{1,0:T(8,128)}, f32[8,256]{1,0:T(8,128)}, f32[8,1024]{1,0:T(8,128)}, bf16[128,1024]{1,0:T(8,128)(2,1)}, f32[256,1024]{1,0:T(8,128)}, /...) custom-call(f32[256,128]{1,0:T(8,128)S(1)} %bitcast.26, f32[6,256]{1,0:T(8,128)} %poses_h.1, ...), custom_call_target="tpu_custom_call" | custom-call | flops 3221225472 | bytes 8388608 | tf_op jit(solution)/shard_map/forward/pallas_call | solution.py:344
  34.9 6.8 %all-to-all-start.1 = ((f32[128,1,384]{2,1,0:T(1,128)}), f32[128,1,384]{2,1,0:T(1,128)S(1)}, u32[]{:S(2)}, u32[]{:S(2)}) async-start(f32[128,1,384]{2,1,0:T(1,128)} %bitcast.10), calls=%async_computation.1 | async-start | bytes 393216 | tf_op jit(solution)/shard_map/all_to_all | solution.py:654
  41.8 7.6 %slopes.2.slope_ah = bf16[384,1024]{1,0:T(8,128)(2,1)} custom-call(f32[8,1024]{1,0:T(8,128)} %get-tuple-element.52.points, bf16[128,12288]{1,0:T(8,128)(2,1)} %get-tuple-element.34.turned_h), custom_call_target="tpu_custom_call" | custom-call | flops 3221225472 | bytes 6291456 | tf_op jit(solution)/shard_map/slopes/pallas_call | solution.py:395
  49.3 2.9 %all-to-all-done.1 = f32[128,1,384]{2,1,0:T(1,128)S(1)} async-done(((f32[128,1,384]{2,1,0:T(1,128)}), f32[128,1,384]{2,1,0:T(1,128)S(1)}, u32[]{:S(2)}, u32[]{:S(2)}) %all-to-all-start.1) | async-done | bytes 196640 | tf_op jit(solution)/shard_map/all_to_all | solution.py:654
  52.3 2.9 %rays.1 = (f32[32,128]{1,0:T(8,128)}, f32[384,128]{1,0:T(8,128)}) custom-call(f32[384,128]{1,0:T(8,128)S(1)} %bitcast.23, f32[256,128]{1,0:T(8,128)} %get-tuple-element.39.route, s32[4,32]{1,0:T(4,128)} %bitcast.35, f32[32,128]{1,0:T(8,128)} %targets.1), custom_call_target="tpu_custom_call" | custom-call | tf_op jit(solution)/shard_map/rays/pallas_call | solution.py:468
  55.2 6.8 %all-to-all-start.2 = ((f32[128,1,384]{2,1,0:T(1,128)}), f32[128,1,384]{2,1,0:T(1,128)S(1)}, u32[]{:S(2)}, u32[]{:S(2)}) async-start(f32[128,1,384]{2,1,0:T(1,128)} %bitcast.12), calls=%async_computation.2 | async-start | bytes 393216 | tf_op jit(solution)/shard_map/all_to_all | solution.py:654
  62.0 7.6 %slopes.3.slope_bh = bf16[384,1024]{1,0:T(8,128)(2,1)} custom-call(f32[8,1024]{1,0:T(8,128)} %get-tuple-element.52.points, bf16[128,12288]{1,0:T(8,128)(2,1)} %get-tuple-element.34.turned_h), custom_call_target="tpu_custom_call" | custom-call | flops 3221225472 | bytes 6291456 | tf_op jit(solution)/shard_map/slopes/pallas_call | solution.py:395
  69.6 2.9 %all-to-all-done.2 = f32[128,1,384]{2,1,0:T(1,128)S(1)} async-done(((f32[128,1,384]{2,1,0:T(1,128)}), f32[128,1,384]{2,1,0:T(1,128)S(1)}, u32[]{:S(2)}, u32[]{:S(2)}) %all-to-all-start.2) | async-done | bytes 196640 | tf_op jit(solution)/shard_map/all_to_all | solution.py:654
  72.6 4.9 %backward.1 = (f32[64,256]{1,0:T(8,128)}, f32[256,128]{1,0:T(8,128)}, f32[1,256]{1,0:T(1,128)}, f32[256,256]{1,0:T(8,128)}, f32[128,256]{1,0:T(8,128)}, /*index=5*/bf16[1024,128]{1,0:T(8,128)(2,1)}) custom-call(f32[384,128]{1,0:T(8,128)S(1)} %bitcast.22, f32[1,1024]{1,0:T(1,128)} %get-tuple-element.43.dens_h, f32[128,1024]{1,0:T(8,128)} %get-tuple-element.44.colors_h, ...), custom_call_target="tpu_custom_call" | custom-call | tf_op jit(solution)/shard_map/backward/pallas_call | solution.py:597
  77.5 3.8 %all-to-all-start.3 = ((f32[8,8,256]{2,1,0:T(8,128)}), f32[8,8,256]{2,1,0:T(8,128)S(1)}, u32[]{:S(2)}, u32[]{:S(2)}) async-start(f32[8,8,256]{2,1,0:T(8,128)} %bitcast.14), calls=%async_computation.3 | async-start | bytes 131072 | tf_op jit(solution)/shard_map/all_to_all | solution.py:660
  81.3 6.3 %plane_grads.2.rest_0_ = f32[12288,128]{1,0:T(8,128)} custom-call(f32[8,1024]{1,0:T(8,128)} %get-tuple-element.52.points, bf16[1024,128]{1,0:T(8,128)(2,1)} %get-tuple-element.55.cot), custom_call_target="tpu_custom_call" | custom-call | flops 1610612736 | bytes 3145728 | tf_op jit(solution)/shard_map/plane_grads/pallas_call | solution.py:638
  87.6 0.0 all-to-all-done.3
  87.6 0.7 add.2
  88.3 5.1 %all-to-all-start.4 = ((f32[16,8,256]{2,1,0:T(8,128)}), f32[16,8,256]{2,1,0:T(8,128)S(1)}, u32[]{:S(2)}, u32[]{:S(2)}) async-start(f32[16,8,256]{2,1,0:T(8,128)} %bitcast.20), calls=%async_computation.4 | async-start | bytes 262144 | tf_op jit(solution)/shard_map/all_to_all | solution.py:660
  93.4 6.4 %plane_grads.3 = f32[12288,128]{1,0:T(8,128)} custom-call(f32[8,1024]{1,0:T(8,128)} %get-tuple-element.52.points, bf16[1024,128]{1,0:T(8,128)(2,1)} %get-tuple-element.55.cot, f32[12288,128]{1,0:T(8,128)} %plane_grads.2.rest_0_), custom_call_target="tpu_custom_call", output_to_operand_aliasing={{}: (2, {})} | custom-call | flops 1610612736 | bytes 3145728 | tf_op jit(solution)/shard_map/plane_grads/pallas_call | solution.py:638
  99.8 0.8 all-to-all-done.4
  100.5 0.6 add.3
Async XLA Ops:
  2.6 21.5 %all-to-all-start = ((f32[128,1,256]{2,1,0:T(1,128)}), f32[128,1,256]{2,1,0:T(1,128)S(1)}, u32[]{:S(2)}, u32[]{:S(2)}) async-start(f32[128,1,256]{2,1,0:T(1,128)} %bitcast.4), calls=%async_computation | async-start | bytes 262144 | tf_op jit(solution)/shard_map/all_to_all | solution.py:654
  34.9 17.3 %all-to-all-start.1 = ((f32[128,1,384]{2,1,0:T(1,128)}), f32[128,1,384]{2,1,0:T(1,128)S(1)}, u32[]{:S(2)}, u32[]{:S(2)}) async-start(f32[128,1,384]{2,1,0:T(1,128)} %bitcast.10), calls=%async_computation.1 | async-start | bytes 393216 | tf_op jit(solution)/shard_map/all_to_all | solution.py:654
  55.2 17.4 %all-to-all-start.2 = ((f32[128,1,384]{2,1,0:T(1,128)}), f32[128,1,384]{2,1,0:T(1,128)S(1)}, u32[]{:S(2)}, u32[]{:S(2)}) async-start(f32[128,1,384]{2,1,0:T(1,128)} %bitcast.12), calls=%async_computation.2 | async-start | bytes 393216 | tf_op jit(solution)/shard_map/all_to_all | solution.py:654
  77.5 10.1 %all-to-all-start.3 = ((f32[8,8,256]{2,1,0:T(8,128)}), f32[8,8,256]{2,1,0:T(8,128)S(1)}, u32[]{:S(2)}, u32[]{:S(2)}) async-start(f32[8,8,256]{2,1,0:T(8,128)} %bitcast.14), calls=%async_computation.3 | async-start | bytes 131072 | tf_op jit(solution)/shard_map/all_to_all | solution.py:660
  88.3 12.2 %all-to-all-start.4 = ((f32[16,8,256]{2,1,0:T(8,128)}), f32[16,8,256]{2,1,0:T(8,128)S(1)}, u32[]{:S(2)}, u32[]{:S(2)}) async-start(f32[16,8,256]{2,1,0:T(8,128)} %bitcast.20), calls=%async_computation.4 | async-start | bytes 262144 | tf_op jit(solution)/shard_map/all_to_all | solution.py:660

commit v3 on v2

v3 whole, which is shorter than its diff:
```python
import jax
import jax.numpy as jnp
from jax import lax
from jax.experimental import pallas as pl
from jax.experimental.pallas import tpu as pltpu
from jax.sharding import PartitionSpec as P

K = 4
S = 4
CELLS = 64
LANES = 128
STEP = 0.125
AXES = ("gx", "gy")
F32 = jnp.float32
BF16 = jnp.bfloat16
EXACT = lax.Precision.HIGHEST


def contract(left, right, left_dim, right_dim, precision=None):
    return lax.dot_general(
        left,
        right,
        (((left_dim,), (right_dim,)), ((), ())),
        precision=precision,
        preferred_element_type=F32,
    )


def iota(shape, dim):
    return lax.broadcasted_iota(jnp.int32, shape, dim)


def grant(mebibytes):
    return pltpu.CompilerParams(vmem_limit_bytes=mebibytes * 2**20)


def far(x):
    return pltpu.with_memory_space_constraint(x, pltpu.HBM)


def price(flops, moved):
    return pl.CostEstimate(flops=flops, bytes_accessed=moved, transcendentals=0)


def select_rows(onehot, values, left_dim, right_dim, parts=3):
    picked = onehot.astype(BF16)
    total = None
    rest = values
    for _ in range(parts):
        part = rest.astype(BF16)
        rest = rest - part.astype(F32)
        term = contract(picked, part, left_dim, right_dim)
        total = term if total is None else total + term
    return total


def eye(size):
    return (iota((size, size), 0) == iota((size, size), 1)).astype(F32)


def spread_of(rays):
    segs = rays * K
    spread = (iota((rays, segs), 0) == iota((rays, segs), 1) % rays).astype(F32)
    own = iota((K, segs), 0) == iota((K, segs), 1) // rays
    return spread, own


def segment_row(table, spread, own):
    four = contract(table[...].astype(F32).astype(BF16), spread.astype(BF16), 1, 0)
    return jnp.sum(jnp.where(own, four, 0.0), axis=0, keepdims=True)


def route_of(id_row, bricks):
    segs = id_row.shape[1]
    onehot = (iota((bricks, segs), 0) == id_row.astype(jnp.int32)).astype(F32)
    earlier = (iota((segs, segs), 0) < iota((segs, segs), 1)).astype(F32)
    before = contract(onehot.astype(BF16), earlier.astype(BF16), 1, 0)
    return [jnp.where((before > 0.5) == (slot == 1), onehot, 0.0) for slot in range(2)]


def cross(a, b):
    return (
        a[1] * b[2] - a[2] * b[1],
        a[2] * b[0] - a[0] * b[2],
        a[0] * b[1] - a[1] * b[0],
    )


def dispatch_kernel(anchors, directions, start, cameras, ids, ranks, poses, out, packed):
    bricks = out.shape[0] // 2
    rays = anchors.shape[1]
    spread, own = spread_of(rays)
    id_row = segment_row(ids, spread, own)
    picked = (iota((poses.shape[1], rays), 0) == cameras[...]).astype(F32)
    pose = contract(poses[...], picked, 1, 0, EXACT)
    turn = [pose[i : i + 1] for i in range(3)]
    anchor = [anchors[i : i + 1, :] for i in range(3)]
    direction = [directions[i : i + 1, :] for i in range(3)]
    turned = cross(turn, anchor)
    bent = cross(turn, direction)
    for i in range(3):
        packed[i : i + 1, :] = anchor[i] + turned[i] + pose[3 + i : 4 + i]
        packed[3 + i : 4 + i, :] = direction[i] + bent[i]
    packed[6:9, :] = anchors[...]
    packed[9:12, :] = directions[...]
    packed[12:13, :] = start[...]
    packed[13:14, :] = cameras[...].astype(F32)
    packed[14:16, :] = jnp.zeros((2, rays), F32)
    rank_row = segment_row(ranks, spread, own)
    values = contract(packed[...], spread, 1, 0, EXACT)
    values = values + jnp.where(iota((16, 1), 0) == 12, rank_row * (S * STEP), 0.0)
    for slot, taken in enumerate(route_of(id_row, bricks)):
        rows = select_rows(taken, values, 1, 1)
        both = jnp.concatenate([rows, jnp.zeros((bricks, LANES - 16), F32)], axis=1)
        out[pl.ds(slot, bricks, stride=2), :] = both


def dispatch(anchors, directions, start, cameras, ids, ranks, poses, bricks):
    return pl.pallas_call(
        dispatch_kernel,
        out_shape=jax.ShapeDtypeStruct((2 * bricks, LANES), F32),
        scratch_shapes=[pltpu.VMEM((16, anchors.shape[1]), F32)],
        compiler_params=grant(2),
        name="dispatch",
    )(*map(far, (anchors, directions, start, cameras, ids, ranks, poses)))


def ray_rows(received, sources):
    same = eye(sources)
    return jnp.concatenate(
        [
            contract(received[pl.ds(slot, sources, stride=2), :], same, 0, 0, EXACT)[0:16]
            for slot in range(2)
        ],
        axis=1,
    )


def sample_rows(rows):
    distance = [rows[12:13] + (s + 0.5) * STEP for s in range(S)]
    return [
        jnp.concatenate(
            [rows[i : i + 1] + distance[s] * rows[3 + i : 4 + i] for s in range(S)], axis=1
        )
        for i in range(3)
    ]


def factors(coordinate):
    count = coordinate.shape[1]
    scaled = coordinate * CELLS
    floor_c = jnp.floor(scaled)
    fraction = scaled - floor_c
    weight = fraction * fraction * (3.0 - 2.0 * fraction)
    slope = (6.0 * CELLS) * fraction * (1.0 - fraction)
    low = lax.bitwise_and(floor_c.astype(jnp.int32), CELLS - 1)
    high = lax.bitwise_and(low + 1, CELLS - 1)
    cell = iota((CELLS, count), 0)
    at_low = cell == low
    at_high = cell == high
    value = jnp.where(at_low, 1.0 - weight, 0.0) + jnp.where(at_high, weight, 0.0)
    change = jnp.where(at_high, slope, 0.0) - jnp.where(at_low, slope, 0.0)
    return value, change


BLOCK = 1024
TILE = 256


def plane_axes(step):
    plane = step // (CELLS * CELLS // BLOCK)
    first = plane // 2
    second = jnp.minimum(plane + 1, 2)
    start = (step % (CELLS * CELLS // BLOCK)) * (BLOCK // CELLS)
    return first * CELLS + start, second * CELLS, first, second


def table_tile(rows_ref, row_base, part, columns, lane):
    pieces = []
    for i in range(TILE // CELLS):
        row = rows_ref[pl.ds(row_base + part * (TILE // CELLS) + i, 1), lane : lane + TILE]
        pieces.append((row * columns).astype(BF16))
    return jnp.concatenate(pieces, axis=0)


IN_HBM = pl.BlockSpec(memory_space=pltpu.HBM)
IN_VMEM = pl.BlockSpec(memory_space=pltpu.VMEM)


def shapes(*arrays):
    return [jax.ShapeDtypeStruct(x.shape, x.dtype) for x in arrays]


def fetch(sources, places, sems, first=0):
    copies = [
        pltpu.make_async_copy(source, place, sems.at[first + i])
        for i, (source, place) in enumerate(zip(sources, places))
    ]
    for copy in copies:
        copy.start()
    return copies


def plane_copies(planes, held, sems, first_step, last_step):
    def copy(step):
        start = pl.multiple_of(step * BLOCK, BLOCK)
        local = pl.multiple_of((step - first_step) * BLOCK, BLOCK)
        return pltpu.make_async_copy(
            planes.at[pl.ds(start, BLOCK), :], held.at[pl.ds(local, BLOCK), :], sems.at[step - first_step]
        )

    for step in range(first_step, last_step):
        copy(step).start()
    return copy


def prepare_kernel(
    planes, first_h, hidden_h, feature_h, density_h, ids_h,
    turned, first_t, hidden_t, feature_t, density_w, first_oh, hidden_oh, feature_oh, route_h,
    held, first_w, hidden_w, feature_w, ids, first_o, hidden_o, feature_o, route, plane_sems, in_sems, out_sems,
):
    steps = planes.shape[0] // BLOCK
    arriving = fetch(
        (ids_h, first_h, hidden_h, feature_h, density_h), (ids, first_w, hidden_w, feature_w, density_w), in_sems
    )
    plane_copy = plane_copies(planes, held, plane_sems, 0, steps)
    for copy in arriving:
        copy.wait()
    for source, plain, flipped in (
        (first_w, first_o, first_t),
        (hidden_w, hidden_o, hidden_t),
        (feature_w, feature_o, feature_t),
    ):
        plain[...] = source[...].astype(BF16)
        flipped[...] = source[...].T.astype(BF16)
    bricks = route.shape[0] // 4
    spread, own = spread_of(ids.shape[1])
    for slot, taken in enumerate(route_of(segment_row(ids, spread, own), bricks)):
        route[slot * bricks : (slot + 1) * bricks, :] = taken.astype(BF16)
        route[(2 + slot) * bricks : (3 + slot) * bricks, :] = taken.T.astype(BF16)
    leaving = fetch((first_o, hidden_o, feature_o, route), (first_oh, hidden_oh, feature_oh, route_h), out_sems)

    @pl.loop(0, steps)
    def _(step):
        plane_copy(step).wait()
        span = pl.ds(pl.multiple_of(step * BLOCK, BLOCK), BLOCK)
        turned[:, span] = held[span, :].T.astype(BF16)

    for copy in leaving:
        copy.wait()


def prepare(planes, first_w, hidden_w, feature_w, density_w, ids, bricks):
    cells, channels = planes.shape
    flips = [jax.ShapeDtypeStruct(w.shape[::-1], BF16) for w in (first_w, hidden_w, feature_w)]
    plains = [pltpu.HBM(w.shape, BF16) for w in (first_w, hidden_w, feature_w)]
    return pl.pallas_call(
        prepare_kernel,
        in_specs=[IN_HBM] * 6,
        out_specs=[IN_VMEM] * 5 + [IN_HBM] * 4,
        out_shape=[jax.ShapeDtypeStruct((channels, cells), BF16)]
        + flips
        + shapes(density_w)
        + plains
        + [pltpu.HBM((4 * bricks, ids.shape[1] * K), BF16)],
        scratch_shapes=[pltpu.VMEM((cells, channels), F32)]
        + [pltpu.VMEM(x.shape, x.dtype) for x in (first_w, hidden_w, feature_w, ids)]
        + [pltpu.VMEM(w.shape, BF16) for w in (first_w, hidden_w, feature_w)]
        + [
            pltpu.VMEM((4 * bricks, ids.shape[1] * K), BF16),
            pltpu.SemaphoreType.DMA((cells // BLOCK,)),
            pltpu.SemaphoreType.DMA((5,)),
            pltpu.SemaphoreType.DMA((4,)),
        ],
        compiler_params=grant(16),
        cost_estimate=price(0, 10 * 2**20),
        name="prepare",
    )(*map(far, (planes, first_w, hidden_w, feature_w, density_w, ids)))


def forward_kernel(
    received, turned, first_t, hidden_t, feature_t, density_w,
    out_h, rows_h, points_h, feats_h, v1_h, v2_h, colors_h,
    out, rows_v, points_v, feats_v, v1_v, v2_v, colors_v,
    factor, total, out_sems,
):
    sources = received.shape[0] // 2
    slots = 2 * sources
    count = slots * S
    steps = turned.shape[1] // BLOCK
    rows = ray_rows(received, sources)
    rows_v[...] = rows
    points = sample_rows(rows)
    for axis, coordinate in enumerate(points):
        factor[axis * CELLS : (axis + 1) * CELLS, :] = factors(coordinate)[0]
        points_v[axis : axis + 1, :] = coordinate
    points_v[3:8, :] = jnp.zeros((5, count), F32)
    leaving = fetch((rows_v, points_v), (rows_h, points_h), out_sems)
    total[...] = jnp.zeros_like(total)

    @pl.loop(0, steps, unroll=4)
    def _(step):
        row_base, col_base, _, _ = plane_axes(step)
        for lane in range(0, count, TILE):
            columns = factor[pl.ds(pl.multiple_of(col_base, CELLS), CELLS), lane : lane + TILE]
            acc = total[:, lane : lane + TILE]
            for part in range(BLOCK // TILE):
                tile = table_tile(factor, row_base, part, columns, lane)
                acc = acc + contract(plane_tile(turned, step, part), tile, 1, 0)
            total[:, lane : lane + TILE] = acc

    feats = total[...].astype(BF16)
    feats_v[...] = feats
    v1 = contract(first_t[...], feats, 1, 0)
    v1_v[...] = v1
    leaving += fetch((feats_v, v1_v), (feats_h, v1_h), out_sems, 2)
    h1 = (v1 * jax.nn.sigmoid(v1)).astype(BF16)
    v2 = contract(hidden_t[...], h1, 1, 0)
    v2_v[...] = v2
    leaving += fetch((v2_v,), (v2_h,), out_sems, 4)
    h2 = (v2 * jax.nn.sigmoid(v2)).astype(BF16)
    colors = jnp.tanh(contract(feature_t[...], h2, 1, 0))
    colors_v[0:LANES, :] = colors
    raw = contract(density_w[...].astype(BF16), h2, 1, 0)
    colors_v[LANES : LANES + 8, :] = jnp.broadcast_to(raw, (8, count))
    leaving += fetch((colors_v,), (colors_h,), out_sems, 5)
    depth = (jnp.maximum(raw, 0.0) + jnp.log1p(jnp.exp(-jnp.abs(raw)))) * STEP
    seg = jnp.zeros((LANES, slots), F32)
    front = jnp.zeros((1, slots), F32)
    for s in range(S):
        e = depth[:, s * slots : (s + 1) * slots]
        weight = jnp.exp(-front) * (1.0 - jnp.exp(-e))
        seg = seg + weight * colors[:, s * slots : (s + 1) * slots]
        front = front + e
    through = jnp.exp(-front)
    out[pl.ds(0, sources, stride=3), :] = seg[:, 0:sources].T
    out[pl.ds(1, sources, stride=3), :] = seg[:, sources:slots].T
    sub = iota((8, sources), 0)
    both = jnp.where(
        sub == 0, through[:, 0:sources], jnp.where(sub == 1, through[:, sources:slots], 0.0)
    )
    place = (iota((8, LANES), 0) == iota((8, LANES), 1)).astype(F32)
    out[pl.ds(2, sources, stride=3), :] = contract(both, place, 0, 0, EXACT)
    leaving += fetch((out,), (out_h,), out_sems, 6)
    for copy in leaving:
        copy.wait()


def plane_tile(turned, step, part):
    return turned[:, pl.ds(pl.multiple_of(step * BLOCK + part * TILE, TILE), TILE)]


def forward(received, turned, first_t, hidden_t, feature_t, density_w):
    sources = received.shape[0] // 2
    slots = 2 * sources
    count = slots * S
    channels, cells = turned.shape
    hidden = first_t.shape[0]
    saved = [
        ((3 * sources, LANES), F32),
        ((16, slots), F32),
        ((8, count), F32),
        ((channels, count), BF16),
        ((hidden, count), F32),
        ((hidden, count), F32),
        ((channels + 8, count), F32),
    ]
    return pl.pallas_call(
        forward_kernel,
        in_specs=[IN_VMEM] * 6,
        out_specs=[IN_HBM] * len(saved),
        out_shape=[pltpu.HBM(shape, kind) for shape, kind in saved],
        scratch_shapes=[pltpu.VMEM(shape, kind) for shape, kind in saved]
        + [
            pltpu.VMEM((3 * CELLS, count), F32),
            pltpu.VMEM((channels, count), F32),
            pltpu.SemaphoreType.DMA((len(saved),)),
        ],
        compiler_params=grant(16),
        cost_estimate=price(2 * cells * count * channels, 8 * 2**20),
        name="forward",
    )(received, turned, first_t, hidden_t, feature_t, density_w)


def slopes(points, planes, first_step, last_step, carried, begun=None):
    count = points.shape[1]
    channels = planes.shape[1]
    steps = last_step - first_step
    moved = len(carried)
    ending = begun is not None
    ins = list(carried) + ([begun] if ending else [])

    def slope_kernel(points_h, planes_h, *refs):
        given, refs = refs[: len(ins)], refs[len(ins) :]
        out, brought, refs = refs[0], refs[1 : 1 + moved], refs[1 + moved :]
        held, turned, points, factor, slope, total, plane_sems, in_sems = refs[:8]
        total = out if ending else total
        arriving = fetch((points_h,), (points,), in_sems)
        plane_copy = plane_copies(planes_h, held, plane_sems, first_step, last_step)
        arriving += fetch(given, brought + refs[8:], in_sems, 1)
        total[...] = jnp.zeros_like(total)
        arriving[0].wait()
        for axis in range(3):
            span = slice(axis * CELLS, (axis + 1) * CELLS)
            factor[span, :], slope[span, :] = factors(points[axis : axis + 1, :])

        @pl.loop(first_step, last_step, unroll=3)
        def _(step):
            plane_copy(step).wait()
            local = pl.ds(pl.multiple_of((step - first_step) * BLOCK, BLOCK), BLOCK)
            turned[...] = held[local, :].T.astype(BF16)
            row_base, col_base, first, second = plane_axes(step)
            for rows_ref, cols_ref, axis in ((slope, factor, first), (factor, slope, second)):
                base = pl.multiple_of(axis * LANES, LANES)
                for lane in range(0, count, TILE):
                    columns = cols_ref[
                        pl.ds(pl.multiple_of(col_base, CELLS), CELLS), lane : lane + TILE
                    ]
                    acc = total[pl.ds(base, LANES), lane : lane + TILE]
                    for part in range(BLOCK // TILE):
                        tile = table_tile(rows_ref, row_base, part, columns, lane)
                        acc = acc + contract(turned[:, part * TILE : (part + 1) * TILE], tile, 1, 0)
                    total[pl.ds(base, LANES), lane : lane + TILE] = acc

        for copy in arriving[1:]:
            copy.wait()
        if ending:
            out[...] = out[...] + refs[8][...].astype(F32)
        else:
            out[...] = total[...].astype(BF16)

    shape = (3 * channels, count)
    return pl.pallas_call(
        slope_kernel,
        in_specs=[IN_HBM] * (2 + len(ins)),
        out_specs=[IN_VMEM] * (1 + moved),
        out_shape=[jax.ShapeDtypeStruct(shape, F32) if ending else pltpu.HBM(shape, BF16)] + shapes(*carried),
        scratch_shapes=[
            pltpu.VMEM((steps * BLOCK, channels), F32),
            pltpu.VMEM((channels, BLOCK), BF16),
            pltpu.VMEM(points.shape, F32),
            pltpu.VMEM((3 * CELLS, count), F32),
            pltpu.VMEM((3 * CELLS, count), F32),
            pltpu.VMEM((8, 128) if ending else shape, F32),
            pltpu.SemaphoreType.DMA((steps,)),
            pltpu.SemaphoreType.DMA((1 + len(ins),)),
        ]
        + ([pltpu.VMEM(shape, BF16)] if ending else []),
        compiler_params=grant(16),
        cost_estimate=price(4 * steps * BLOCK * count * channels, 6 * 2**20),
        name="slopes",
    )(far(points), far(planes), *map(far, ins))


def rays_kernel(home, route, ranks, targets, ray_h, back_h, ray_out, back, grads, out_sems):
    bricks = home.shape[0] // 3
    rays = targets.shape[0]
    slot = [route[(2 + c) * bricks : (3 + c) * bricks, :] for c in range(2)]
    seg = select_rows(slot[0], home[pl.ds(0, bricks, stride=3), :], 1, 0) + select_rows(
        slot[1], home[pl.ds(1, bricks, stride=3), :], 1, 0
    )
    lane = iota((1, LANES), 1)
    through = home[pl.ds(2, bricks, stride=3), :]
    passing = jnp.sum(
        select_rows(slot[0], jnp.where(lane == 0, through, 0.0), 1, 0)
        + select_rows(slot[1], jnp.where(lane == 1, through, 0.0), 1, 0),
        axis=1,
        keepdims=True,
    )
    feature = [seg[k * rays : (k + 1) * rays] for k in range(K)]
    pass_k = [passing[k * rays : (k + 1) * rays] for k in range(K)]
    rank_cols = contract(eye(rays), ranks[...].astype(F32), 1, 1, EXACT)
    rank = [rank_cols[:, k : k + 1] for k in range(K)]
    ones = jnp.ones((rays, 1), F32)

    def seen(k, skip=None):
        product = ones
        for other in range(K):
            if other != k and other != skip:
                product = product * jnp.where(rank[other] < rank[k], pass_k[other], 1.0)
        return product

    transmit = [seen(k) for k in range(K)]
    ray = jnp.zeros_like(feature[0])
    for k in range(K):
        ray = ray + transmit[k] * feature[k]
    ray_out[...] = ray
    leaving = fetch((ray_out,), (ray_h,), out_sems)
    grad = ray - targets[...]
    pull = [jnp.sum(grad * feature[k], axis=1, keepdims=True) for k in range(K)]
    for k in range(K):
        grads[k * rays : (k + 1) * rays, 0:LANES] = transmit[k] * grad
        pass_grad = jnp.zeros((rays, 1), F32)
        for behind in range(K):
            if behind != k:
                pass_grad = pass_grad + jnp.where(
                    rank[k] < rank[behind], pull[behind] * seen(behind, k), 0.0
                )
        grads[k * rays : (k + 1) * rays, LANES : 2 * LANES] = jnp.broadcast_to(
            pass_grad, (rays, LANES)
        )
    spread = None
    for c in range(2):
        both = select_rows(route[c * bricks : (c + 1) * bricks, :], grads[...], 1, 0)
        back[pl.ds(c, bricks, stride=3), :] = both[:, 0:LANES]
        own = jnp.where(lane == c, both[:, LANES : 2 * LANES], 0.0)
        spread = own if spread is None else spread + own
    back[pl.ds(2, bricks, stride=3), :] = spread
    leaving += fetch((back,), (back_h,), out_sems, 1)
    for copy in leaving:
        copy.wait()


def rays_step(home, route, ranks, targets):
    return pl.pallas_call(
        rays_kernel,
        out_specs=[IN_HBM] * 2,
        out_shape=(pltpu.HBM(targets.shape, F32), pltpu.HBM(home.shape, F32)),
        scratch_shapes=[
            pltpu.VMEM(targets.shape, F32),
            pltpu.VMEM(home.shape, F32),
            pltpu.VMEM((route.shape[1], 2 * LANES), F32),
            pltpu.SemaphoreType.DMA((2,)),
        ],
        compiler_params=grant(4),
        name="rays",
    )(home, route, ranks, targets)


def backward_kernel(
    cot, slope_ref, colors_ref, v2_ref, feature_w, density_h, v1_h, hidden_h, feats_h, first_h, rows_h,
    pose_gh, feature_gh, density_gh, hidden_gh, first_gh, feat_cot_h,
    density_w, v1_ref, hidden_w, feats, first_w, rows_ref,
    feature_g, density_g, hidden_g, first_g, feat_cot,
    color_cot, pair, pose_g, in_sems, out_sems,
):
    arriving = fetch(
        (density_h, v1_h, hidden_h, feats_h, first_h, rows_h),
        (density_w, v1_ref, hidden_w, feats, first_w, rows_ref),
        in_sems,
    )
    sources = cot.shape[0] // 3
    slots = 2 * sources
    seg_cot = jnp.concatenate(
        [cot[pl.ds(slot, sources, stride=3), :].T for slot in range(2)], axis=1
    )
    turned = cot[pl.ds(2, sources, stride=3), :].T
    pass_cot = jnp.concatenate([turned[0:1], turned[1:2]], axis=1)
    raw = colors_ref[LANES : LANES + 1, :]
    depth = (jnp.maximum(raw, 0.0) + jnp.log1p(jnp.exp(-jnp.abs(raw)))) * STEP
    front = jnp.zeros((1, slots), F32)
    weights, kept, pulls = [], [], []
    for s in range(S):
        span = slice(s * slots, (s + 1) * slots)
        e = depth[:, span]
        reach = jnp.exp(-front)
        weight = reach * (1.0 - jnp.exp(-e))
        colors = colors_ref[0:LANES, span]
        pulls.append(jnp.sum(colors * seg_cot, axis=0, keepdims=True))
        color_cot[:, span] = (weight * seg_cot * (1.0 - colors * colors)).astype(BF16)
        weights.append(weight)
        kept.append(reach * jnp.exp(-e))
        front = front + e
    behind = pass_cot * jnp.exp(-front)
    depth_cot = [None] * S
    for s in reversed(range(S)):
        depth_cot[s] = pulls[s] * kept[s] - behind
        behind = behind + pulls[s] * weights[s]
    raw_cot = (jnp.concatenate(depth_cot, axis=1) * STEP * jax.nn.sigmoid(raw)).astype(BF16)

    v2 = v2_ref[...]
    gate2 = jax.nn.sigmoid(v2)
    h2 = (v2 * gate2).astype(BF16)
    color_c = color_cot[...]
    feature_g[...] = contract(h2, color_c, 1, 1).astype(BF16).astype(F32)
    density_g[...] = contract(raw_cot, h2, 1, 1).astype(BF16).astype(F32)
    for copy in arriving:
        copy.wait()
    leaving = fetch((feature_g, density_g), (feature_gh, density_gh), out_sems)
    wide = jnp.where(iota((8, 1), 0) == 0, density_w[...].astype(F32), 0.0).astype(BF16)
    wide_cot = jnp.where(iota((8, 1), 0) == 0, raw_cot.astype(F32), 0.0).astype(BF16)
    h2_cot = (
        contract(feature_w[...], color_c, 1, 0) + contract(wide.T, wide_cot, 1, 0)
    ).astype(BF16).astype(F32)
    v2_cot = (h2_cot * gate2 * (1.0 + v2 * (1.0 - gate2))).astype(BF16)
    v1 = v1_ref[...]
    gate1 = jax.nn.sigmoid(v1)
    h1 = (v1 * gate1).astype(BF16)
    hidden_g[...] = contract(h1, v2_cot, 1, 1).astype(BF16).astype(F32)
    leaving += fetch((hidden_g,), (hidden_gh,), out_sems, 2)
    h1_cot = contract(hidden_w[...], v2_cot, 1, 0).astype(BF16).astype(F32)
    v1_cot = (h1_cot * gate1 * (1.0 + v1 * (1.0 - gate1))).astype(BF16)
    first_g[...] = contract(feats[...], v1_cot, 1, 1).astype(BF16).astype(F32)
    f_cot = contract(first_w[...], v1_cot, 1, 0).astype(BF16).astype(F32)
    feat_cot[...] = f_cot.T.astype(BF16)
    leaving += fetch((first_g, feat_cot), (first_gh, feat_cot_h), out_sems, 3)

    pull = [
        jnp.sum(slope_ref[a * LANES : (a + 1) * LANES, :] * f_cot, axis=0, keepdims=True)
        for a in range(3)
    ]
    rows = rows_ref[...]
    shift = [jnp.zeros((1, slots), F32)] * 3
    turn = [jnp.zeros((1, slots), F32)] * 3
    for s in range(S):
        distance = rows[12:13] + (s + 0.5) * STEP
        place = [rows[6 + i : 7 + i] + distance * rows[9 + i : 10 + i] for i in range(3)]
        part = [pull[a][:, s * slots : (s + 1) * slots] for a in range(3)]
        twist = cross(place, part)
        for a in range(3):
            shift[a] = shift[a] + part[a]
            turn[a] = turn[a] + twist[a]
    sub = iota((8, slots), 0)
    grads = jnp.zeros((8, slots), F32)
    for a in range(3):
        grads = jnp.where(sub == a, turn[a], grads)
        grads = jnp.where(sub == 3 + a, shift[a], grads)
    cams = 2 * LANES
    picked = (iota((cams, slots), 0) == rows[13:14].astype(jnp.int32)).astype(F32)
    pose = contract(grads, picked, 1, 1, EXACT)
    for copy in range(2):
        for half in range(2):
            start = copy * 12 + half * 6
            pair[start : start + 6, :] = pose[0:6, half * LANES : (half + 1) * LANES]
    two = pair[...]
    for copy in range(pose_g.shape[0] // 24):
        pose_g[copy * 24 : (copy + 1) * 24, :] = two
    leaving += fetch((pose_g,), (pose_gh,), out_sems, 5)
    for copy in leaving:
        copy.wait()


def backward(cot, near, distant, copies):
    density_w, _, hidden_w, feats, first_w, _ = distant
    feature_w = near[-1]
    channels, count = feats.shape
    outs = [(w.shape, F32) for w in (feature_w, density_w, hidden_w, first_w)] + [((count, channels), BF16)]
    return pl.pallas_call(
        backward_kernel,
        in_specs=[IN_VMEM] * (len(near) + 1) + [IN_HBM] * len(distant),
        out_specs=[IN_HBM] * (1 + len(outs)),
        out_shape=[pltpu.HBM((12 * copies, LANES), F32)] + [pltpu.HBM(shape, kind) for shape, kind in outs],
        scratch_shapes=[pltpu.VMEM(x.shape, x.dtype) for x in distant]
        + [pltpu.VMEM(shape, kind) for shape, kind in outs]
        + [
            pltpu.VMEM((channels, count), BF16),
            pltpu.VMEM((24, LANES), F32),
            pltpu.VMEM((12 * copies, LANES), F32),
            pltpu.SemaphoreType.DMA((len(distant),)),
            pltpu.SemaphoreType.DMA((1 + len(outs),)),
        ],
        compiler_params=grant(16),
        name="backward",
    )(cot, *near, *map(far, distant))


def plane_grads(points, cot, cells):
    count = points.shape[1]
    channels = cot.shape[1]
    blocks = 2

    def plane_kernel(points, cot, out, factor):
        @pl.when(pl.program_id(0) == 0)
        def _():
            for axis in range(3):
                factor[axis * CELLS : (axis + 1) * CELLS, :] = factors(points[axis : axis + 1, :])[0]

        for block in range(blocks):
            row_base, col_base, _, _ = plane_axes(pl.program_id(0) * blocks + block)
            for part in range(BLOCK // TILE):
                acc = jnp.zeros((TILE, channels), F32)
                for lane in range(0, count, TILE):
                    columns = factor[pl.ds(pl.multiple_of(col_base, CELLS), CELLS), lane : lane + TILE]
                    tile = table_tile(factor, row_base, part, columns, lane)
                    acc = acc + contract(tile, cot[lane : lane + TILE, :], 1, 0)
                start = block * BLOCK + part * TILE
                out[start : start + TILE, :] = acc

    return pl.pallas_call(
        plane_kernel,
        grid=(cells // (blocks * BLOCK),),
        in_specs=[IN_VMEM, IN_VMEM],
        out_specs=pl.BlockSpec((blocks * BLOCK, channels), lambda step: (step, 0)),
        out_shape=pltpu.HBM((cells, channels), F32),
        scratch_shapes=[pltpu.VMEM((3 * CELLS, count), F32)],
        compiler_params=grant(8),
        cost_estimate=price(2 * cells * count * channels, cells * channels * 4),
        name="plane_grads",
    )(far(points), far(cot))


def exchange(rows, peers):
    wide = rows.reshape(peers, 1, rows.size // peers)
    moved = lax.all_to_all(wide, AXES, split_axis=0, concat_axis=0, tiled=True)
    return moved.reshape(rows.shape)


def add_kernel(parts, out):
    total = parts[0:24, :]
    for source in range(1, parts.shape[0] // 24):
        total = total + parts[source * 24 : (source + 1) * 24, :]
    total = total[0:12] + total[12:24]
    out[:, 0:LANES] = total[0:6]
    out[:, LANES : 2 * LANES] = total[6:12]


def add(parts, shape):
    return pl.pallas_call(
        add_kernel, out_shape=pltpu.HBM(shape, F32), compiler_params=grant(2), name="add"
    )(parts)


def per_device(
    anchors, directions, ray_start, camera_ids, brick_ids, brick_rank, targets,
    planes, first_weight, hidden_weight, feature_weight, density_weight, poses,
):
    bricks = lax.axis_size(AXES)
    cells = planes.shape[1]
    steps = cells // BLOCK
    ids, ranks = brick_ids.T, brick_rank.T
    outgoing = dispatch(
        anchors, directions, ray_start[None], camera_ids[None], ids, ranks, poses, bricks
    )
    received = exchange(outgoing, bricks)
    turned, first_t, hidden_t, feature_t, density_o, first_o, hidden_o, feature_o, route = prepare(
        planes[0], first_weight[0], hidden_weight[0, 0], feature_weight[0], density_weight, ids, bricks
    )
    sent, rows, points, feats, v1, v2, colors = forward(
        received, turned, first_t, hidden_t, feature_t, density_o
    )
    home = exchange(sent, bricks)
    begun, *ray_data = slopes(points, planes[0], 0, steps // 2, [route, ranks, targets])
    ray_feature, back = rays_step(home, *ray_data)
    cot = exchange(back, bricks)
    later_points, back = lax.optimization_barrier((points, back))
    near = slopes(
        later_points, planes[0], steps // 2, steps, [colors, v2, feature_o], begun
    )
    distant = [density_weight, v1, hidden_o, feats, first_o, rows]
    pose_part, feature_g, density_g, hidden_g, first_g, feat_cot = backward(
        cot, near, distant, bricks
    )
    pose_grad = add(exchange(pose_part, bricks), poses.shape)
    plane_grad = plane_grads(points, feat_cot, cells)
    return (
        ray_feature,
        plane_grad[None],
        first_g[None],
        hidden_g[None, None],
        feature_g[None],
        density_g,
        pose_grad,
    )


def solution(mesh):
    rays = P(AXES)
    in_specs = (
        P(None, AXES), P(None, AXES), rays, rays, P(AXES, None), P(AXES, None), P(AXES, None),
        P(AXES, None, None), P(AXES, None, None), P(AXES, None, None, None), P(AXES, None, None),
        P(AXES, None), P(),
    )
    out_specs = (
        P(AXES, None), P(AXES, None, None), P(AXES, None, None), P(AXES, None, None, None),
        P(AXES, None, None), P(AXES, None), P(),
    )
    return jax.shard_map(
        per_device, mesh=mesh, in_specs=in_specs, out_specs=out_specs, check_vma=False
    )
```

time: 102 us -> 93 us (0.912)
  Pallas kernels: 56.8 us -> 44.5 us
  waiting for transfers between devices: 9.65 us -> 18.6 us
  starting transfers between devices: 34 us -> 28.8 us
    pallas_call x10 -> x8, Pallas kernels: 54.8 us -> 42.5 us  [the longest x2 14.1 us: slopes(): pl.pallas_call(slope_kernel, in_specs=[IN_HBM] * (2 + len(ins)), out_spec...]
    all_to_all x3 -> x4, waiting for transfers between devices: 8.87 us -> 18.6 us  [exchange(): moved = lax.all_to_all(wide, AXES, split_axis=0, concat_axis=0, tiled=True)]
    all_to_all x2 -> x0, starting transfers between devices: 8.92 us -> none  [swap(): lax.all_to_all(stacked, (axis,), split_axis=0, concat_axis=0, tiled=True)]
    all_to_all x3 -> x4, starting transfers between devices: 25.1 us -> 28.8 us  [exchange(): moved = lax.all_to_all(wide, AXES, split_axis=0, concat_axis=0, tiled=True)]
  transfers between devices with their start and end apart: 5 -> 4, of which waited for: 4 -> 4; matrix products, arithmetic and copies ran while one was open for 0% -> 0% of each run, Pallas kernels for 34% -> 31%
where the time goes in v3:
time: 93 us; the launch traced here: 92.6 us
  Pallas kernels  44.5 us (48%)
  starting transfers between devices  28.8 us (31%)
  waiting for transfers between devices  18.6 us (20%)
    all_to_all x4, starting transfers between devices, exchange(): moved = lax.all_to_all(wide, AXES, split_axis=0, concat_axis=0, tiled=True)  28.8 us
    all_to_all x4, waiting for transfers between devices, exchange(): moved = lax.all_to_all(wide, AXES, split_axis=0, concat_axis=0, tiled=True)  18.6 us
    pallas_call x2, Pallas kernels, slopes(): pl.pallas_call(slope_kernel, in_specs=[IN_HBM] * (2 + len(ins)), out_spec...  14.1 us
    pallas_call x1, Pallas kernels, plane_grads(): pl.pallas_call(plane_kernel, grid=(cells // (blocks * BLOCK),), in_specs=...  9.68 us
    pallas_call x1, Pallas kernels, forward(): pl.pallas_call(forward_kernel, in_specs=[IN_VMEM] * 6, out_specs=[IN_HBM]...  6.9 us
    pallas_call x1, Pallas kernels, prepare(): pl.pallas_call(prepare_kernel, in_specs=[IN_HBM] * 6, out_specs=[IN_VMEM]...  4.84 us
    pallas_call x1, Pallas kernels, backward(): pl.pallas_call(backward_kernel, in_specs=[IN_VMEM] * (len(near) + 1) + [I...  4.54 us
    pallas_call x1, Pallas kernels, dispatch(): pl.pallas_call(dispatch_kernel, out_shape=jax.ShapeDtypeStruct((2 * brick...  1.99 us
  transfers between devices with their start and end apart: 4, of which 4 were waited for; matrix products, arithmetic and copies ran while one was open for 0% of the time, Pallas kernels for 31%

profile of v3, /device:TPU:1, one launch (start us, length us, event | category | flops | bytes accessed | tf_op | source)
XLA Modules:
  0.0 92.6 jit_solution(879815641706827215)
XLA Ops:
  0.6 2.0 %dispatch.1 = f32[256,128]{1,0:T(8,128)} custom-call(f32[3,32]{1,0:T(4,128)} %anchors.1, f32[3,32]{1,0:T(4,128)} %directions.1, f32[1,32]{1,0:T(1,128)} %bitcast.37, s32[1,32]{1,0:T(1,128)} %bitcast.38, s32[4,32]{1,0:T(4,128)} %bitcast.33, s32[4,32]{1,0:T(4,128)} %bitcast.35, f32[6,256]{1,0:T(8,128)} %poses.1), custom_call_target="tpu_custom_call" | custom-call | tf_op jit(solution)/shard_map/dispatch/pallas_call | solution.py:119
  2.6 11.5 %all-to-all-start = ((f32[128,1,256]{2,1,0:T(1,128)}), f32[128,1,256]{2,1,0:T(1,128)S(1)}, u32[]{:S(2)}, u32[]{:S(2)}) async-start(f32[128,1,256]{2,1,0:T(1,128)} %bitcast.4), calls=%async_computation | async-start | bytes 262144 | tf_op jit(solution)/shard_map/all_to_all | solution.py:694
  14.1 4.8 %prepare.1 = (bf16[128,12288]{1,0:T(8,128)(2,1)S(1)}, bf16[256,128]{1,0:T(8,128)(2,1)S(1)}, bf16[256,256]{1,0:T(8,128)(2,1)S(1)}, bf16[128,256]{1,0:T(8,128)(2,1...) custom-call(f32[12288,128]{1,0:T(8,128)} %bitcast.24, ...), custom_call_target="tpu_custom_call" | custom-call | bytes 10485760 | tf_op jit(solution)/shard_map/prepare/pallas_call | solution.py:257
  19.0 5.2 %all-to-all-done = f32[128,1,256]{2,1,0:T(1,128)S(1)} async-done(((f32[128,1,256]{2,1,0:T(1,128)}), f32[128,1,256]{2,1,0:T(1,128)S(1)}, u32[]{:S(2)}, u32[]{:S(2)}) %all-to-all-start) | async-done | bytes 131104 | tf_op jit(solution)/shard_map/all_to_all | solution.py:694
  24.1 6.9 %forward.1 = (f32[384,128]{1,0:T(8,128)}, f32[16,256]{1,0:T(8,128)}, f32[8,1024]{1,0:T(8,128)}, bf16[128,1024]{1,0:T(8,128)(2,1)}, f32[256,1024]{1,0:T(8,128)}, ...) custom-call(f32[256,128]{1,0:T(8,128)S(1)} %bitcast.23, bf16[128,12288]{1,0:T(8,128)(2,1)S(1)} %get-tuple-element.40.turned, ...), custom_call_target="tpu_custom_call" | custom-call | flops 3221225472 | bytes 8388608 | tf_op jit(solution)/shard_map/forward/pallas_call | solution.py:368
  31.0 4.6 %all-to-all-start.1 = ((f32[128,1,384]{2,1,0:T(1,128)}), f32[128,1,384]{2,1,0:T(1,128)S(1)}, u32[]{:S(2)}, u32[]{:S(2)}) async-start(f32[128,1,384]{2,1,0:T(1,128)} %bitcast.29), calls=%async_computation.1 | async-start | bytes 393216 | tf_op jit(solution)/shard_map/all_to_all | solution.py:694
  35.7 7.5 %slopes.2 = (bf16[384,1024]{1,0:T(8,128)(2,1)}, bf16[512,128]{1,0:T(8,128)(2,1)S(1)}, s32[4,32]{1,0:T(4,128)S(1)}, f32[32,128]{1,0:T(8,128)S(1)}) custom-call(f32[8,1024]{1,0:T(8,128)} %get-tuple-element.53.points_h.points, f32[12288,128]{1,0:T(8,128)} %bitcast.25, bf16[512,128]{1,0:T(8,128)(2,1)} %get-tuple-element.47.refs_0_, s32[4,32]{1,0:T(4,128)} %bitcast.36, ...), custom_call_target="tpu_custom_call" | custom-call | flops 3221225472 | bytes 6291456 | tf_op jit(solution)/shard_map/slopes/pallas_call | solution.py:433
  43.2 3.0 %all-to-all-done.1 = f32[128,1,384]{2,1,0:T(1,128)S(1)} async-done(((f32[128,1,384]{2,1,0:T(1,128)}), f32[128,1,384]{2,1,0:T(1,128)S(1)}, u32[]{:S(2)}, u32[]{:S(2)}) %all-to-all-start.1) | async-done | bytes 196640 | tf_op jit(solution)/shard_map/all_to_all | solution.py:694
  46.2 1.8 %rays.1 = (f32[32,128]{1,0:T(8,128)}, f32[384,128]{1,0:T(8,128)}) custom-call(f32[384,128]{1,0:T(8,128)S(1)} %bitcast.22, bf16[512,128]{1,0:T(8,128)(2,1)S(1)} %get-tuple-element.48.route, s32[4,32]{1,0:T(4,128)S(1)} %get-tuple-element.49.ranks, f32[32,128]{1,0:T(8,128)S(1)} %get-tuple-element.50.targets), custom_call_target="tpu_custom_call" | custom-call | tf_op jit(solution)/shard_map/rays/pallas_call | solution.py:515
  48.0 6.8 %all-to-all-start.2 = ((f32[128,1,384]{2,1,0:T(1,128)}), f32[128,1,384]{2,1,0:T(1,128)S(1)}, u32[]{:S(2)}, u32[]{:S(2)}) async-start(f32[128,1,384]{2,1,0:T(1,128)} %bitcast.30), calls=%async_computation.2 | async-start | bytes 393216 | tf_op jit(solution)/shard_map/all_to_all | solution.py:694
  54.8 6.6 %slopes.3 = (f32[384,1024]{1,0:T(8,128)S(1)}, f32[136,1024]{1,0:T(8,128)S(1)}, f32[256,1024]{1,0:T(8,128)S(1)}, bf16[256,128]{1,0:T(8,128)(2,1)S(1)}) custom-call(f32[8,1024]{1,0:T(8,128)} %get-tuple-element.53.points_h.points, f32[12288,128]{1,0:T(8,128)} %bitcast.26, f32[136,1024]{1,0:T(8,128)} %get-tuple-element.54.refs_0_, ...), custom_call_target="tpu_custom_call" | custom-call | flops 3221225472 | bytes 6291456 | tf_op jit(solution)/shard_map/slopes/pallas_call | solution.py:433
  61.4 3.9 %all-to-all-done.2 = f32[128,1,384]{2,1,0:T(1,128)S(1)} async-done(((f32[128,1,384]{2,1,0:T(1,128)}), f32[128,1,384]{2,1,0:T(1,128)S(1)}, u32[]{:S(2)}, u32[]{:S(2)}) %all-to-all-start.2) | async-done | bytes 196640 | tf_op jit(solution)/shard_map/all_to_all | solution.py:694
  65.3 4.5 %backward.1 = (f32[1536,128]{1,0:T(8,128)}, f32[256,128]{1,0:T(8,128)}, f32[1,256]{1,0:T(1,128)}, f32[256,256]{1,0:T(8,128)}, f32[128,256]{1,0:T(8,128)}, /*index=5*/bf16[1024,128]{1,0:T(8,128)(2,1)}) custom-call(f32[384,128]{1,0:T(8,128)S(1)} %bitcast.21, f32[384,1024]{1,0:T(8,128)S(1)} %get-tuple-element.58.slope_ref, ...), custom_call_target="tpu_custom_call" | custom-call | tf_op jit(solution)/shard_map/backward/pallas_call | solution.py:638
  69.9 5.8 %all-to-all-start.3 = ((f32[128,1,1536]{2,1,0:T(1,128)}), f32[128,1,1536]{2,1,0:T(1,128)S(1)}, u32[]{:S(2)}, u32[]{:S(2)}) async-start(f32[128,1,1536]{2,1,0:T(1,128)} %bitcast.27), calls=%async_computation.3 | async-start | bytes 1572864 | tf_op jit(solution)/shard_map/all_to_all | solution.py:694
  75.7 9.7 %plane_grads.1 = f32[12288,128]{1,0:T(8,128)} custom-call(f32[8,1024]{1,0:T(8,128)} %get-tuple-element.53.points_h.points, bf16[1024,128]{1,0:T(8,128)(2,1)} %get-tuple-element.67.cot), custom_call_target="tpu_custom_call" | custom-call | flops 3221225472 | bytes 6291456 | tf_op jit(solution)/shard_map/plane_grads/pallas_call | solution.py:679
  85.4 6.5 %all-to-all-done.3 = f32[128,1,1536]{2,1,0:T(1,128)S(1)} async-done(((f32[128,1,1536]{2,1,0:T(1,128)}), f32[128,1,1536]{2,1,0:T(1,128)S(1)}, u32[]{:S(2)}, u32[]{:S(2)}) %all-to-all-start.3) | async-done | bytes 786464 | tf_op jit(solution)/shard_map/all_to_all | solution.py:694
  91.9 0.7 add.1
Async XLA Ops:
  2.6 21.5 %all-to-all-start = ((f32[128,1,256]{2,1,0:T(1,128)}), f32[128,1,256]{2,1,0:T(1,128)S(1)}, u32[]{:S(2)}, u32[]{:S(2)}) async-start(f32[128,1,256]{2,1,0:T(1,128)} %bitcast.4), calls=%async_computation | async-start | bytes 262144 | tf_op jit(solution)/shard_map/all_to_all | solution.py:694
  31.0 15.1 %all-to-all-start.1 = ((f32[128,1,384]{2,1,0:T(1,128)}), f32[128,1,384]{2,1,0:T(1,128)S(1)}, u32[]{:S(2)}, u32[]{:S(2)}) async-start(f32[128,1,384]{2,1,0:T(1,128)} %bitcast.29), calls=%async_computation.1 | async-start | bytes 393216 | tf_op jit(solution)/shard_map/all_to_all | solution.py:694
  48.0 17.3 %all-to-all-start.2 = ((f32[128,1,384]{2,1,0:T(1,128)}), f32[128,1,384]{2,1,0:T(1,128)S(1)}, u32[]{:S(2)}, u32[]{:S(2)}) async-start(f32[128,1,384]{2,1,0:T(1,128)} %bitcast.30), calls=%async_computation.2 | async-start | bytes 393216 | tf_op jit(solution)/shard_map/all_to_all | solution.py:694
  69.9 22.1 %all-to-all-start.3 = ((f32[128,1,1536]{2,1,0:T(1,128)}), f32[128,1,1536]{2,1,0:T(1,128)S(1)}, u32[]{:S(2)}, u32[]{:S(2)}) async-start(f32[128,1,1536]{2,1,0:T(1,128)} %bitcast.27), calls=%async_computation.3 | async-start | bytes 1572864 | tf_op jit(solution)/shard_map/all_to_all | solution.py:694

commit v4 on v3

--- a/solution.py
+++ b/solution.py
@@ -54,6 +54,18 @@
     return total
 
 
+def with_onehot(values, onehot, left_dim, right_dim):
+    picked = onehot.astype(BF16)
+    total = None
+    rest = values
+    for _ in range(3):
+        part = rest.astype(BF16)
+        rest = rest - part.astype(F32)
+        term = contract(part, picked, left_dim, right_dim)
+        total = term if total is None else total + term
+    return total
+
+
 def eye(size):
     return (iota((size, size), 0) == iota((size, size), 1)).astype(F32)
 
@@ -92,7 +104,7 @@
     spread, own = spread_of(rays)
     id_row = segment_row(ids, spread, own)
     picked = (iota((poses.shape[1], rays), 0) == cameras[...]).astype(F32)
-    pose = contract(poses[...], picked, 1, 0, EXACT)
+    pose = with_onehot(poses[...], picked, 1, 0)
     turn = [pose[i : i + 1] for i in range(3)]
     anchor = [anchors[i : i + 1, :] for i in range(3)]
     direction = [directions[i : i + 1, :] for i in range(3)]
@@ -107,7 +119,7 @@
     packed[13:14, :] = cameras[...].astype(F32)
     packed[14:16, :] = jnp.zeros((2, rays), F32)
     rank_row = segment_row(ranks, spread, own)
-    values = contract(packed[...], spread, 1, 0, EXACT)
+    values = with_onehot(packed[...], spread, 1, 0)
     values = values + jnp.where(iota((16, 1), 0) == 12, rank_row * (S * STEP), 0.0)
     for slot, taken in enumerate(route_of(id_row, bricks)):
         rows = select_rows(taken, values, 1, 1)
@@ -126,13 +138,8 @@
 
 
 def ray_rows(received, sources):
-    same = eye(sources)
     return jnp.concatenate(
-        [
-            contract(received[pl.ds(slot, sources, stride=2), :], same, 0, 0, EXACT)[0:16]
-            for slot in range(2)
-        ],
-        axis=1,
+        [received[pl.ds(slot, sources, stride=2), :].T[0:16] for slot in range(2)], axis=1
     )
 
 
@@ -170,7 +177,7 @@
 def plane_axes(step):
     plane = step // (CELLS * CELLS // BLOCK)
     first = plane // 2
-    second = jnp.minimum(plane + 1, 2)
+    second = min(plane + 1, 2) if isinstance(step, int) else jnp.minimum(plane + 1, 2)
     start = (step % (CELLS * CELLS // BLOCK)) * (BLOCK // CELLS)
     return first * CELLS + start, second * CELLS, first, second
 
@@ -280,7 +287,7 @@
 
 def forward_kernel(
     received, turned, first_t, hidden_t, feature_t, density_w,
-    out_h, rows_h, points_h, feats_h, v1_h, v2_h, colors_h,
+    out_h, rows_h, points_h, feats_h, v1_h, v2_h, colors_h, turned_h,
     out, rows_v, points_v, feats_v, v1_v, v2_v, colors_v,
     factor, total, out_sems,
 ):
@@ -288,6 +295,7 @@
     slots = 2 * sources
     count = slots * S
     steps = turned.shape[1] // BLOCK
+    leaving = fetch((turned,), (turned_h,), out_sems, 7)
     rows = ray_rows(received, sources)
     rows_v[...] = rows
     points = sample_rows(rows)
@@ -295,18 +303,18 @@
         factor[axis * CELLS : (axis + 1) * CELLS, :] = factors(coordinate)[0]
         points_v[axis : axis + 1, :] = coordinate
     points_v[3:8, :] = jnp.zeros((5, count), F32)
-    leaving = fetch((rows_v, points_v), (rows_h, points_h), out_sems)
+    leaving += fetch((rows_v, points_v), (rows_h, points_h), out_sems)
     total[...] = jnp.zeros_like(total)
 
-    @pl.loop(0, steps, unroll=4)
-    def _(step):
+    for step in range(steps):
         row_base, col_base, _, _ = plane_axes(step)
         for lane in range(0, count, TILE):
-            columns = factor[pl.ds(pl.multiple_of(col_base, CELLS), CELLS), lane : lane + TILE]
+            columns = factor[col_base : col_base + CELLS, lane : lane + TILE]
             acc = total[:, lane : lane + TILE]
             for part in range(BLOCK // TILE):
                 tile = table_tile(factor, row_base, part, columns, lane)
-                acc = acc + contract(plane_tile(turned, step, part), tile, 1, 0)
+                start = step * BLOCK + part * TILE
+                acc = acc + contract(turned[:, start : start + TILE], tile, 1, 0)
             total[:, lane : lane + TILE] = acc
 
     feats = total[...].astype(BF16)
@@ -335,19 +343,14 @@
     through = jnp.exp(-front)
     out[pl.ds(0, sources, stride=3), :] = seg[:, 0:sources].T
     out[pl.ds(1, sources, stride=3), :] = seg[:, sources:slots].T
-    sub = iota((8, sources), 0)
+    sub = iota((LANES, sources), 0)
     both = jnp.where(
         sub == 0, through[:, 0:sources], jnp.where(sub == 1, through[:, sources:slots], 0.0)
     )
-    place = (iota((8, LANES), 0) == iota((8, LANES), 1)).astype(F32)
-    out[pl.ds(2, sources, stride=3), :] = contract(both, place, 0, 0, EXACT)
+    out[pl.ds(2, sources, stride=3), :] = both.T
     leaving += fetch((out,), (out_h,), out_sems, 6)
     for copy in leaving:
         copy.wait()
-
-
-def plane_tile(turned, step, part):
-    return turned[:, pl.ds(pl.multiple_of(step * BLOCK + part * TILE, TILE), TILE)]
 
 
 def forward(received, turned, first_t, hidden_t, feature_t, density_w):
@@ -368,13 +371,13 @@
     return pl.pallas_call(
         forward_kernel,
         in_specs=[IN_VMEM] * 6,
-        out_specs=[IN_HBM] * len(saved),
-        out_shape=[pltpu.HBM(shape, kind) for shape, kind in saved],
+        out_specs=[IN_HBM] * (len(saved) + 1),
+        out_shape=[pltpu.HBM(shape, kind) for shape, kind in saved + [(turned.shape, BF16)]],
         scratch_shapes=[pltpu.VMEM(shape, kind) for shape, kind in saved]
         + [
             pltpu.VMEM((3 * CELLS, count), F32),
             pltpu.VMEM((channels, count), F32),
-            pltpu.SemaphoreType.DMA((len(saved),)),
+            pltpu.SemaphoreType.DMA((len(saved) + 1,)),
         ],
         compiler_params=grant(16),
         cost_estimate=price(2 * cells * count * channels, 8 * 2**20),
@@ -382,9 +385,9 @@
     )(received, turned, first_t, hidden_t, feature_t, density_w)
 
 
-def slopes(points, planes, first_step, last_step, carried, begun=None):
+def slopes(points, planes_t, first_step, last_step, carried, begun=None):
     count = points.shape[1]
-    channels = planes.shape[1]
+    channels = planes_t.shape[0]
     steps = last_step - first_step
     moved = len(carried)
     ending = begun is not None
@@ -393,51 +396,66 @@
     def slope_kernel(points_h, planes_h, *refs):
         given, refs = refs[: len(ins)], refs[len(ins) :]
         out, brought, refs = refs[0], refs[1 : 1 + moved], refs[1 + moved :]
-        held, turned, points, factor, slope, total, plane_sems, in_sems = refs[:8]
-        total = out if ending else total
+        turned, points, factor, slope, total, plane_sems, in_sems = refs[:7]
+        if ending:
+            total = out
+        else:
+            rounded, out_sems = refs[7:]
         arriving = fetch((points_h,), (points,), in_sems)
-        plane_copy = plane_copies(planes_h, held, plane_sems, first_step, last_step)
-        arriving += fetch(given, brought + refs[8:], in_sems, 1)
+        blocks = [
+            pltpu.make_async_copy(
+                planes_h.at[:, (first_step + step) * BLOCK : (first_step + step + 1) * BLOCK],
+                turned.at[:, step * BLOCK : (step + 1) * BLOCK],
+                plane_sems.at[step],
+            )
+            for step in range(steps)
+        ]
+        for copy in blocks:
+            copy.start()
+        arriving += fetch(given, brought + (refs[7:] if ending else ()), in_sems, 1)
         total[...] = jnp.zeros_like(total)
         arriving[0].wait()
         for axis in range(3):
             span = slice(axis * CELLS, (axis + 1) * CELLS)
             factor[span, :], slope[span, :] = factors(points[axis : axis + 1, :])
 
-        @pl.loop(first_step, last_step, unroll=3)
-        def _(step):
-            plane_copy(step).wait()
-            local = pl.ds(pl.multiple_of((step - first_step) * BLOCK, BLOCK), BLOCK)
-            turned[...] = held[local, :].T.astype(BF16)
-            row_base, col_base, first, second = plane_axes(step)
+        leaving = []
+        for step in range(steps):
+            blocks[step].wait()
+            row_base, col_base, first, second = plane_axes(first_step + step)
             for rows_ref, cols_ref, axis in ((slope, factor, first), (factor, slope, second)):
-                base = pl.multiple_of(axis * LANES, LANES)
+                rows = slice(axis * LANES, (axis + 1) * LANES)
                 for lane in range(0, count, TILE):
-                    columns = cols_ref[
-                        pl.ds(pl.multiple_of(col_base, CELLS), CELLS), lane : lane + TILE
-                    ]
-                    acc = total[pl.ds(base, LANES), lane : lane + TILE]
+                    here = slice(lane, lane + TILE)
+                    columns = cols_ref[col_base : col_base + CELLS, here]
+                    acc = total[rows, here]
                     for part in range(BLOCK // TILE):
                         tile = table_tile(rows_ref, row_base, part, columns, lane)
-                        acc = acc + contract(turned[:, part * TILE : (part + 1) * TILE], tile, 1, 0)
-                    total[pl.ds(base, LANES), lane : lane + TILE] = acc
-
-        for copy in arriving[1:]:
-            copy.wait()
+                        start = step * BLOCK + part * TILE
+                        acc = acc + contract(turned[:, start : start + TILE], tile, 1, 0)
+                    total[rows, here] = acc
         if ending:
-            out[...] = out[...] + refs[8][...].astype(F32)
+            for copy in arriving[1:]:
+                copy.wait()
+            out[...] = out[...] + refs[7][...].astype(F32)
         else:
-            out[...] = total[...].astype(BF16)
+            for axis in range(3):
+                rows = slice(axis * LANES, (axis + 1) * LANES)
+                rounded[rows, :] = total[rows, :].astype(BF16)
+                copy = pltpu.make_async_copy(rounded.at[rows, :], out.at[rows, :], out_sems.at[axis])
+                copy.start()
+                leaving.append(copy)
+            for copy in arriving[1:] + leaving:
+                copy.wait()
 
     shape = (3 * channels, count)
     return pl.pallas_call(
         slope_kernel,
         in_specs=[IN_HBM] * (2 + len(ins)),
-        out_specs=[IN_VMEM] * (1 + moved),
+        out_specs=[IN_VMEM if ending else IN_HBM] + [IN_VMEM] * moved,
         out_shape=[jax.ShapeDtypeStruct(shape, F32) if ending else pltpu.HBM(shape, BF16)] + shapes(*carried),
         scratch_shapes=[
-            pltpu.VMEM((steps * BLOCK, channels), F32),
-            pltpu.VMEM((channels, BLOCK), BF16),
+            pltpu.VMEM((channels, steps * BLOCK), BF16),
             pltpu.VMEM(points.shape, F32),
             pltpu.VMEM((3 * CELLS, count), F32),
             pltpu.VMEM((3 * CELLS, count), F32),
@@ -445,11 +463,12 @@
             pltpu.SemaphoreType.DMA((steps,)),
             pltpu.SemaphoreType.DMA((1 + len(ins),)),
         ]
-        + ([pltpu.VMEM(shape, BF16)] if ending else []),
+        + [pltpu.VMEM(shape, BF16)]
+        + ([] if ending else [pltpu.SemaphoreType.DMA((3,))]),
         compiler_params=grant(16),
         cost_estimate=price(4 * steps * BLOCK * count * channels, 6 * 2**20),
         name="slopes",
-    )(far(points), far(planes), *map(far, ins))
+    )(far(points), far(planes_t), *map(far, ins))
 
 
 def rays_kernel(home, route, ranks, targets, ray_h, back_h, ray_out, back, grads, out_sems):
@@ -617,7 +636,7 @@
         grads = jnp.where(sub == 3 + a, shift[a], grads)
     cams = 2 * LANES
     picked = (iota((cams, slots), 0) == rows[13:14].astype(jnp.int32)).astype(F32)
-    pose = contract(grads, picked, 1, 1, EXACT)
+    pose = with_onehot(grads, picked, 1, 1)
     for copy in range(2):
         for half in range(2):
             start = copy * 12 + half * 6
@@ -725,16 +744,16 @@
     turned, first_t, hidden_t, feature_t, density_o, first_o, hidden_o, feature_o, route = prepare(
         planes[0], first_weight[0], hidden_weight[0, 0], feature_weight[0], density_weight, ids, bricks
     )
-    sent, rows, points, feats, v1, v2, colors = forward(
+    sent, rows, points, feats, v1, v2, colors, turned_far = forward(
         received, turned, first_t, hidden_t, feature_t, density_o
     )
     home = exchange(sent, bricks)
-    begun, *ray_data = slopes(points, planes[0], 0, steps // 2, [route, ranks, targets])
+    begun, *ray_data = slopes(points, turned_far, 0, steps // 2, [route, ranks, targets])
     ray_feature, back = rays_step(home, *ray_data)
     cot = exchange(back, bricks)
     later_points, back = lax.optimization_barrier((points, back))
     near = slopes(
-        later_points, planes[0], steps // 2, steps, [colors, v2, feature_o], begun
+        later_points, turned_far, steps // 2, steps, [colors, v2, feature_o], begun
     )
     distant = [density_weight, v1, hidden_o, feats, first_o, rows]
     pose_part, feature_g, density_g, hidden_g, first_g, feat_cot = backward(

time: 93 us -> 89.9 us (0.967)
  Pallas kernels: 44.5 us -> 41.5 us
  starting transfers between devices: 28.8 us -> 26.4 us
  waiting for transfers between devices: 18.6 us -> 20.8 us
    all_to_all x4, starting transfers between devices: 28.8 us -> 26.4 us  [exchange(): moved = lax.all_to_all(wide, AXES, split_axis=0, concat_axis=0, tiled=True)]
    pallas_call x2, Pallas kernels: 14.1 us -> 11.8 us  [slopes(): pl.pallas_call(slope_kernel, in_specs=[IN_HBM] * (2 + len(ins)), out_spec...]
    all_to_all x4, waiting for transfers between devices: 18.6 us -> 20.8 us  [exchange(): moved = lax.all_to_all(wide, AXES, split_axis=0, concat_axis=0, tiled=True)]
  transfers between devices with their start and end apart: 4 -> 4, of which waited for: 4 -> 4; matrix products, arithmetic and copies ran while one was open for 0% -> 0% of each run, Pallas kernels for 31% -> 30%
where the time goes in v4:
time: 89.9 us; the launch traced here: 89.5 us
  Pallas kernels  41.5 us (46%)
  starting transfers between devices  26.4 us (29%)
  waiting for transfers between devices  20.8 us (23%)
    all_to_all x4, starting transfers between devices, exchange(): moved = lax.all_to_all(wide, AXES, split_axis=0, concat_axis=0, tiled=True)  26.4 us
    all_to_all x4, waiting for transfers between devices, exchange(): moved = lax.all_to_all(wide, AXES, split_axis=0, concat_axis=0, tiled=True)  20.8 us
    pallas_call x2, Pallas kernels, slopes(): pl.pallas_call(slope_kernel, in_specs=[IN_HBM] * (2 + len(ins)), out_spec...  11.8 us
    pallas_call x1, Pallas kernels, plane_grads(): pl.pallas_call(plane_kernel, grid=(cells // (blocks * BLOCK),), in_specs=...  9.79 us
    pallas_call x1, Pallas kernels, forward(): pl.pallas_call(forward_kernel, in_specs=[IN_VMEM] * 6, out_specs=[IN_HBM]...  6.26 us
    pallas_call x1, Pallas kernels, prepare(): pl.pallas_call(prepare_kernel, in_specs=[IN_HBM] * 6, out_specs=[IN_VMEM]...  4.84 us
    pallas_call x1, Pallas kernels, backward(): pl.pallas_call(backward_kernel, in_specs=[IN_VMEM] * (len(near) + 1) + [I...  4.42 us
    pallas_call x1, Pallas kernels, dispatch(): pl.pallas_call(dispatch_kernel, out_shape=jax.ShapeDtypeStruct((2 * brick...  1.95 us
  transfers between devices with their start and end apart: 4, of which 4 were waited for; matrix products, arithmetic and copies ran while one was open for 0% of the time, Pallas kernels for 30%

profile of v4, /device:TPU:1, one launch (start us, length us, event | category | flops | bytes accessed | tf_op | source)
XLA Modules:
  0.0 89.5 jit_solution(3324533613139876047)
XLA Ops:
  0.6 1.9 %dispatch.1 = f32[256,128]{1,0:T(8,128)} custom-call(f32[3,32]{1,0:T(4,128)} %anchors.1, f32[3,32]{1,0:T(4,128)} %directions.1, f32[1,32]{1,0:T(1,128)} %bitcast.35, s32[1,32]{1,0:T(1,128)} %bitcast.36, s32[4,32]{1,0:T(4,128)} %bitcast.31, s32[4,32]{1,0:T(4,128)} %bitcast.33, f32[6,256]{1,0:T(8,128)} %poses.1), custom_call_target="tpu_custom_call" | custom-call | tf_op jit(solution)/shard_map/dispatch/pallas_call | solution.py:131
  2.6 11.5 %all-to-all-start = ((f32[128,1,256]{2,1,0:T(1,128)}), f32[128,1,256]{2,1,0:T(1,128)S(1)}, u32[]{:S(2)}, u32[]{:S(2)}) async-start(f32[128,1,256]{2,1,0:T(1,128)} %bitcast.4), calls=%async_computation | async-start | bytes 262144 | tf_op jit(solution)/shard_map/all_to_all | solution.py:713
  14.1 4.8 %prepare.1 = (bf16[128,12288]{1,0:T(8,128)(2,1)S(1)}, bf16[256,128]{1,0:T(8,128)(2,1)S(1)}, bf16[256,256]{1,0:T(8,128)(2,1)S(1)}, bf16[128,256]{1,0:T(8,128)(2,1...) custom-call(f32[12288,128]{1,0:T(8,128)} %bitcast.24, ...), custom_call_target="tpu_custom_call" | custom-call | bytes 10485760 | tf_op jit(solution)/shard_map/prepare/pallas_call | solution.py:264
  18.9 5.2 %all-to-all-done = f32[128,1,256]{2,1,0:T(1,128)S(1)} async-done(((f32[128,1,256]{2,1,0:T(1,128)}), f32[128,1,256]{2,1,0:T(1,128)S(1)}, u32[]{:S(2)}, u32[]{:S(2)}) %all-to-all-start) | async-done | bytes 131104 | tf_op jit(solution)/shard_map/all_to_all | solution.py:713
  24.1 6.3 %forward.1 = (f32[384,128]{1,0:T(8,128)}, f32[16,256]{1,0:T(8,128)}, f32[8,1024]{1,0:T(8,128)}, bf16[128,1024]{1,0:T(8,128)(2,1)}, f32[256,1024]{1,0:T(8,128)}, ...) custom-call(f32[256,128]{1,0:T(8,128)S(1)} %bitcast.23, ...), custom_call_target="tpu_custom_call" | custom-call | flops 3221225472 | bytes 8388608 | tf_op jit(solution)/shard_map/forward/pallas_call | solution.py:371
  30.4 4.6 %all-to-all-start.1 = ((f32[128,1,384]{2,1,0:T(1,128)}), f32[128,1,384]{2,1,0:T(1,128)S(1)}, u32[]{:S(2)}, u32[]{:S(2)}) async-start(f32[128,1,384]{2,1,0:T(1,128)} %bitcast.27), calls=%async_computation.1 | async-start | bytes 393216 | tf_op jit(solution)/shard_map/all_to_all | solution.py:713
  35.0 6.1 %slopes.2 = (bf16[384,1024]{1,0:T(8,128)(2,1)}, bf16[512,128]{1,0:T(8,128)(2,1)S(1)}, s32[4,32]{1,0:T(4,128)S(1)}, f32[32,128]{1,0:T(8,128)S(1)}) custom-call(f32[8,1024]{1,0:T(8,128)} %get-tuple-element.55.points_h.points, bf16[128,12288]{1,0:T(8,128)(2,1)} %get-tuple-element.48.planes_h, bf16[512,128]{1,0:T(8,128)(2,1)} %get-tuple-element.49.refs_0_, ...), custom_call_target="tpu_custom_call" | custom-call | flops 3221225472 | bytes 6291456 | tf_op jit(solution)/shard_map/slopes/pallas_call | solution.py:452
  41.1 4.4 %all-to-all-done.1 = f32[128,1,384]{2,1,0:T(1,128)S(1)} async-done(((f32[128,1,384]{2,1,0:T(1,128)}), f32[128,1,384]{2,1,0:T(1,128)S(1)}, u32[]{:S(2)}, u32[]{:S(2)}) %all-to-all-start.1) | async-done | bytes 196640 | tf_op jit(solution)/shard_map/all_to_all | solution.py:713
  45.5 1.8 %rays.1 = (f32[32,128]{1,0:T(8,128)}, f32[384,128]{1,0:T(8,128)}) custom-call(f32[384,128]{1,0:T(8,128)S(1)} %bitcast.22, bf16[512,128]{1,0:T(8,128)(2,1)S(1)} %get-tuple-element.50.route, s32[4,32]{1,0:T(4,128)S(1)} %get-tuple-element.51.ranks, f32[32,128]{1,0:T(8,128)S(1)} %get-tuple-element.52.targets), custom_call_target="tpu_custom_call" | custom-call | tf_op jit(solution)/shard_map/rays/pallas_call | solution.py:534
  47.3 5.4 %all-to-all-start.2 = ((f32[128,1,384]{2,1,0:T(1,128)}), f32[128,1,384]{2,1,0:T(1,128)S(1)}, u32[]{:S(2)}, u32[]{:S(2)}) async-start(f32[128,1,384]{2,1,0:T(1,128)} %bitcast.28), calls=%async_computation.2 | async-start | bytes 393216 | tf_op jit(solution)/shard_map/all_to_all | solution.py:713
  52.7 5.7 %slopes.3 = (f32[384,1024]{1,0:T(8,128)S(1)}, f32[136,1024]{1,0:T(8,128)S(1)}, f32[256,1024]{1,0:T(8,128)S(1)}, bf16[256,128]{1,0:T(8,128)(2,1)S(1)}) custom-call(f32[8,1024]{1,0:T(8,128)} %get-tuple-element.55.points_h.points, bf16[128,12288]{1,0:T(8,128)(2,1)} %get-tuple-element.48.planes_h, f32[136,1024]{1,0:T(8,128)} %get-tuple-element.56.refs_0_, ...), custom_call_target="tpu_custom_call" | custom-call | flops 3221225472 | bytes 6291456 | tf_op jit(solution)/shard_map/slopes/pallas_call | solution.py:452
  58.4 4.8 %all-to-all-done.2 = f32[128,1,384]{2,1,0:T(1,128)S(1)} async-done(((f32[128,1,384]{2,1,0:T(1,128)}), f32[128,1,384]{2,1,0:T(1,128)S(1)}, u32[]{:S(2)}, u32[]{:S(2)}) %all-to-all-start.2) | async-done | bytes 196640 | tf_op jit(solution)/shard_map/all_to_all | solution.py:713
  63.2 4.4 %backward.1 = (f32[1536,128]{1,0:T(8,128)}, f32[256,128]{1,0:T(8,128)}, f32[1,256]{1,0:T(1,128)}, f32[256,256]{1,0:T(8,128)}, f32[128,256]{1,0:T(8,128)}, /*index=5*/bf16[1024,128]{1,0:T(8,128)(2,1)}) custom-call(f32[384,128]{1,0:T(8,128)S(1)} %bitcast.21, f32[384,1024]{1,0:T(8,128)S(1)} %get-tuple-element.60.slope_ref, ...), custom_call_target="tpu_custom_call" | custom-call | tf_op jit(solution)/shard_map/backward/pallas_call | solution.py:657
  67.6 5.0 %all-to-all-start.3 = ((f32[128,1,1536]{2,1,0:T(1,128)}), f32[128,1,1536]{2,1,0:T(1,128)S(1)}, u32[]{:S(2)}, u32[]{:S(2)}) async-start(f32[128,1,1536]{2,1,0:T(1,128)} %bitcast.25), calls=%async_computation.3 | async-start | bytes 1572864 | tf_op jit(solution)/shard_map/all_to_all | solution.py:713
  72.6 9.8 %plane_grads.1 = f32[12288,128]{1,0:T(8,128)} custom-call(f32[8,1024]{1,0:T(8,128)} %get-tuple-element.55.points_h.points, bf16[1024,128]{1,0:T(8,128)(2,1)} %get-tuple-element.69.cot), custom_call_target="tpu_custom_call" | custom-call | flops 3221225472 | bytes 6291456 | tf_op jit(solution)/shard_map/plane_grads/pallas_call | solution.py:698
  82.4 6.4 %all-to-all-done.3 = f32[128,1,1536]{2,1,0:T(1,128)S(1)} async-done(((f32[128,1,1536]{2,1,0:T(1,128)}), f32[128,1,1536]{2,1,0:T(1,128)S(1)}, u32[]{:S(2)}, u32[]{:S(2)}) %all-to-all-start.3) | async-done | bytes 786464 | tf_op jit(solution)/shard_map/all_to_all | solution.py:713
  88.8 0.7 add.1
Async XLA Ops:
  2.6 21.5 %all-to-all-start = ((f32[128,1,256]{2,1,0:T(1,128)}), f32[128,1,256]{2,1,0:T(1,128)S(1)}, u32[]{:S(2)}, u32[]{:S(2)}) async-start(f32[128,1,256]{2,1,0:T(1,128)} %bitcast.4), calls=%async_computation | async-start | bytes 262144 | tf_op jit(solution)/shard_map/all_to_all | solution.py:713
  30.4 15.1 %all-to-all-start.1 = ((f32[128,1,384]{2,1,0:T(1,128)}), f32[128,1,384]{2,1,0:T(1,128)S(1)}, u32[]{:S(2)}, u32[]{:S(2)}) async-start(f32[128,1,384]{2,1,0:T(1,128)} %bitcast.27), calls=%async_computation.1 | async-start | bytes 393216 | tf_op jit(solution)/shard_map/all_to_all | solution.py:713
  47.3 15.9 %all-to-all-start.2 = ((f32[128,1,384]{2,1,0:T(1,128)}), f32[128,1,384]{2,1,0:T(1,128)S(1)}, u32[]{:S(2)}, u32[]{:S(2)}) async-start(f32[128,1,384]{2,1,0:T(1,128)} %bitcast.28), calls=%async_computation.2 | async-start | bytes 393216 | tf_op jit(solution)/shard_map/all_to_all | solution.py:713
  67.6 21.2 %all-to-all-start.3 = ((f32[128,1,1536]{2,1,0:T(1,128)}), f32[128,1,1536]{2,1,0:T(1,128)S(1)}, u32[]{:S(2)}, u32[]{:S(2)}) async-start(f32[128,1,1536]{2,1,0:T(1,128)} %bitcast.25), calls=%async_computation.3 | async-start | bytes 1572864 | tf_op jit(solution)/shard_map/all_to_all | solution.py:713

commit v5 on v4

--- a/solution.py
+++ b/solution.py
@@ -547,15 +547,14 @@
 
 
 def backward_kernel(
-    cot, slope_ref, colors_ref, v2_ref, feature_w, density_h, v1_h, hidden_h, feats_h, first_h, rows_h,
-    pose_gh, feature_gh, density_gh, hidden_gh, first_gh, feat_cot_h,
-    density_w, v1_ref, hidden_w, feats, first_w, rows_ref,
-    feature_g, density_g, hidden_g, first_g, feat_cot,
-    color_cot, pair, pose_g, in_sems, out_sems,
+    cot, slope_ref, colors_ref, v2_ref, feature_w, density_h, v1_h, hidden_h, first_h, rows_h,
+    pose_gh, feat_cot_h, color_gh, h2_gh, raw_gh, v2_gh, h1_gh, v1_gh,
+    density_w, v1_ref, hidden_w, first_w, rows_ref,
+    feat_cot, color_cot, h2_v, raw_v, v2_cot_v, h1_v, v1_cot_v, pair, pose_g, in_sems, out_sems,
 ):
     arriving = fetch(
-        (density_h, v1_h, hidden_h, feats_h, first_h, rows_h),
-        (density_w, v1_ref, hidden_w, feats, first_w, rows_ref),
+        (density_h, v1_h, hidden_h, first_h, rows_h),
+        (density_w, v1_ref, hidden_w, first_w, rows_ref),
         in_sems,
     )
     sources = cot.shape[0] // 3
@@ -591,28 +590,31 @@
     gate2 = jax.nn.sigmoid(v2)
     h2 = (v2 * gate2).astype(BF16)
     color_c = color_cot[...]
-    feature_g[...] = contract(h2, color_c, 1, 1).astype(BF16).astype(F32)
-    density_g[...] = contract(raw_cot, h2, 1, 1).astype(BF16).astype(F32)
-    for copy in arriving:
-        copy.wait()
-    leaving = fetch((feature_g, density_g), (feature_gh, density_gh), out_sems)
+    h2_v[...] = h2
+    leaving = fetch((color_cot, h2_v), (color_gh, h2_gh), out_sems)
+    arriving[0].wait()
     wide = jnp.where(iota((8, 1), 0) == 0, density_w[...].astype(F32), 0.0).astype(BF16)
     wide_cot = jnp.where(iota((8, 1), 0) == 0, raw_cot.astype(F32), 0.0).astype(BF16)
+    raw_v[...] = wide_cot
     h2_cot = (
         contract(feature_w[...], color_c, 1, 0) + contract(wide.T, wide_cot, 1, 0)
     ).astype(BF16).astype(F32)
     v2_cot = (h2_cot * gate2 * (1.0 + v2 * (1.0 - gate2))).astype(BF16)
+    for copy in arriving[1:]:
+        copy.wait()
     v1 = v1_ref[...]
     gate1 = jax.nn.sigmoid(v1)
     h1 = (v1 * gate1).astype(BF16)
-    hidden_g[...] = contract(h1, v2_cot, 1, 1).astype(BF16).astype(F32)
-    leaving += fetch((hidden_g,), (hidden_gh,), out_sems, 2)
+    h1_v[...] = h1
+    v2_cot_v[...] = v2_cot
+    leaving += fetch((raw_v, v2_cot_v, h1_v), (raw_gh, v2_gh, h1_gh), out_sems, 2)
     h1_cot = contract(hidden_w[...], v2_cot, 1, 0).astype(BF16).astype(F32)
     v1_cot = (h1_cot * gate1 * (1.0 + v1 * (1.0 - gate1))).astype(BF16)
-    first_g[...] = contract(feats[...], v1_cot, 1, 1).astype(BF16).astype(F32)
+    v1_cot_v[...] = v1_cot
+    leaving += fetch((v1_cot_v,), (v1_gh,), out_sems, 5)
     f_cot = contract(first_w[...], v1_cot, 1, 0).astype(BF16).astype(F32)
     feat_cot[...] = f_cot.T.astype(BF16)
-    leaving += fetch((first_g, feat_cot), (first_gh, feat_cot_h), out_sems, 3)
+    leaving += fetch((feat_cot,), (feat_cot_h,), out_sems, 6)
 
     pull = [
         jnp.sum(slope_ref[a * LANES : (a + 1) * LANES, :] * f_cot, axis=0, keepdims=True)
@@ -644,16 +646,24 @@
     two = pair[...]
     for copy in range(pose_g.shape[0] // 24):
         pose_g[copy * 24 : (copy + 1) * 24, :] = two
-    leaving += fetch((pose_g,), (pose_gh,), out_sems, 5)
+    leaving += fetch((pose_g,), (pose_gh,), out_sems, 7)
     for copy in leaving:
         copy.wait()
 
 
 def backward(cot, near, distant, copies):
-    density_w, _, hidden_w, feats, first_w, _ = distant
-    feature_w = near[-1]
-    channels, count = feats.shape
-    outs = [(w.shape, F32) for w in (feature_w, density_w, hidden_w, first_w)] + [((count, channels), BF16)]
+    first_w = distant[3]
+    channels, hidden = first_w.shape
+    count = near[0].shape[1]
+    outs = [
+        ((count, channels), BF16),
+        ((channels, count), BF16),
+        ((hidden, count), BF16),
+        ((8, count), BF16),
+        ((hidden, count), BF16),
+        ((hidden, count), BF16),
+        ((hidden, count), BF16),
+    ]
     return pl.pallas_call(
         backward_kernel,
         in_specs=[IN_VMEM] * (len(near) + 1) + [IN_HBM] * len(distant),
@@ -662,7 +672,6 @@
         scratch_shapes=[pltpu.VMEM(x.shape, x.dtype) for x in distant]
         + [pltpu.VMEM(shape, kind) for shape, kind in outs]
         + [
-            pltpu.VMEM((channels, count), BF16),
             pltpu.VMEM((24, LANES), F32),
             pltpu.VMEM((12 * copies, LANES), F32),
             pltpu.SemaphoreType.DMA((len(distant),)),
@@ -673,39 +682,76 @@
     )(cot, *near, *map(far, distant))
 
 
-def plane_grads(points, cot, cells):
+def gradient_kernel(
+    points_h, cot_h, color_h, h2_h, raw_h, v2_h, h1_h, v1_h, feats_h,
+    planes_gh, first_gh, hidden_gh, feature_gh, density_gh,
+    points, cot, color_c, h2, raw_c, v2_cot, h1, v1_cot, feats,
+    planes_g, first_g, hidden_g, feature_g, density_g,
+    factor, in_sems, plane_sems, out_sems,
+):
     count = points.shape[1]
-    channels = cot.shape[1]
-    blocks = 2
-
-    def plane_kernel(points, cot, out, factor):
-        @pl.when(pl.program_id(0) == 0)
-        def _():
-            for axis in range(3):
-                factor[axis * CELLS : (axis + 1) * CELLS, :] = factors(points[axis : axis + 1, :])[0]
-
-        for block in range(blocks):
-            row_base, col_base, _, _ = plane_axes(pl.program_id(0) * blocks + block)
-            for part in range(BLOCK // TILE):
-                acc = jnp.zeros((TILE, channels), F32)
-                for lane in range(0, count, TILE):
-                    columns = factor[pl.ds(pl.multiple_of(col_base, CELLS), CELLS), lane : lane + TILE]
-                    tile = table_tile(factor, row_base, part, columns, lane)
-                    acc = acc + contract(tile, cot[lane : lane + TILE, :], 1, 0)
-                start = block * BLOCK + part * TILE
-                out[start : start + TILE, :] = acc
-
+    arriving = fetch(
+        (points_h, cot_h, color_h, h2_h, raw_h, v2_h, h1_h, v1_h, feats_h),
+        (points, cot, color_c, h2, raw_c, v2_cot, h1, v1_cot, feats),
+        in_sems,
+    )
+    arriving[0].wait()
+    for axis in range(3):
+        factor[axis * CELLS : (axis + 1) * CELLS, :] = factors(points[axis : axis + 1, :])[0]
+    arriving[1].wait()
+    blocks = planes_g.shape[0] // BLOCK
+    leaving = []
+    for block in range(blocks):
+        row_base, col_base, _, _ = plane_axes(block)
+        for part in range(BLOCK // TILE):
+            acc = jnp.zeros((TILE, cot.shape[1]), F32)
+            for lane in range(0, count, TILE):
+                columns = factor[col_base : col_base + CELLS, lane : lane + TILE]
+                tile = table_tile(factor, row_base, part, columns, lane)
+                acc = acc + contract(tile, cot[lane : lane + TILE, :], 1, 0)
+            start = block * BLOCK + part * TILE
+            planes_g[start : start + TILE, :] = acc
+        rows = slice(block * BLOCK, (block + 1) * BLOCK)
+        copy = pltpu.make_async_copy(planes_g.at[rows, :], planes_gh.at[rows, :], plane_sems.at[block])
+        copy.start()
+        leaving.append(copy)
+        if block == blocks // 2:
+            for arrival in arriving[2:]:
+                arrival.wait()
+            first_g[...] = contract(feats[...], v1_cot[...], 1, 1).astype(BF16).astype(F32)
+            hidden_g[...] = contract(h1[...], v2_cot[...], 1, 1).astype(BF16).astype(F32)
+            feature_g[...] = contract(h2[...], color_c[...], 1, 1).astype(BF16).astype(F32)
+            density_g[...] = contract(raw_c[...], h2[...], 1, 1)[0:1].astype(BF16).astype(F32)
+            leaving += fetch(
+                (first_g, hidden_g, feature_g, density_g), (first_gh, hidden_gh, feature_gh, density_gh), out_sems
+            )
+    for copy in leaving:
+        copy.wait()
+
+
+def gradients(points, cots, feats, cells):
+    count = points.shape[1]
+    cot, color_c, h2 = cots[:3]
+    channels, hidden = feats.shape[0], h2.shape[0]
+    ins = [points, *cots, feats]
+    outs = [(cells, channels), (channels, hidden), (hidden, hidden), (hidden, channels), (1, hidden)]
     return pl.pallas_call(
-        plane_kernel,
-        grid=(cells // (blocks * BLOCK),),
-        in_specs=[IN_VMEM, IN_VMEM],
-        out_specs=pl.BlockSpec((blocks * BLOCK, channels), lambda step: (step, 0)),
-        out_shape=pltpu.HBM((cells, channels), F32),
-        scratch_shapes=[pltpu.VMEM((3 * CELLS, count), F32)],
-        compiler_params=grant(8),
+        gradient_kernel,
+        in_specs=[IN_HBM] * len(ins),
+        out_specs=[IN_HBM] * len(outs),
+        out_shape=[pltpu.HBM(shape, F32) for shape in outs],
+        scratch_shapes=[pltpu.VMEM(x.shape, x.dtype) for x in ins]
+        + [pltpu.VMEM(shape, F32) for shape in outs]
+        + [
+            pltpu.VMEM((3 * CELLS, count), F32),
+            pltpu.SemaphoreType.DMA((len(ins),)),
+            pltpu.SemaphoreType.DMA((cells // BLOCK,)),
+            pltpu.SemaphoreType.DMA((4,)),
+        ],
+        compiler_params=grant(24),
         cost_estimate=price(2 * cells * count * channels, cells * channels * 4),
-        name="plane_grads",
-    )(far(points), far(cot))
+        name="gradients",
+    )(*map(far, ins))
 
 
 def exchange(rows, peers):
@@ -755,12 +801,10 @@
     near = slopes(
         later_points, turned_far, steps // 2, steps, [colors, v2, feature_o], begun
     )
-    distant = [density_weight, v1, hidden_o, feats, first_o, rows]
-    pose_part, feature_g, density_g, hidden_g, first_g, feat_cot = backward(
-        cot, near, distant, bricks
-    )
+    distant = [density_weight, v1, hidden_o, first_o, rows]
+    pose_part, *cots = backward(cot, near, distant, bricks)
     pose_grad = add(exchange(pose_part, bricks), poses.shape)
-    plane_grad = plane_grads(points, feat_cot, cells)
+    plane_grad, first_g, hidden_g, feature_g, density_g = gradients(points, cots, feats, cells)
     return (
         ray_feature,
         plane_grad[None],

time: 89.9 us -> 89.4 us (level)
  transfers between devices with their start and end apart: 4 -> 4, of which waited for: 4 -> 4; matrix products, arithmetic and copies ran while one was open for 0% -> 0% of each run, Pallas kernels for 30% -> 29%
where the time goes in v5:
time: 89.4 us; the launch traced here: 89 us
  Pallas kernels  40.7 us (46%)
  starting transfers between devices  26.4 us (30%)
  waiting for transfers between devices  21.1 us (24%)
    all_to_all x4, starting transfers between devices, exchange(): moved = lax.all_to_all(wide, AXES, split_axis=0, concat_axis=0, tiled=True)  26.4 us
    all_to_all x4, waiting for transfers between devices, exchange(): moved = lax.all_to_all(wide, AXES, split_axis=0, concat_axis=0, tiled=True)  21.1 us
    pallas_call x2, Pallas kernels, slopes(): pl.pallas_call(slope_kernel, in_specs=[IN_HBM] * (2 + len(ins)), out_spec...  11.8 us
    pallas_call x1, Pallas kernels, gradients(): pl.pallas_call(gradient_kernel, in_specs=[IN_HBM] * len(ins), out_specs=[...  9.43 us
    pallas_call x1, Pallas kernels, forward(): pl.pallas_call(forward_kernel, in_specs=[IN_VMEM] * 6, out_specs=[IN_HBM]...  6.26 us
    pallas_call x1, Pallas kernels, prepare(): pl.pallas_call(prepare_kernel, in_specs=[IN_HBM] * 6, out_specs=[IN_VMEM]...  4.84 us
    pallas_call x1, Pallas kernels, backward(): pl.pallas_call(backward_kernel, in_specs=[IN_VMEM] * (len(near) + 1) + [I...  3.94 us
    pallas_call x1, Pallas kernels, dispatch(): pl.pallas_call(dispatch_kernel, out_shape=jax.ShapeDtypeStruct((2 * brick...  1.95 us
  transfers between devices with their start and end apart: 4, of which 4 were waited for; matrix products, arithmetic and copies ran while one was open for 0% of the time, Pallas kernels for 29%

profile of v5, /device:TPU:1, one launch (start us, length us, event | category | flops | bytes accessed | tf_op | source)
XLA Modules:
  0.0 89.0 jit_solution(2087271697442619958)
XLA Ops:
  0.6 1.9 %dispatch.1 = f32[256,128]{1,0:T(8,128)} custom-call(f32[3,32]{1,0:T(4,128)} %anchors.1, f32[3,32]{1,0:T(4,128)} %directions.1, f32[1,32]{1,0:T(1,128)} %bitcast.35, s32[1,32]{1,0:T(1,128)} %bitcast.36, s32[4,32]{1,0:T(4,128)} %bitcast.31, s32[4,32]{1,0:T(4,128)} %bitcast.33, f32[6,256]{1,0:T(8,128)} %poses.1), custom_call_target="tpu_custom_call" | custom-call | tf_op jit(solution)/shard_map/dispatch/pallas_call | solution.py:131
  2.6 11.5 %all-to-all-start = ((f32[128,1,256]{2,1,0:T(1,128)}), f32[128,1,256]{2,1,0:T(1,128)S(1)}, u32[]{:S(2)}, u32[]{:S(2)}) async-start(f32[128,1,256]{2,1,0:T(1,128)} %bitcast.4), calls=%async_computation | async-start | bytes 262144 | tf_op jit(solution)/shard_map/all_to_all | solution.py:759
  14.1 4.8 %prepare.1 = (bf16[128,12288]{1,0:T(8,128)(2,1)S(1)}, bf16[256,128]{1,0:T(8,128)(2,1)S(1)}, bf16[256,256]{1,0:T(8,128)(2,1)S(1)}, bf16[128,256]{1,0:T(8,128)(2,1...) custom-call(f32[12288,128]{1,0:T(8,128)} %bitcast.24, ...), custom_call_target="tpu_custom_call" | custom-call | bytes 10485760 | tf_op jit(solution)/shard_map/prepare/pallas_call | solution.py:264
  18.9 5.2 %all-to-all-done = f32[128,1,256]{2,1,0:T(1,128)S(1)} async-done(((f32[128,1,256]{2,1,0:T(1,128)}), f32[128,1,256]{2,1,0:T(1,128)S(1)}, u32[]{:S(2)}, u32[]{:S(2)}) %all-to-all-start) | async-done | bytes 131104 | tf_op jit(solution)/shard_map/all_to_all | solution.py:759
  24.1 6.3 %forward.1 = (f32[384,128]{1,0:T(8,128)}, f32[16,256]{1,0:T(8,128)}, f32[8,1024]{1,0:T(8,128)}, bf16[128,1024]{1,0:T(8,128)(2,1)}, f32[256,1024]{1,0:T(8,128)}, ...) custom-call(f32[256,128]{1,0:T(8,128)S(1)} %bitcast.23, ...), custom_call_target="tpu_custom_call" | custom-call | flops 3221225472 | bytes 8388608 | tf_op jit(solution)/shard_map/forward/pallas_call | solution.py:371
  30.4 4.6 %all-to-all-start.1 = ((f32[128,1,384]{2,1,0:T(1,128)}), f32[128,1,384]{2,1,0:T(1,128)S(1)}, u32[]{:S(2)}, u32[]{:S(2)}) async-start(f32[128,1,384]{2,1,0:T(1,128)} %bitcast.27), calls=%async_computation.1 | async-start | bytes 393216 | tf_op jit(solution)/shard_map/all_to_all | solution.py:759
  35.0 6.1 %slopes.2 = (bf16[384,1024]{1,0:T(8,128)(2,1)}, bf16[512,128]{1,0:T(8,128)(2,1)S(1)}, s32[4,32]{1,0:T(4,128)S(1)}, f32[32,128]{1,0:T(8,128)S(1)}) custom-call(f32[8,1024]{1,0:T(8,128)} %get-tuple-element.62.points_h, bf16[128,12288]{1,0:T(8,128)(2,1)} %get-tuple-element.55.planes_h, bf16[512,128]{1,0:T(8,128)(2,1)} %get-tuple-element.56.refs_0_, ...), custom_call_target="tpu_custom_call" | custom-call | flops 3221225472 | bytes 6291456 | tf_op jit(solution)/shard_map/slopes/pallas_call | solution.py:452
  41.1 4.4 %all-to-all-done.1 = f32[128,1,384]{2,1,0:T(1,128)S(1)} async-done(((f32[128,1,384]{2,1,0:T(1,128)}), f32[128,1,384]{2,1,0:T(1,128)S(1)}, u32[]{:S(2)}, u32[]{:S(2)}) %all-to-all-start.1) | async-done | bytes 196640 | tf_op jit(solution)/shard_map/all_to_all | solution.py:759
  45.5 1.8 %rays.1 = (f32[32,128]{1,0:T(8,128)}, f32[384,128]{1,0:T(8,128)}) custom-call(f32[384,128]{1,0:T(8,128)S(1)} %bitcast.22, bf16[512,128]{1,0:T(8,128)(2,1)S(1)} %get-tuple-element.57.route, s32[4,32]{1,0:T(4,128)S(1)} %get-tuple-element.58.ranks, f32[32,128]{1,0:T(8,128)S(1)} %get-tuple-element.59.targets), custom_call_target="tpu_custom_call" | custom-call | tf_op jit(solution)/shard_map/rays/pallas_call | solution.py:534
  47.3 5.4 %all-to-all-start.2 = ((f32[128,1,384]{2,1,0:T(1,128)}), f32[128,1,384]{2,1,0:T(1,128)S(1)}, u32[]{:S(2)}, u32[]{:S(2)}) async-start(f32[128,1,384]{2,1,0:T(1,128)} %bitcast.28), calls=%async_computation.2 | async-start | bytes 393216 | tf_op jit(solution)/shard_map/all_to_all | solution.py:759
  52.7 5.7 %slopes.3 = (f32[384,1024]{1,0:T(8,128)S(1)}, f32[136,1024]{1,0:T(8,128)S(1)}, f32[256,1024]{1,0:T(8,128)S(1)}, bf16[256,128]{1,0:T(8,128)(2,1)S(1)}) custom-call(f32[8,1024]{1,0:T(8,128)} %get-tuple-element.62.points_h, bf16[128,12288]{1,0:T(8,128)(2,1)} %get-tuple-element.55.planes_h, f32[136,1024]{1,0:T(8,128)} %get-tuple-element.63.refs_0_, ...), custom_call_target="tpu_custom_call" | custom-call | flops 3221225472 | bytes 6291456 | tf_op jit(solution)/shard_map/slopes/pallas_call | solution.py:452
  58.4 4.8 %all-to-all-done.2 = f32[128,1,384]{2,1,0:T(1,128)S(1)} async-done(((f32[128,1,384]{2,1,0:T(1,128)}), f32[128,1,384]{2,1,0:T(1,128)S(1)}, u32[]{:S(2)}, u32[]{:S(2)}) %all-to-all-start.2) | async-done | bytes 196640 | tf_op jit(solution)/shard_map/all_to_all | solution.py:759
  63.2 3.9 %backward.1 = (f32[1536,128]{1,0:T(8,128)}, bf16[1024,128]{1,0:T(8,128)(2,1)}, bf16[128,1024]{1,0:T(8,128)(2,1)}, bf16[256,1024]{1,0:T(8,128)(2,1)}, bf16[8,1024...) custom-call(f32[384,128]{1,0:T(8,128)S(1)} %bitcast.21, ...), custom_call_target="tpu_custom_call" | custom-call | tf_op jit(solution)/shard_map/backward/pallas_call | solution.py:667
  67.1 5.0 %all-to-all-start.3 = ((f32[128,1,1536]{2,1,0:T(1,128)}), f32[128,1,1536]{2,1,0:T(1,128)S(1)}, u32[]{:S(2)}, u32[]{:S(2)}) async-start(f32[128,1,1536]{2,1,0:T(1,128)} %bitcast.25), calls=%async_computation.3 | async-start | bytes 1572864 | tf_op jit(solution)/shard_map/all_to_all | solution.py:759
  72.1 9.4 %gradients.1 = (f32[12288,128]{1,0:T(8,128)}, f32[128,256]{1,0:T(8,128)}, f32[256,256]{1,0:T(8,128)}, f32[256,128]{1,0:T(8,128)}, f32[1,256]{1,0:T(1,128)}) custom-call(f32[8,1024]{1,0:T(8,128)} %get-tuple-element.62.points_h, bf16[1024,128]{1,0:T(8,128)(2,1)} %get-tuple-element.75.cot_h, bf16[128,1024]{1,0:T(8,128)(2,1)} %get-tuple-element.76.color_h, ...), custom_call_target="tpu_custom_call" | custom-call | flops 3221225472 | bytes 6291456 | tf_op jit(solution)/shard_map/gradients/pallas_call | solution.py:738
  81.5 6.8 %all-to-all-done.3 = f32[128,1,1536]{2,1,0:T(1,128)S(1)} async-done(((f32[128,1,1536]{2,1,0:T(1,128)}), f32[128,1,1536]{2,1,0:T(1,128)S(1)}, u32[]{:S(2)}, u32[]{:S(2)}) %all-to-all-start.3) | async-done | bytes 786464 | tf_op jit(solution)/shard_map/all_to_all | solution.py:759
  88.3 0.7 add.1
Async XLA Ops:
  2.6 21.5 %all-to-all-start = ((f32[128,1,256]{2,1,0:T(1,128)}), f32[128,1,256]{2,1,0:T(1,128)S(1)}, u32[]{:S(2)}, u32[]{:S(2)}) async-start(f32[128,1,256]{2,1,0:T(1,128)} %bitcast.4), calls=%async_computation | async-start | bytes 262144 | tf_op jit(solution)/shard_map/all_to_all | solution.py:759
  30.4 15.1 %all-to-all-start.1 = ((f32[128,1,384]{2,1,0:T(1,128)}), f32[128,1,384]{2,1,0:T(1,128)S(1)}, u32[]{:S(2)}, u32[]{:S(2)}) async-start(f32[128,1,384]{2,1,0:T(1,128)} %bitcast.27), calls=%async_computation.1 | async-start | bytes 393216 | tf_op jit(solution)/shard_map/all_to_all | solution.py:759
  47.3 15.9 %all-to-all-start.2 = ((f32[128,1,384]{2,1,0:T(1,128)}), f32[128,1,384]{2,1,0:T(1,128)S(1)}, u32[]{:S(2)}, u32[]{:S(2)}) async-start(f32[128,1,384]{2,1,0:T(1,128)} %bitcast.28), calls=%async_computation.2 | async-start | bytes 393216 | tf_op jit(solution)/shard_map/all_to_all | solution.py:759
  67.1 21.2 %all-to-all-start.3 = ((f32[128,1,1536]{2,1,0:T(1,128)}), f32[128,1,1536]{2,1,0:T(1,128)S(1)}, u32[]{:S(2)}, u32[]{:S(2)}) async-start(f32[128,1,1536]{2,1,0:T(1,128)} %bitcast.25), calls=%async_computation.3 | async-start | bytes 1572864 | tf_op jit(solution)/shard_map/all_to_all | solution.py:759
